TPU v7x, 128 devices: a whole 4x4x4 slice. The times are simulated.
128 devices in a mesh: dp: 4 (over x), tensor: 32 (over z, y, core).
Axes of the slice: x: 4, y: 4, z: 4, core: 2. Of those that a mesh axis runs over, the one named last changes fastest.
Arguments:
- tokens: bfloat16 [8192, 2048], P(('dp', 'tensor')), may hold values from -40 to 40
- attn_gain: bfloat16 [2048], replicated, may hold values from 0.099609375 to 1.8984375
- moe_gain: bfloat16 [2048], replicated, may hold values from 0.099609375 to 1.8984375
- q_gain: bfloat16 [128], replicated, may hold values from 0.099609375 to 1.8984375
- k_gain: bfloat16 [128], replicated, may hold values from 0.099609375 to 1.8984375
- query_weight: bfloat16 [2048, 4096], P(None, 'tensor'), may hold values from -0.125 to 0.125
- w_kv: bfloat16 [256, 4, 2048], P('tensor'), may hold values from -0.125 to 0.125
- w_o: bfloat16 [4096, 2048], P('tensor'), may hold values from -0.5 to 0.5
- w_gate: bfloat16 [64, 768, 2048], P('tensor'), may hold values from -0.125 to 0.125
- w_up: bfloat16 [64, 768, 2048], P('tensor'), may hold values from -0.125 to 0.125
- w_down: bfloat16 [64, 768, 2048], P('tensor'), may hold values from -0.21875 to 0.21875
- shrink_qkv: bfloat16 [16, 48, 2048], P('dp'), may hold values from -0.125 to 0.125
- shrink_o: bfloat16 [16, 16, 4096], P(None, None, 'tensor'), may hold values from -0.5 to 0.5
- query_up_factors: bfloat16 [16, 16, 4096], P(None, None, 'tensor'), may hold values from -1.5 to 1.5
- key_value_up_factors: bfloat16 [16, 16, 1024], replicated, may hold values from -1.5 to 1.5
- expand_o: bfloat16 [16, 16, 2048], replicated, may hold values from -1.5 to 1.5
- lengths: int32 [4, 32], P('dp'), may hold values from 1 to 256, 2048 in all within a row
- groups: int32 [4, 32], P('dp'), may hold values from 0 to 3, never falling along the last dimension, each value on 1 to 16 neighbouring positions
- adapter_of_request: int32 [4, 32], P('dp'), may hold values from 0 to 15
- adapter_slot: int32 [16], replicated, may hold values from 0 to 15, each once
- page_table: int32 [4, 64], P('dp'), may hold values from 0 to 63, each once within a row
- expert_ids: int32 [8192, 8], P('dp'), may hold values from 0 to 63, all different within a row; in each aligned block of 64 rows (0 to 63, 64 to 127, ...) at most 16 rows name the same one
- expert_gates: float32 [8192, 8], P('dp'), may hold values from 0.05 to 1
Outputs:
- attn_out: bfloat16 [8192, 2048], P(('dp', 'tensor'))
- moe_out: bfloat16 [8192, 2048], P(('dp', 'tensor'))
- kv_pages: bfloat16 [256, 1024, 128], P('dp', 'tensor')
Inputs may be any that keep to these rules, and one draw needn't show every extreme that they name: `lengths`: each row sums to 2048; its largest entry is exactly 256. `groups`: never falling along a row; each group holds 1 to 16 consecutive requests, one exactly 16. `adapter_slot`: A permutation; the factors of slots k * 16 / 4 to (k + 1) * 16 / 4 - 1 are held at dp index k. `page_table`: each row is a permutation of the pages of that token group's pool. `expert_ids`: A token's 8 experts are distinct; within each aligned block of 64 rows (the rows of one device) no expert is chosen by more than 16 tokens, a bound that some block reaches.
All inputs are finite; a program needn't handle non-finite values.
Results may differ from a plain program's by a relative error of at most 0.025.
Values may be sent and summed in bfloat16 or wider, within the bound.
A program may use at most 128 MiB of HBM per device.

v0:
```python
import math

import jax
import jax.numpy as jnp
from jax import lax
from jax.sharding import PartitionSpec as P

EXPERTS = 64
PAGE = 128
CAP_DEV = 16


NORM_EPS = 1e-06
ROPE_BASE = 1000000.0
ADAPTER_FACTOR = 0.5


def normalize(values, gain):
    return (
        values
        * lax.rsqrt(jnp.mean(values * values, axis=-1, keepdims=True) + NORM_EPS)
        * gain.astype(jnp.float32)
    )


def rotate(values, position):
    half = values.shape[-1] // 2
    freq = jnp.exp(
        -jnp.arange(half, dtype=jnp.float32) * (2.0 * math.log(ROPE_BASE) / values.shape[-1])
    )
    angle = position.astype(jnp.float32)[:, None, None] * freq[None, None, :]
    cosine = jnp.cos(angle)
    sine = jnp.sin(angle)
    first = values[..., :half]
    second = values[..., half:]
    return jnp.concatenate(
        [first * cosine - second * sine, second * cosine + first * sine], axis=-1
    )


def lookup(index_value, table):
    match = index_value[:, None] == jnp.arange(table.shape[0], dtype=jnp.int32)[None, :]
    return jnp.sum(jnp.where(match, table[None, :], 0), axis=1)


def token_layout(length_row, group_row, adapter_row, adapter_slot, page_row, grand_total):
    position = jnp.arange(grand_total, dtype=jnp.int32)
    ends = jnp.cumsum(length_row)
    starts = ends - length_row
    request = jnp.sum((ends[None, :] <= position[:, None]).astype(jnp.int32), axis=1)
    group = lookup(request, group_row)
    same = group_row[:, None] == group_row[None, :]
    group_first = jnp.min(jnp.where(same, starts[None, :], grand_total), axis=1)
    rope_pos = position - lookup(request, group_first)
    offset = position - lookup(request, starts)
    per_request = page_row.shape[0] // length_row.shape[0]
    page = lookup(request * per_request + offset // PAGE, page_row)
    cell = page * PAGE + offset % PAGE
    adapter_position = lookup(request, lookup(adapter_row, adapter_slot))
    return (group, rope_pos, cell, adapter_position)


def spread_rows(values, adapter_position, adapters):
    match = adapter_position[:, None] == jnp.arange(adapters, dtype=jnp.int32)[None, :]
    placed = jnp.where(match[:, :, None], values[:, None, :], jnp.zeros((), values.dtype))
    return placed.reshape(values.shape[0], -1)


def routing(chosen, gates, experts, capacity):
    token_count = chosen.shape[0]
    choose = chosen[:, :, None] == jnp.arange(experts, dtype=jnp.int32)[None, None, :]
    share = gates / jnp.sum(gates, axis=1, keepdims=True)
    weight = jnp.sum(jnp.where(choose, share[:, :, None], 0.0), axis=1)
    hit = jnp.any(choose, axis=1)
    place = jnp.cumsum(hit.astype(jnp.int32), axis=0) - 1
    column = jnp.where(hit, place, capacity)
    expert_grid = jnp.broadcast_to(jnp.arange(experts, dtype=jnp.int32)[None, :], hit.shape)
    token_grid = jnp.broadcast_to(jnp.arange(token_count, dtype=jnp.int32)[:, None], hit.shape)
    slot_token = (
        jnp.zeros((experts, capacity + 1), jnp.int32)
        .at[expert_grid, column]
        .set(token_grid)[:, :capacity]
    )
    slot_weight = (
        jnp.zeros((experts, capacity + 1), jnp.float32)
        .at[expert_grid, column]
        .set(weight)[:, :capacity]
    )
    return (slot_token, slot_weight)


def attend(query_rows_out, keys, values, group, scale):
    grand_total = query_rows_out.shape[0]
    block = min(512, grand_total)
    position = jnp.arange(grand_total, dtype=jnp.int32)

    def one_block(number):
        first = number * block
        query_block = lax.dynamic_slice_in_dim(query_rows_out, first, block, 0)
        rows_here = first + jnp.arange(block, dtype=jnp.int32)
        group_here = lax.dynamic_slice_in_dim(group, first, block, 0)
        allowed = (position[None, :] <= rows_here[:, None]) & (
            group[None, :] == group_here[:, None]
        )
        scores = (
            jnp.einsum("qhd,kd->hqk", query_block, keys, preferred_element_type=jnp.float32) * scale
        )
        raised = jnp.where(allowed[None], jnp.exp(scores), 0.0)
        shares = (raised / jnp.sum(raised, axis=-1, keepdims=True)).astype(jnp.bfloat16)
        mixed = jnp.einsum("hqk,kd->qhd", shares, values, preferred_element_type=jnp.float32)
        return mixed.astype(jnp.bfloat16).reshape(block, -1)

    return lax.map(one_block, jnp.arange(grand_total // block, dtype=jnp.int32)).reshape(
        grand_total, -1
    )


def expert_apply(rows, gate_rows, up_rows, down_rows):
    gate_value = jnp.einsum("secx,efx->secf", rows, gate_rows, preferred_element_type=jnp.float32)
    up_value = jnp.einsum("secx,efx->secf", rows, up_rows, preferred_element_type=jnp.float32)
    hidden = (jax.nn.silu(gate_value) * up_value).astype(jnp.bfloat16)
    out = jnp.einsum("secf,efx->secx", hidden, down_rows, preferred_element_type=jnp.float32)
    return lax.optimization_barrier(out.astype(jnp.bfloat16))


def local(
    tokens,
    attn_gain,
    moe_gain,
    q_gain,
    k_gain,
    query_weight,
    w_kv,
    w_o,
    w_gate,
    w_up,
    w_down,
    shrink_qkv,
    shrink_o,
    query_up_factors,
    key_value_up_factors,
    expand_o,
    lengths,
    groups,
    adapter_of_request,
    adapter_slot,
    page_table,
    expert_ids,
    expert_gates,
):
    parts = lax.axis_size("tensor")
    place = lax.axis_index("tensor")
    own_rows, width = tokens.shape
    grand_total = own_rows * parts
    head_length = q_gain.shape[0]
    adapters, rank, kv_width = key_value_up_factors.shape
    key_value_heads = kv_width // (2 * head_length)
    group, rope_pos, cell, adapter_position = token_layout(
        lengths[0], groups[0], adapter_of_request[0], adapter_slot, page_table[0], grand_total
    )
    own_slot = lax.dynamic_slice_in_dim(adapter_position, place * own_rows, own_rows, 0)
    normed_own = normalize(tokens.astype(jnp.float32), attn_gain).astype(jnp.bfloat16)
    piece = lax.all_gather(shrink_qkv, "dp", axis=0, tiled=True)
    projected = jnp.einsum("td,prd->tpr", normed_own, piece, preferred_element_type=jnp.float32)
    match = own_slot[:, None] == jnp.arange(piece.shape[0], dtype=jnp.int32)[None, :]
    shrunk_own = jnp.sum(jnp.where(match[:, :, None], projected, 0.0), axis=1)
    shrunk_own = shrunk_own.astype(jnp.bfloat16)
    normalized_input, shrunken_rows = (
        lax.all_gather(normed_own, "tensor", axis=0, tiled=True),
        lax.all_gather(shrunk_own, "tensor", axis=0, tiled=True),
    )
    head = place * key_value_heads // parts
    local_cols = kv_width // parts
    token_extent = w_kv.shape[0]
    span_begin = place * token_extent
    base_key_value = jnp.einsum(
        "td,chd->thc", normalized_input, w_kv, preferred_element_type=jnp.float32
    )
    upward_split = key_value_up_factors.reshape(adapters, rank, key_value_heads, 2 * head_length)
    upward_local = lax.dynamic_slice_in_dim(upward_split, span_begin, token_extent, 3).reshape(
        adapters * rank, key_value_heads * token_extent
    )
    key_adapter_delta = jnp.dot(
        spread_rows(shrunken_rows[:, rank : 2 * rank], adapter_position, adapters),
        upward_local,
        preferred_element_type=jnp.float32,
    )
    value_adapter_delta = jnp.dot(
        spread_rows(shrunken_rows[:, 2 * rank :], adapter_position, adapters),
        upward_local,
        preferred_element_type=jnp.float32,
    )
    whether_key = jnp.tile(
        span_begin + jnp.arange(token_extent, dtype=jnp.int32) < head_length, key_value_heads
    )
    adapter_delta_term = jnp.where(
        whether_key[None, :], key_adapter_delta, value_adapter_delta
    ).reshape(grand_total, key_value_heads, token_extent)
    resident_key_value = (base_key_value + ADAPTER_FACTOR * adapter_delta_term).astype(jnp.bfloat16)
    every_kv = lax.all_gather(resident_key_value, "tensor", axis=2, tiled=True)
    head_kv = lax.dynamic_index_in_dim(every_kv, head, 1, keepdims=False)
    divided_key_value = head_kv.reshape(grand_total, 2, head_length)
    keys = rotate(normalize(divided_key_value[:, :1].astype(jnp.float32), k_gain), rope_pos).astype(
        jnp.bfloat16
    )[:, 0]
    values = divided_key_value[:, 1]
    entries = jnp.concatenate([keys, values], axis=1)
    mine = lax.dynamic_slice_in_dim(
        entries, place * local_cols - head * 2 * head_length, local_cols, 1
    )
    pages_held = page_table.shape[1]
    kv_pages = jnp.zeros((pages_held * PAGE, local_cols), jnp.bfloat16).at[cell].set(mine)
    kv_pages = kv_pages.reshape(pages_held, PAGE, local_cols).transpose(0, 2, 1)
    query_cols = query_weight.shape[1]
    heads_here = query_cols // head_length
    query_rows_out = jnp.dot(
        normalized_input, query_weight, preferred_element_type=jnp.float32
    ) + ADAPTER_FACTOR * jnp.dot(
        spread_rows(shrunken_rows[:, :rank], adapter_position, adapters),
        query_up_factors.reshape(adapters * rank, query_cols),
        preferred_element_type=jnp.float32,
    )
    query_rows_out = rotate(
        normalize(query_rows_out.reshape(grand_total, heads_here, head_length), q_gain), rope_pos
    ).astype(jnp.bfloat16)
    mixed = attend(query_rows_out, keys, values, group, head_length ** (-0.5))
    shrink_table = shrink_o.reshape(adapters * rank, query_cols)
    upward_wide_rows = expand_o.reshape(adapters * rank, width).astype(jnp.float32)
    lower_rank_rows = lax.dot_general(
        mixed, shrink_table, (((1,), (1,)), ((), ())), preferred_element_type=jnp.float32
    )
    retained_mask = jnp.repeat(
        adapter_position[:, None] == jnp.arange(adapters, dtype=jnp.int32)[None, :], rank, axis=1
    )
    adapter_contribution = jnp.dot(mixed, w_o, preferred_element_type=jnp.float32)
    attn_own = lax.psum_scatter(
        (
            adapter_contribution
            + ADAPTER_FACTOR
            * jnp.dot(
                jnp.where(retained_mask, lower_rank_rows, 0.0),
                upward_wide_rows,
                precision=lax.Precision.HIGHEST,
            )
        ).astype(jnp.bfloat16),
        "tensor",
        scatter_dimension=0,
        tiled=True,
    ).astype(jnp.float32)
    moe_own = normalize(tokens.astype(jnp.float32) + attn_own, moe_gain).astype(jnp.bfloat16)
    experts_here = w_gate.shape[0]
    moe_in = lax.all_gather(moe_own, "tensor", axis=0, tiled=True)
    capacity = CAP_DEV * parts
    slot_token, slot_weight = routing(expert_ids, expert_gates, EXPERTS, capacity)
    own_tokens = lax.dynamic_slice_in_dim(slot_token, place * experts_here, experts_here, 0)
    own_weights = lax.dynamic_slice_in_dim(slot_weight, place * experts_here, experts_here, 0)
    outputs = expert_apply(moe_in[own_tokens][None], w_gate, w_up, w_down)[0]
    weighted = outputs.astype(jnp.float32) * own_weights[:, :, None]
    moe_terms = (
        jnp.zeros((grand_total, width), jnp.float32)
        .at[own_tokens.reshape(-1)]
        .add(weighted.reshape(-1, width))
    )
    moe_total = lax.psum_scatter(
        moe_terms.astype(jnp.bfloat16), "tensor", scatter_dimension=0, tiled=True
    )
    return (attn_own.astype(jnp.bfloat16), moe_total, kv_pages)


def solution(mesh):
    placed = (
        P(("dp", "tensor"), None),
        P(),
        P(),
        P(),
        P(),
        P(None, "tensor"),
        P("tensor", None, None),
        P("tensor", None),
        P("tensor", None, None),
        P("tensor", None, None),
        P("tensor", None, None),
        P("dp", None, None),
        P(None, None, "tensor"),
        P(None, None, "tensor"),
        P(),
        P(),
        P("dp", None),
        P("dp", None),
        P("dp", None),
        P(),
        P("dp", None),
        P("dp", None),
        P("dp", None),
    )
    return jax.shard_map(
        local,
        mesh=mesh,
        in_specs=placed,
        out_specs=(P(("dp", "tensor"), None), P(("dp", "tensor"), None), P("dp", "tensor", None)),
        check_vma=False,
    )
```

profile of v0, /device:TPU:1, one launch (start us, length us, event | category | flops | bytes accessed | tf_op | source)
XLA Modules:
  0.0 1458.9 jit_solution(13291466150013901253)
XLA Ops:
  12.7 5.8 copy.107
  20.3 32.0 %all-gather.8.cloned.1.call-done = bf16[16,48,2048]{2,1,0:T(8,128)(2,1)} async-done(((bf16[4,48,2048]{2,1,0:T(8,128)(2,1)}), bf16[16,48,2048]{2,1,0:T(8,128)(2,1)}) %all-gather.8.cloned.1.call-update) | async-done | bytes 3145744 | tf_op jit(solution)/shard_map/all_gather | solution.py:163
  52.3 2.9 fusion.38
  55.2 25.8 %all-gather = bf16[32,64,48]{1,2,0:T(8,128)(2,1)S(1)} all-gather(bf16[1,64,48]{1,2,0:T(8,128)(2,1)S(1)} %bitcast.231), channel_id=1, replica_groups=mesh['dp'=4,'tensor'=32] {'tensor'}, dimensions={0}, use_global_device_ids=true | all-gather | bytes 202752 | tf_op jit(solution)/shard_map/all_gather | solution.py:170
  82.0 27.2 %all-gather.6.cloned.1.call-done = bf16[2048,2048]{1,0:T(8,128)(2,1)} async-done(((bf16[64,2048]{1,0:T(8,128)(2,1)}), bf16[2048,2048]{1,0:T(8,128)(2,1)}) %all-gather.6.cloned.1.call-update) | async-done | bytes 8388624 | tf_op jit(solution)/shard_map/all_gather | solution.py:169
  109.2 5.9 fusion.29
  117.9 6.3 fusion.89
  124.9 37.3 %all-gather.10.cloned.1.call-done = bf16[2048,4,256]{0,2,1:T(8,128)(2,1)} async-done(((bf16[2048,4,8]{0,2,1:T(8,128)(2,1)}), bf16[2048,4,256]{0,2,1:T(8,128)(2,1)}) %all-gather.10.cloned.1.call-update) | async-done | bytes 4194320 | tf_op jit(solution)/shard_map/all_gather | solution.py:200
  163.8 3.4 fusion.70
  171.1 19.9 %while.11 = (s32[]{:T(128)}, bf16[4,512,128]{2,1,0:T(8,128)(2,1)S(1)}, s32[4]{0:T(128)S(1)}, s32[2048]{0:T(1024)S(1)}, bf16[2048,1,128]{0,2,1:T(8,128)(2,1)}, /*...) while((s32[]{:T(128)}, ...), condition=%wide.region_13.14_spmd.clone, body=%wide.region_11.13_spmd.clone.sunk | while | flops 545325056 | bytes 11819227 | solution.py:113
  177.4 2.8 fusion.122
  191.8 3.5 fusion.90
  197.1 12.1 add_convert_fusion
  209.8 89.5 %reduce-scatter.3.cloned.1.call-done = bf16[64,2048]{1,0:T(8,128)(2,1)} async-done(((bf16[2048,2048]{1,0:T(8,128)(2,1)}), bf16[64,2048]{1,0:T(8,128)(2,1)}) %reduce-scatter.3.cloned.1.call-update) | async-done | bytes 262160 | tf_op jit(solution)/shard_map/reduce_scatter | solution.py:236
  304.4 28.0 %reduce-window.11 = s32[64,16,128]{2,1,0:T(8,128)S(1)} reduce-window(s32[64,16,128]{2,1,0:T(8,128)S(1)} %bitcast.225, s32[]{:T(128)} %constant.54.clone.1), window={size=1x1x128 pad=0_0x0_0x127_0}, to_apply=%region_16.17 | reduce-window | flops 16646144 | bytes 1048580 | tf_op jit(solution)/shard_map/reduce-window.1
  334.8 478.7 %scatter_custom_fusion.3 = f32[32832]{0:T(1024)S(1)} fusion(s32[131072]{0:T(1024)S(1)} %reshape.655, f32[131072]{0:T(1024)S(1)} %reshape.663, f32[]{:T(128)} %constant.58.clone.1), kind=kCustom, calls=%fused_computation.123 | custom fusion | bytes 131332
  814.0 478.7 %scatter_custom_fusion.2 = s32[32832]{0:T(1024)S(1)} fusion(s32[131072]{0:T(1024)S(1)} %reshape.655, s32[131072]{0:T(1024)S(1)} %reshape.657, s32[]{:T(128)} %constant.54.clone.1), kind=kCustom, calls=%fused_computation.125 | custom fusion | bytes 131332
  1292.9 13.3 gather_fusion
  1306.2 9.2 fusion.91
  1315.4 13.3 convert_bitcast_fusion
  1328.7 21.8 %scatter_custom_fusion = f32[2048,2048]{1,0:T(8,128)} fusion(s32[1024]{0:T(1024)S(1)} %bitcast.239, bf16[1024,2048]{1,0:T(8,128)(2,1)} %bitcast.217, f32[]{:T(128)} %constant.58.clone.1, f32[1024]{0:T(1024)S(1)} %bitcast.233), kind=kCustom, calls=%fused_computation.21 | custom fusion | flops 6291456 | bytes 20975620 | tf_op jit(solution)/shard_map/scatter-add | solution.py:262
  1350.5 9.1 convert_element_type.130
  1361.8 6.8 scatter_custom_fusion.1
  1370.1 81.8 %reduce-scatter.5.cloned.1.call-done = bf16[64,2048]{1,0:T(8,128)(2,1)} async-done(((bf16[2048,2048]{1,0:T(8,128)(2,1)}), bf16[64,2048]{1,0:T(8,128)(2,1)}) %reduce-scatter.5.cloned.1.call-update) | async-done | bytes 262160 | tf_op jit(solution)/shard_map/reduce_scatter | solution.py:264
  (185 shorter events, 46.2 us)
Async XLA Ops:
  7.2 189.9 %copy-start = (bf16[16,16,2048]{2,1,0:T(8,128)(2,1)S(1)}, bf16[16,16,2048]{2,1,0:T(8,128)(2,1)}, u32[]{:S(2)}) copy-start(bf16[16,16,2048]{2,1,0:T(8,128)(2,1)} %param.40) | copy-start | bytes 3145732
  7.2 12.5 copy-start.21
  7.2 12.3 copy-start.25
  7.2 12.3 copy-start.26
  7.2 12.4 copy-start.17
  7.2 45.1 %all-gather.8.cloned.1.call-start = ((), (), s32[]{:S(2)}) async-start(), calls=%async_computation.3 | async-start | bytes 3932160 | tf_op jit(solution)/shard_map/all_gather | solution.py:163
  8.0 101.2 %all-gather.6.cloned.1.call-start = ((), (), s32[]{:S(2)}) async-start(), calls=%async_computation.2 | async-start | bytes 8650752 | tf_op jit(solution)/shard_map/all_gather | solution.py:169
  11.6 40.7 %copy-start.5 = (bf16[64,2048]{1,0:T(8,128)(2,1)S(1)}, bf16[64,2048]{1,0:T(8,128)(2,1)}, u32[]{:S(2)}) copy-start(bf16[64,2048]{1,0:T(8,128)(2,1)} %fusion.63) | copy-start | bytes 786436
  11.6 150.5 %all-gather.10.cloned.1.call-start = ((), (), s32[]{:S(2)}) async-start(), calls=%async_computation.4 | async-start | bytes 4325376 | tf_op jit(solution)/shard_map/all_gather | solution.py:200
  20.3 88.9 %copy-start.23 = (bf16[8,4,2048]{2,1,0:T(4,128)(2,1)S(1)}, bf16[8,4,2048]{2,1,0:T(4,128)(2,1)}, u32[]{:S(2)}) copy-start(bf16[8,4,2048]{2,1,0:T(4,128)(2,1)} %param.31) | copy-start | bytes 393220
  82.0 34.2 %copy-start.27 = (bf16[128]{0:T(256)(128)(2,1)S(1)}, bf16[128]{0:T(256)(128)(2,1)}, u32[]{:S(2)}) copy-start(bf16[128]{0:T(256)(128)(2,1)} %param.28) | copy-start | bytes 772
  82.0 34.2 %copy-start.28 = (bf16[128]{0:T(256)(128)(2,1)S(1)}, bf16[128]{0:T(256)(128)(2,1)}, u32[]{:S(2)}) copy-start(bf16[128]{0:T(256)(128)(2,1)} %param.29) | copy-start | bytes 772
  82.0 35.9 %copy-start.11 = (bf16[2048,128]{1,0:T(8,128)(2,1)S(1)}, bf16[2048,128]{1,0:T(8,128)(2,1)}, u32[]{:S(2)}) copy-start(bf16[2048,128]{1,0:T(8,128)(2,1)} %param.30) | copy-start | bytes 1572868
  116.1 183.3 %reduce-scatter.3.cloned.1.call-start = ((), (), s32[]{:S(2)}) async-start(), calls=%async_computation.5 | async-start | bytes 8650752 | tf_op jit(solution)/shard_map/reduce_scatter | solution.py:236
  117.9 6.3 copy-start.24
  171.1 20.7 %copy-start.12 = (bf16[128,2048]{1,0:T(8,128)(2,1)S(1)}, bf16[128,2048]{1,0:T(8,128)(2,1)}, u32[]{:S(2)}) copy-start(bf16[128,2048]{1,0:T(8,128)(2,1)} %param.32) | copy-start | bytes 1572868
  209.1 90.2 %copy-start.2 = (bf16[64,2048]{1,0:T(8,128)(2,1)S(1)}, bf16[64,2048]{1,0:T(8,128)(2,1)}, u32[]{:S(2)}) copy-start(bf16[64,2048]{1,0:T(8,128)(2,1)} %param.25) | copy-start | bytes 786436
  209.2 93.2 %copy-start.15 = (f32[2048,8]{0,1:T(8,128)S(1)}, f32[2048,8]{0,1:T(8,128)}, u32[]{:S(2)}) copy-start(f32[2048,8]{0,1:T(8,128)} %param.47) | copy-start | bytes 196612
  209.2 93.3 %copy-start.14 = (s32[2048,8]{0,1:T(8,128)S(1)}, s32[2048,8]{0,1:T(8,128)}, u32[]{:S(2)}) copy-start(s32[2048,8]{0,1:T(8,128)} %param.46) | copy-start | bytes 196612
  209.2 1083.8 %all-gather.12.cloned.1.call-start = ((), (), s32[]{:S(2)}) async-start(), calls=%async_computation.6 | async-start | bytes 8650752 | tf_op jit(solution)/shard_map/all_gather | solution.py:252
  302.3 1149.5 %reduce-scatter.5.cloned.1.call-start = ((), (), s32[]{:S(2)}) async-start(), calls=%async_computation.7 | async-start | bytes 8650752 | tf_op jit(solution)/shard_map/reduce_scatter | solution.py:264
  303.3 30.4 %copy-start.20 = (s32[2]{0:T(128)S(1)}, s32[2]{0:T(128)}, u32[]{:S(2)}) copy-start(s32[2]{0:T(128)} %constant.148) | copy-start | bytes 28
  304.2 29.6 %copy-start.19 = (s32[2]{0:T(128)S(1)}, s32[2]{0:T(128)}, u32[]{:S(2)}) copy-start(s32[2]{0:T(128)} %constant.151) | copy-start | bytes 28
  1359.7 92.2 %copy-start.1 = (bf16[16,16,2048]{2,1,0:T(8,128)(2,1)S(1)}, bf16[16,16,2048]{2,1,0:T(8,128)(2,1)}, u32[]{:S(2)}) copy-start(bf16[16,16,2048]{2,1,0:T(8,128)(2,1)} %param.40) | copy-start | bytes 3145732
  (14 other events, 30.7 us)
Sparse Core Ops, SparseCore 0:
  9.7 42.5 all-gather.7
  55.2 53.9 all-gather.5
  116.2 45.8 all-gather.9
  209.3 89.9 reduce-scatter.2
  302.4 54.3 all-gather.11
  1359.8 92.0 reduce-scatter.4
where the time goes:
time: 1460 us
  local copies, waits for them, and re-layouts  1000 us (68%)
  waiting for transfers between devices  269 us (18%)
  other arithmetic  75 us (5%)
  matrix products  70.9 us (5%)
  blocking collectives  25.8 us (2%)
  between operations  15.1 us (1%)
    unnamed x69, local copies, waits for them, and re-layouts  964 us
    reduce_scatter x1, waiting for transfers between devices, local(): lax.psum_scatter((adapter_contribution + ADAPTER_FACTOR * jnp.dot(jnp.whe...  89.5 us
    reduce_scatter x1, waiting for transfers between devices, local(): lax.psum_scatter(moe_terms.astype(jnp.bfloat16), 'tensor', scatter_dimens...  81.8 us
    all_gather x1, waiting for transfers between devices, local(): every_kv = lax.all_gather(resident_key_value, 'tensor', axis=2, tiled=True)  37.3 us
    all_gather x1, waiting for transfers between devices, local(): piece = lax.all_gather(shrink_qkv, 'dp', axis=0, tiled=True)  32 us
  transfers between devices with their start and end apart: 6, of which 5 were waited for; matrix products, arithmetic and copies ran while one was open for 70% of the time, Pallas kernels for 0%

commit v1 on v0

--- a/solution.py
+++ b/solution.py
@@ -64,29 +64,6 @@
     match = adapter_position[:, None] == jnp.arange(adapters, dtype=jnp.int32)[None, :]
     placed = jnp.where(match[:, :, None], values[:, None, :], jnp.zeros((), values.dtype))
     return placed.reshape(values.shape[0], -1)
-
-
-def routing(chosen, gates, experts, capacity):
-    token_count = chosen.shape[0]
-    choose = chosen[:, :, None] == jnp.arange(experts, dtype=jnp.int32)[None, None, :]
-    share = gates / jnp.sum(gates, axis=1, keepdims=True)
-    weight = jnp.sum(jnp.where(choose, share[:, :, None], 0.0), axis=1)
-    hit = jnp.any(choose, axis=1)
-    place = jnp.cumsum(hit.astype(jnp.int32), axis=0) - 1
-    column = jnp.where(hit, place, capacity)
-    expert_grid = jnp.broadcast_to(jnp.arange(experts, dtype=jnp.int32)[None, :], hit.shape)
-    token_grid = jnp.broadcast_to(jnp.arange(token_count, dtype=jnp.int32)[:, None], hit.shape)
-    slot_token = (
-        jnp.zeros((experts, capacity + 1), jnp.int32)
-        .at[expert_grid, column]
-        .set(token_grid)[:, :capacity]
-    )
-    slot_weight = (
-        jnp.zeros((experts, capacity + 1), jnp.float32)
-        .at[expert_grid, column]
-        .set(weight)[:, :capacity]
-    )
-    return (slot_token, slot_weight)
 
 
 def attend(query_rows_out, keys, values, group, scale):
@@ -250,17 +227,36 @@
     moe_own = normalize(tokens.astype(jnp.float32) + attn_own, moe_gain).astype(jnp.bfloat16)
     experts_here = w_gate.shape[0]
     moe_in = lax.all_gather(moe_own, "tensor", axis=0, tiled=True)
-    capacity = CAP_DEV * parts
-    slot_token, slot_weight = routing(expert_ids, expert_gates, EXPERTS, capacity)
-    own_tokens = lax.dynamic_slice_in_dim(slot_token, place * experts_here, experts_here, 0)
-    own_weights = lax.dynamic_slice_in_dim(slot_weight, place * experts_here, experts_here, 0)
-    outputs = expert_apply(moe_in[own_tokens][None], w_gate, w_up, w_down)[0]
-    weighted = outputs.astype(jnp.float32) * own_weights[:, :, None]
-    moe_terms = (
-        jnp.zeros((grand_total, width), jnp.float32)
-        .at[own_tokens.reshape(-1)]
-        .add(weighted.reshape(-1, width))
-    )
+    own_experts = place * experts_here + jnp.arange(experts_here, dtype=jnp.int32)
+    choose = expert_ids[:, :, None] == own_experts[None, None, :]
+    share = expert_gates / jnp.sum(expert_gates, axis=1, keepdims=True)
+    weight = jnp.sum(jnp.where(choose, share[:, :, None], 0.0), axis=1)
+    hit = jnp.any(choose, axis=1).reshape(parts, own_rows, experts_here)
+    weight = weight.reshape(parts, own_rows, experts_here)
+    below = jnp.tril(jnp.ones((own_rows, own_rows), jnp.bfloat16))
+    rank_in_block = jnp.einsum(
+        "ut,ste->sue", below, hit.astype(jnp.bfloat16), preferred_element_type=jnp.float32
+    )
+    numbers = jnp.arange(1, CAP_DEV + 1, dtype=jnp.float32)
+    picked = hit[..., None] & (rank_in_block[..., None] == numbers)
+    pick = picked.astype(jnp.bfloat16)
+    slot_weight = jnp.sum(jnp.where(picked, weight[..., None], 0.0), axis=1)
+    rows = jnp.einsum(
+        "stek,std->eskd",
+        pick,
+        moe_in.reshape(parts, own_rows, width),
+        preferred_element_type=jnp.float32,
+    ).astype(jnp.bfloat16)
+    rows = rows.reshape(1, experts_here, parts * CAP_DEV, width)
+    outputs = expert_apply(rows, w_gate, w_up, w_down)[0]
+    slot_weight = slot_weight.transpose(1, 0, 2).reshape(experts_here, parts * CAP_DEV, 1)
+    weighted = (outputs.astype(jnp.float32) * slot_weight).astype(jnp.bfloat16)
+    moe_terms = jnp.einsum(
+        "stek,eskd->std",
+        pick,
+        weighted.reshape(experts_here, parts, CAP_DEV, width),
+        preferred_element_type=jnp.float32,
+    ).reshape(grand_total, width)
     moe_total = lax.psum_scatter(
         moe_terms.astype(jnp.bfloat16), "tensor", scatter_dimension=0, tiled=True
     )

time: 1460 us -> 501 us (0.34)
  local copies, waits for them, and re-layouts: 1000 us -> 30.3 us
  other arithmetic: 75 us -> 15.1 us
  waiting for transfers between devices: 269 us -> 319 us
    unnamed x69 -> x58, local copies, waits for them, and re-layouts: 964 us -> 8.03 us
    all_gather x1, waiting for transfers between devices: 0.02 us -> 52.7 us  [local(): moe_in = lax.all_gather(moe_own, 'tensor', axis=0, tiled=True)]
    another operation x4 -> x2, other arithmetic: 28.4 us -> 0.17 us
    scatter-add x1 -> x0, other arithmetic: 21.8 us -> none  [local(): moe_terms = jnp.zeros((grand_total, width), jnp.float32).at[own_tokens.re...]
  transfers between devices with their start and end apart: 6 -> 6, of which waited for: 5 -> 6; matrix products, arithmetic and copies ran while one was open for 70% -> 7% of each run, Pallas kernels for 0% -> 0%
where the time goes in v1:
time: 501 us; the launch traced here: 491 us
  waiting for transfers between devices  319 us (64%)
  matrix products  82.3 us (16%)
  local copies, waits for them, and re-layouts  30.3 us (6%)
  blocking collectives  25.8 us (5%)
  other arithmetic  15.1 us (3%)
  between operations  14.9 us (3%)
    reduce_scatter x1, waiting for transfers between devices, local(): lax.psum_scatter((adapter_contribution + ADAPTER_FACTOR * jnp.dot(jnp.whe...  89.5 us
    reduce_scatter x1, waiting for transfers between devices, local(): lax.psum_scatter(moe_terms.astype(jnp.bfloat16), 'tensor', scatter_dimens...  80 us
    all_gather x1, waiting for transfers between devices, local(): moe_in = lax.all_gather(moe_own, 'tensor', axis=0, tiled=True)  52.7 us
    all_gather x1, waiting for transfers between devices, local(): every_kv = lax.all_gather(resident_key_value, 'tensor', axis=2, tiled=True)  37.3 us
    all_gather x1, waiting for transfers between devices, local(): piece = lax.all_gather(shrink_qkv, 'dp', axis=0, tiled=True)  32 us
    all_gather x1, waiting for transfers between devices, local(): lax.all_gather(normed_own, 'tensor', axis=0, tiled=True)  27.2 us
    all_gather x1, blocking collectives, local(): lax.all_gather(shrunk_own, 'tensor', axis=0, tiled=True)  25.8 us
    dot_general x1, matrix products, expert_apply(): jnp.einsum('secf,efx->secx', hidden, down_rows, preferred_element_type=jn...  13.4 us
  transfers between devices with their start and end apart: 6, of which 6 were waited for; matrix products, arithmetic and copies ran while one was open for 7% of the time, Pallas kernels for 0%

profile of v1, /device:TPU:1, one launch (start us, length us, event | category | flops | bytes accessed | tf_op | source)
XLA Modules:
  0.0 491.3 jit_solution(7418017794389099014)
XLA Ops:
  12.7 5.8 %copy.123 = bf16[16,16,1024]{1,0,2:T(8,128)(2,1)} copy(bf16[16,16,1024]{2,1,0:T(8,128)(2,1)} %param.39) | data formatting | bytes 1048576 | tf_op jit(solution)/shard_map/reshape | solution.py:156
  20.3 32.0 %all-gather.8.cloned.1.call-done = bf16[16,48,2048]{2,1,0:T(8,128)(2,1)} async-done(((bf16[4,48,2048]{2,1,0:T(8,128)(2,1)}), bf16[16,48,2048]{2,1,0:T(8,128)(2,1)}) %all-gather.8.cloned.1.call-update) | async-done | bytes 3145744 | tf_op jit(solution)/shard_map/all_gather | solution.py:140
  52.3 2.9 fusion.37
  55.2 25.8 %all-gather = bf16[32,64,48]{1,2,0:T(8,128)(2,1)S(1)} all-gather(bf16[1,64,48]{1,2,0:T(8,128)(2,1)S(1)} %bitcast.218), channel_id=1, replica_groups=mesh['dp'=4,'tensor'=32] {'tensor'}, dimensions={0}, use_global_device_ids=true | all-gather | bytes 202752 | tf_op jit(solution)/shard_map/all_gather | solution.py:147
  82.0 27.2 %all-gather.6.cloned.1.call-done = bf16[2048,2048]{1,0:T(8,128)(2,1)} async-done(((bf16[64,2048]{1,0:T(8,128)(2,1)}), bf16[2048,2048]{1,0:T(8,128)(2,1)}) %all-gather.6.cloned.1.call-update) | async-done | bytes 8388624 | tf_op jit(solution)/shard_map/all_gather | solution.py:146
  109.2 5.9 %fusion.28 = f32[2048,4,8]{0,2,1:T(8,128)S(1)} fusion(bf16[2048,2048]{1,0:T(8,128)(2,1)} %all-gather.6.cloned.1.call-done, bf16[8,4,2048]{2,1,0:T(4,128)(2,1)S(1)} %copy-done.22), kind=kOutput, calls=%fused_computation.35 | convolution fusion | flops 268435456 | bytes 8781824 | tf_op jit(solution)/shard_map/td,chd->thc/dot_general | solution.py:153
  117.9 6.3 %fusion.89 = f32[2048,128]{0,1:T(8,128)S(1)} fusion(bf16[2048,2048]{1,0:T(8,128)(2,1)} %all-gather.6.cloned.1.call-done, bf16[2048,128]{1,0:T(8,128)(2,1)S(1)} %copy-done.12), kind=kOutput, calls=%fused_computation.159 | convolution fusion | flops 1073741824 | bytes 9961472 | tf_op jit(solution)/shard_map/dot_general | solution.py:193
  124.9 37.3 %all-gather.10.cloned.1.call-done = bf16[2048,4,256]{0,2,1:T(8,128)(2,1)} async-done(((bf16[2048,4,8]{0,2,1:T(8,128)(2,1)}), bf16[2048,4,256]{0,2,1:T(8,128)(2,1)}) %all-gather.10.cloned.1.call-update) | async-done | bytes 4194320 | tf_op jit(solution)/shard_map/all_gather | solution.py:177
  163.8 3.4 fusion.67
  171.1 19.9 %while.11 = (s32[]{:T(128)}, bf16[4,512,128]{2,1,0:T(8,128)(2,1)S(1)}, s32[4]{0:T(128)S(1)}, s32[2048]{0:T(1024)S(1)}, bf16[2048,1,128]{0,2,1:T(8,128)(2,1)}, /*...) while((s32[]{:T(128)}, ...), condition=%wide.region_13.14_spmd.clone, body=%wide.region_11.13_spmd.clone.sunk | while | flops 545325056 | bytes 11819227 | solution.py:90
  172.4 2.8 fusion.127
  177.4 2.8 fusion.127
  182.4 2.8 fusion.127
  187.3 2.8 fusion.127
  191.8 3.5 fusion.90
  197.1 12.1 %add_convert_fusion = bf16[2048,2048]{1,0:T(8,128)(2,1)} fusion(f32[2048,2048]{1,0:T(8,128)S(1)} %fusion.90, f32[2048,256]{1,0:T(8,128)} %convolution_select_fusion, bf16[256,2048]{1,0:T(8,128)(2,1)S(1)} %bitcast.197), kind=kOutput, calls=%fused_computation.16 | convolution fusion | flops 12897484800 | bytes 28311552 | tf_op jit(solution)/shard_map/dot_general | solution.py:217
  209.8 89.5 %reduce-scatter.3.cloned.1.call-done = bf16[64,2048]{1,0:T(8,128)(2,1)} async-done(((bf16[2048,2048]{1,0:T(8,128)(2,1)}), bf16[64,2048]{1,0:T(8,128)(2,1)}) %reduce-scatter.3.cloned.1.call-update) | async-done | bytes 262160 | tf_op jit(solution)/shard_map/reduce_scatter | solution.py:213
  304.1 52.7 %all-gather.12.cloned.1.call-done = bf16[2048,2048]{1,0:T(8,128)(2,1)} async-done(((bf16[64,2048]{1,0:T(8,128)(2,1)}), bf16[2048,2048]{1,0:T(8,128)(2,1)}) %all-gather.12.cloned.1.call-update) | async-done | bytes 8388624 | tf_op jit(solution)/shard_map/all_gather | solution.py:229
  356.8 4.6 fusion.91
  364.5 7.9 %fusion.92 = f32[2,512,768]{2,1,0:T(8,128)} fusion(bf16[2,512,2048]{2,1,0:T(8,128)(2,1)S(1)} %bitcast.208, bf16[2,768,2048]{2,1,0:T(8,128)(2,1)} %param.34), kind=kOutput, calls=%fused_computation.162 | convolution fusion | flops 3221225472 | bytes 13631488 | tf_op jit(solution)/shard_map/secx,efx->secf/dot_general | solution.py:97
  372.4 13.4 %convert_bitcast_fusion = bf16[1,2,512,2048]{3,2,1,0:T(8,128)(2,1)} fusion(bf16[2,768,2048]{2,1,0:T(8,128)(2,1)} %param.35, f32[2,512,768]{2,1,0:T(8,128)} %fusion.92, bf16[2,512,2048]{2,1,0:T(8,128)(2,1)} %bitcast.209, bf16[2,768,2048]{2,1,0:T(8,128)(2,1)} %param.33), kind=kOutput, calls=%fused_computation.22 | convolution fusion | flops 6449266688 | bytes 24117248 | tf_op jit(solution)/shard_map/secf,efx->secx/dot_general | solution.py:99
  385.9 7.9 %bitcast_convert_fusion = bf16[32,64,2048]{2,1,0:T(8,128)(2,1)} fusion(f32[2,32,16]{2,0,1:T(2,128)S(1)} %bitcast.215, f32[32,64,2]{1,2,0:T(2,128)S(1)} %copy.115, f32[16]{0:T(128)S(1)} %iota_add_fusion.1, pred[32,64,2]{1,2,0:T(4,128)(4,1)S(1)} %copy.114, bf16[2,32,16,2048]{3,2,1,0:T(8,128)(2,1)} %bitcast.206), kind=kOutput, calls=%fused_computation.15 | convolution fusion | flops 279052288 | bytes 12607552 | tf_op jit(solution)/shard_map/stek,eskd->std/dot_general | solution.py:254
  395.9 6.8 %scatter_custom_fusion = bf16[8192,32]{1,0:T(8,128)(2,1)S(1)} fusion(s32[2048]{0:T(1024)S(1)} %bitcast.220, bf16[2048,32]{1,0:T(8,128)(2,1)} %copy.119, bf16[]{:T(256)} %constant.56.clone.1), kind=kCustom, calls=%fused_computation.53 | custom fusion | bytes 524800 | tf_op jit(solution)/shard_map/scatter | solution.py:189
  404.2 80.0 %reduce-scatter.5.cloned.1.call-done = bf16[64,2048]{1,0:T(8,128)(2,1)} async-done(((bf16[2048,2048]{1,0:T(8,128)(2,1)}), bf16[64,2048]{1,0:T(8,128)(2,1)}) %reduce-scatter.5.cloned.1.call-update) | async-done | bytes 262160 | tf_op jit(solution)/shard_map/reduce_scatter | solution.py:260
  (163 shorter events, 37.7 us)
Async XLA Ops:
  7.2 189.9 %copy-start = (bf16[16,16,2048]{2,1,0:T(8,128)(2,1)S(1)}, bf16[16,16,2048]{2,1,0:T(8,128)(2,1)}, u32[]{:S(2)}) copy-start(bf16[16,16,2048]{2,1,0:T(8,128)(2,1)} %param.40) | copy-start | bytes 3145732
  7.2 12.5 %copy-start.20 = (s32[1,32]{1,0:T(1,128)S(1)}, s32[1,32]{1,0:T(1,128)}, u32[]{:S(2)}) copy-start(s32[1,32]{1,0:T(1,128)} %param.41) | copy-start | bytes 388
  7.2 12.3 %copy-start.24 = (s32[16]{0:T(128)S(1)}, s32[16]{0:T(128)}, u32[]{:S(2)}) copy-start(s32[16]{0:T(128)} %param.44) | copy-start | bytes 196
  7.2 12.3 %copy-start.25 = (s32[1,32]{1,0:T(1,128)S(1)}, s32[1,32]{1,0:T(1,128)}, u32[]{:S(2)}) copy-start(s32[1,32]{1,0:T(1,128)} %param.43) | copy-start | bytes 388
  7.2 12.4 %copy-start.18 = (s32[1,32]{1,0:T(1,128)S(1)}, s32[1,32]{1,0:T(1,128)}, u32[]{:S(2)}) copy-start(s32[1,32]{1,0:T(1,128)} %param.42) | copy-start | bytes 388
  7.2 45.1 %all-gather.8.cloned.1.call-start = ((), (), s32[]{:S(2)}) async-start(), calls=%async_computation.3 | async-start | bytes 3932160 | tf_op jit(solution)/shard_map/all_gather | solution.py:140
  8.0 101.2 %all-gather.6.cloned.1.call-start = ((), (), s32[]{:S(2)}) async-start(), calls=%async_computation.2 | async-start | bytes 8650752 | tf_op jit(solution)/shard_map/all_gather | solution.py:146
  11.6 40.7 %copy-start.6 = (bf16[64,2048]{1,0:T(8,128)(2,1)S(1)}, bf16[64,2048]{1,0:T(8,128)(2,1)}, u32[]{:S(2)}) copy-start(bf16[64,2048]{1,0:T(8,128)(2,1)} %fusion.62) | copy-start | bytes 786436
  11.6 150.5 %all-gather.10.cloned.1.call-start = ((), (), s32[]{:S(2)}) async-start(), calls=%async_computation.4 | async-start | bytes 4325376 | tf_op jit(solution)/shard_map/all_gather | solution.py:177
  20.3 88.9 %copy-start.22 = (bf16[8,4,2048]{2,1,0:T(4,128)(2,1)S(1)}, bf16[8,4,2048]{2,1,0:T(4,128)(2,1)}, u32[]{:S(2)}) copy-start(bf16[8,4,2048]{2,1,0:T(4,128)(2,1)} %param.31) | copy-start | bytes 393220
  82.0 34.2 %copy-start.26 = (bf16[128]{0:T(256)(128)(2,1)S(1)}, bf16[128]{0:T(256)(128)(2,1)}, u32[]{:S(2)}) copy-start(bf16[128]{0:T(256)(128)(2,1)} %param.28) | copy-start | bytes 772
  82.0 34.2 %copy-start.27 = (bf16[128]{0:T(256)(128)(2,1)S(1)}, bf16[128]{0:T(256)(128)(2,1)}, u32[]{:S(2)}) copy-start(bf16[128]{0:T(256)(128)(2,1)} %param.29) | copy-start | bytes 772
  82.0 35.9 %copy-start.12 = (bf16[2048,128]{1,0:T(8,128)(2,1)S(1)}, bf16[2048,128]{1,0:T(8,128)(2,1)}, u32[]{:S(2)}) copy-start(bf16[2048,128]{1,0:T(8,128)(2,1)} %param.30) | copy-start | bytes 1572868
  116.1 183.3 %reduce-scatter.3.cloned.1.call-start = ((), (), s32[]{:S(2)}) async-start(), calls=%async_computation.5 | async-start | bytes 8650752 | tf_op jit(solution)/shard_map/reduce_scatter | solution.py:213
  117.9 6.3 %copy-start.23 = (bf16[16,16,128]{2,1,0:T(8,128)(2,1)S(1)}, bf16[16,16,128]{2,1,0:T(8,128)(2,1)}, u32[]{:S(2)}) copy-start(bf16[16,16,128]{2,1,0:T(8,128)(2,1)} %param.38) | copy-start | bytes 196612
  167.2 3.9 copy-start.7
  171.1 20.7 %copy-start.13 = (bf16[128,2048]{1,0:T(8,128)(2,1)S(1)}, bf16[128,2048]{1,0:T(8,128)(2,1)}, u32[]{:S(2)}) copy-start(bf16[128,2048]{1,0:T(8,128)(2,1)} %param.32) | copy-start | bytes 1572868
  191.8 3.5 copy-start.17
  209.1 90.2 %copy-start.3 = (bf16[64,2048]{1,0:T(8,128)(2,1)S(1)}, bf16[64,2048]{1,0:T(8,128)(2,1)}, u32[]{:S(2)}) copy-start(bf16[64,2048]{1,0:T(8,128)(2,1)} %param.25) | copy-start | bytes 786436
  209.1 93.7 %copy-start.16 = (s32[2048,8]{0,1:T(8,128)S(1)}, s32[2048,8]{0,1:T(8,128)}, u32[]{:S(2)}) copy-start(s32[2048,8]{0,1:T(8,128)} %param.46) | copy-start | bytes 196612
  209.1 94.1 %copy-start.15 = (f32[2048,8]{0,1:T(8,128)S(1)}, f32[2048,8]{0,1:T(8,128)}, u32[]{:S(2)}) copy-start(f32[2048,8]{0,1:T(8,128)} %param.47) | copy-start | bytes 196612
  209.2 147.6 %all-gather.12.cloned.1.call-start = ((), (), s32[]{:S(2)}) async-start(), calls=%async_computation.6 | async-start | bytes 8650752 | tf_op jit(solution)/shard_map/all_gather | solution.py:229
  302.3 181.9 %reduce-scatter.5.cloned.1.call-start = ((), (), s32[]{:S(2)}) async-start(), calls=%async_computation.7 | async-start | bytes 8650752 | tf_op jit(solution)/shard_map/reduce_scatter | solution.py:260
  393.8 90.4 %copy-start.1 = (bf16[16,16,2048]{2,1,0:T(8,128)(2,1)S(1)}, bf16[16,16,2048]{2,1,0:T(8,128)(2,1)}, u32[]{:S(2)}) copy-start(bf16[16,16,2048]{2,1,0:T(8,128)(2,1)} %param.40) | copy-start | bytes 3145732
  (13 other events, 25.3 us)
Sparse Core Ops, SparseCore 0:
  9.7 42.5 all-gather.7
  55.2 53.9 all-gather.5
  116.2 45.8 all-gather.9
  209.3 89.9 reduce-scatter.2
  302.4 54.3 all-gather.11
  393.9 90.2 reduce-scatter.4

commit v2 on v1

--- a/solution.py
+++ b/solution.py
@@ -1,18 +1,243 @@
+import functools
 import math
-
-import jax
-import jax.numpy as jnp
+import jax, jax.numpy as jnp
 from jax import lax
+from jax.experimental import pallas as pl
+from jax.experimental.pallas import tpu as pltpu
 from jax.sharding import PartitionSpec as P
 
-EXPERTS = 64
-PAGE = 128
-CAP_DEV = 16
-
-
+SIDE = 4
+HALF = 32
+
+def spot(z, y, core):
+    return lax.rem(z, SIDE) * 8 + lax.rem(y, SIDE) * 2 + core
+
+def whereabouts():
+    me = lax.axis_index("tensor")
+    return me, lax.div(me, 8), lax.rem(lax.div(me, 2), SIDE), lax.rem(me, 2)
+
+def greet(partners):
+    barrier = pltpu.get_barrier_semaphore()
+    for partner in partners:
+        pl.semaphore_signal(barrier, inc=1, device_id={"tensor": partner}, device_id_type=pl.DeviceIdType.MESH)
+    pl.semaphore_wait(barrier, len(partners))
+
+class Copies:
+    def __init__(self, send, recv):
+        self.send, self.recv, self.n, self.all = send, recv, 0, []
+    def make(self, src, dst, axis, target):
+        k = self.n
+        self.n += 1
+        copy = pltpu.make_async_remote_copy(src_ref=src, dst_ref=dst, send_sem=self.send.at[k], recv_sem=self.recv.at[k],
+            device_id={axis: target}, device_id_type=pl.DeviceIdType.MESH)
+        self.all.append(copy)
+        return copy
+    def go(self, src, dst, axis, target):
+        copy = self.make(src, dst, axis, target)
+        copy.start()
+        return copy
+    def finish(self):
+        for copy in self.all:
+            copy.wait_send()
+
+def gather_rows(out, z, y, core, copies, hooks=()):
+    hooks = list(hooks)
+    def hook():
+        if hooks:
+            hooks.pop(0)()
+    side = spot(z, y, 1 - core)
+    shared = []
+    def share(block, row, rows):
+        piece = out.at[block, pl.ds(row, rows)]
+        shared.append(copies.go(piece, piece, "tensor", side))
+    def send(block, row, rows, target):
+        piece = out.at[block, pl.ds(row, rows)]
+        return copies.go(piece, piece, "tensor", target)
+    class Part: pass
+    parts = []
+    for number in range(2):
+        p = Part()
+        p.row = number * HALF
+        if number == 0:
+            p.at = lambda u, v: spot(z + v, y + u, core)
+        else:
+            p.at = lambda u, v: spot(z + u, y + v, core)
+        parts.append(p)
+    def ring_open(p, along_u, u):
+        block = p.at(u, 0)
+        up, down = (p.at(1, 0), p.at(3, 0)) if along_u else (p.at(0, 1), p.at(0, 3))
+        return [send(block, p.row, HALF, up), send(block, p.row, HALF, down)]
+    def ring_pass(p, along_u, u, opened, which):
+        opened[which].wait_recv()
+        off = 3 if which == 0 else 1
+        block = p.at(off, 0) if along_u else p.at(u, off)
+        target = (p.at(1, 0), p.at(3, 0))[which] if along_u else (p.at(0, 1), p.at(0, 3))[which]
+        fwd = send(block, p.row + which * (HALF // 2), HALF // 2, target)
+        share(block, p.row, HALF)
+        return fwd
+    me = spot(z, y, core)
+    for p in parts:
+        p.u = ring_open(p, True, 0)
+    for p in parts:
+        p.v = {0: ring_open(p, False, 0)}
+    share(me, 0, 2 * HALF)
+    hook()
+    for which in range(2):
+        for p in parts:
+            p.u.append(ring_pass(p, True, 0, p.u, which))
+            off = 3 if which == 0 else 1
+            p.v[off] = ring_open(p, False, off)
+    for which in range(2):
+        for p in parts:
+            p.v[0].append(ring_pass(p, False, 0, p.v[0], which))
+    hook()
+    for p in parts:
+        p.u[2].wait_recv()
+        p.u[3].wait_recv()
+        share(p.at(2, 0), p.row, HALF)
+        p.v[2] = ring_open(p, False, 2)
+    for off in (3, 1):
+        for which in range(2):
+            for p in parts:
+                p.v[off].append(ring_pass(p, False, off, p.v[off], which))
+        for p in parts:
+            done = 0 if off == 3 else 3
+            p.v[done][2].wait_recv()
+            p.v[done][3].wait_recv()
+            share(p.at(done, 2), p.row, HALF)
+        hook()
+    for which in range(2):
+        for p in parts:
+            p.v[2].append(ring_pass(p, False, 2, p.v[2], which))
+    for off in (1, 2):
+        for p in parts:
+            p.v[off][2].wait_recv()
+            p.v[off][3].wait_recv()
+            share(p.at(off, 2), p.row, HALF)
+    for copy in shared:
+        copy.wait_recv()
+
+def add_rows(dst, start, rows, sources):
+    for first in range(0, rows, 16):
+        total = dst[pl.ds(start + first, 16)].astype(jnp.float32)
+        for ref, row in sources:
+            total = total + ref[pl.ds(row + first, 16)].astype(jnp.float32)
+        dst[pl.ds(start + first, 16)] = total.astype(dst.dtype)
+
+ORDER = (2, 1, 3, 0)
+SCATTER_COPIES = 32 + 32 + 8
+
+def scatter_rows(terms, acc, sib, landed, local, z, y, core, copies, result):
+    side = spot(z, y, 1 - core)
+    loads, shared = {}, {}
+    def cell(number, v, u):
+        return (v, u) if number == 0 else (u, v)
+    for v in ORDER:
+        for u in ORDER:
+            for number in range(2):
+                i, j = cell(number, v, u)
+                rows = pl.ds(number * HALF, HALF)
+                shared[number, v, u] = copies.go(
+                    terms.at[spot(z + i, y + j, 1 - core), rows], sib.at[i, j, rows], "tensor", side)
+                load = pltpu.make_async_copy(
+                    terms.at[spot(z + i, y + j, core), rows], acc.at[i, j, rows], local.at[number * 16 + v * 4 + u])
+                load.start()
+                loads[number, v, u] = load
+    def neighbour(number, along_v, step):
+        along_z = (number == 0) == along_v
+        return spot(z + step, y, core) if along_z else spot(z, y + step, core)
+    def own(number, v, u):
+        return acc.at[cell(number, v, u)]
+    def pair(number, v, u):
+        loads[number, v, u].wait()
+        shared[number, v, u].wait_recv()
+        return (sib.at[cell(number, v, u)], number * HALF)
+    def buf(number, u):
+        return landed.at[number * 5 + u]
+    ring = {}
+    def far(number, along_v, u, block):
+        row = number * HALF
+        b = buf(number, u)
+        key = (number, u)
+        ring[key] = [
+            copies.go(block.at[pl.ds(row, 16)], b.at[pl.ds(0, 16)], "tensor", neighbour(number, along_v, 1)),
+            copies.go(block.at[pl.ds(row + 16, 16)], b.at[pl.ds(16, 16)], "tensor", neighbour(number, along_v, 3)),
+        ]
+    def near(number, along_v, u, block, which):
+        row = number * HALF
+        b = buf(number, u)
+        ring[number, u].append(
+            copies.go(block.at[pl.ds(row, HALF)], b.at[pl.ds(32 + 32 * which, HALF)], "tensor",
+                      neighbour(number, along_v, (1, 3)[which])))
+    for u in ORDER:
+        for number in range(2):
+            block = own(number, 2, u)
+            add_rows(block, number * HALF, HALF, [pair(number, 2, u)])
+            far(number, True, u, block)
+    for u in ORDER:
+        for number in range(2):
+            row = number * HALF
+            for which in range(2):
+                v = (1, 3)[which]
+                block = own(number, v, u)
+                other, first = pair(number, v, u)
+                ring[number, u][which].wait_recv()
+                for part in range(2):
+                    sources = [(other, first + 16 * part)]
+                    if part == which:
+                        sources.append((buf(number, u), 16 * which))
+                    add_rows(block, row + 16 * part, 16, sources)
+                near(number, True, u, block, which)
+    for u in ORDER:
+        for number in range(2):
+            row = number * HALF
+            block = own(number, 0, u)
+            source = pair(number, 0, u)
+            b = buf(number, u)
+            ring[number, u][2].wait_recv()
+            ring[number, u][3].wait_recv()
+            sources = [source, (b, 32), (b, 64)]
+            last = buf(number, 4)
+            if u == 2:
+                add_rows(block, row, HALF, sources)
+                far(number, False, 4, block)
+            elif u in (1, 3):
+                which = (1, 3).index(u)
+                ring[number, 4][which].wait_recv()
+                for part in range(2):
+                    more = [(ref, r + 16 * part) for ref, r in sources]
+                    if part == which:
+                        more.append((last, 16 * which))
+                    add_rows(block, row + 16 * part, 16, more)
+                near(number, False, 4, block, which)
+            else:
+                ring[number, 4][2].wait_recv()
+                ring[number, 4][3].wait_recv()
+                for first in range(0, HALF, 16):
+                    total = block[pl.ds(row + first, 16)].astype(jnp.float32)
+                    for ref, r in sources + [(last, 32), (last, 64)]:
+                        total = total + ref[pl.ds(r + first, 16)].astype(jnp.float32)
+                    result[pl.ds(row + first, 16)] = total
+
+def scatter_scratch(width):
+    return [
+        pltpu.VMEM((4, 4, 64, width), jnp.bfloat16),
+        pltpu.VMEM((4, 4, 64, width), jnp.bfloat16),
+        pltpu.VMEM((10, 96, width), jnp.bfloat16),
+        pltpu.SemaphoreType.DMA((32,)),
+    ]
+
+def partners(z, y, core):
+    return [spot(z, y, 1 - core), spot(z + 1, y, core), spot(z + 3, y, core), spot(z, y + 1, core), spot(z, y + 3, core)]
+
+
+GATHER_COPIES = 2 * 20 + 31
+EXTRA_COPIES = 7 + 11
 NORM_EPS = 1e-06
 ROPE_BASE = 1000000.0
 ADAPTER_FACTOR = 0.5
+PAGE = 128
+CAP_DEV = 16
 
 
 def normalize(values, gain):
@@ -21,6 +246,200 @@
         * lax.rsqrt(jnp.mean(values * values, axis=-1, keepdims=True) + NORM_EPS)
         * gain.astype(jnp.float32)
     )
+
+
+def enter_kernel(
+    tokens_ref, gain_ref, shrink_ref, wkv_ref, rows_ref, factors_ref, wkv_all_ref, local, send, recv
+):
+    me, z, y, core = whereabouts()
+    group = lax.axis_index("dp")
+    up, down = lax.rem(group + 1, SIDE), lax.rem(group + 3, SIDE)
+    across = lax.rem(group + 2, SIDE)
+    copies = Copies(send, recv)
+    homes = [
+        pltpu.make_async_copy(shrink_ref, factors_ref.at[pl.ds(4 * group, 4)], local.at[0]),
+        pltpu.make_async_copy(wkv_ref.at[z], wkv_all_ref.at[y, core, z], local.at[1]),
+    ]
+    for home in homes:
+        home.start()
+    rows_ref[me] = normalize(tokens_ref[...].astype(jnp.float32), gain_ref[...]).astype(
+        rows_ref.dtype
+    )
+    barrier = pltpu.get_barrier_semaphore()
+    near = partners(z, y, core) + [spot(z + 2, y, core)]
+    for partner in near:
+        pl.semaphore_signal(
+            barrier, inc=1, device_id={"tensor": partner}, device_id_type=pl.DeviceIdType.MESH
+        )
+    for partner in (up, down):
+        pl.semaphore_signal(
+            barrier, inc=1, device_id={"dp": partner}, device_id_type=pl.DeviceIdType.MESH
+        )
+    pl.semaphore_wait(barrier, len(near) + 2)
+    side = spot(z, y, 1 - core)
+    state = {}
+
+    def open_extras():
+        spread = []
+        for step in (1, 3, 2):
+            there = lax.rem(z + step, SIDE)
+            spread.append(
+                copies.go(
+                    wkv_ref.at[there], wkv_all_ref.at[y, core, z], "tensor", spot(there, y, core)
+                )
+            )
+        state["spread"] = spread
+        half = factors_ref.at[pl.ds(4 * group + 2 * core, 2)]
+        mine = shrink_ref.at[pl.ds(2 * core, 2)]
+        state["factors"] = [copies.go(mine, half, "dp", up), copies.go(mine, half, "dp", down)]
+
+    def kv(y_at, first=0, count=4):
+        return wkv_all_ref.at[lax.rem(y_at, SIDE), core, pl.ds(first, count)]
+
+    def middle_extras():
+        for copy in state["spread"]:
+            copy.wait_recv()
+        homes[1].wait()
+        block = kv(y)
+        state["kv"] = [
+            copies.go(block, block, "tensor", spot(z, y + 1, core)),
+            copies.go(block, block, "tensor", spot(z, y + 3, core)),
+        ]
+        state["shared"] = [copies.go(block, block, "tensor", side)]
+        for which, (origin, target) in enumerate(((down, up), (up, down))):
+            state["factors"][which].wait_recv()
+            one = factors_ref.at[4 * origin + 2 * core + which]
+            state["factors"].append(copies.go(one, one, "dp", target))
+            both = factors_ref.at[pl.ds(4 * origin + 2 * core, 2)]
+            state["shared"].append(copies.go(both, both, "tensor", side))
+
+    def pass_extras():
+        for which, (origin, target) in enumerate(((y + 3, y + 1), (y + 1, y + 3))):
+            state["kv"][which].wait_recv()
+            piece = kv(origin, 2 * which, 2)
+            state["kv"].append(copies.go(piece, piece, "tensor", spot(z, target, core)))
+            whole = kv(origin)
+            state["shared"].append(copies.go(whole, whole, "tensor", side))
+        state["factors"][2].wait_recv()
+        state["factors"][3].wait_recv()
+        both = factors_ref.at[pl.ds(4 * across + 2 * core, 2)]
+        state["shared"].append(copies.go(both, both, "tensor", side))
+
+    def close_extras():
+        state["kv"][2].wait_recv()
+        state["kv"][3].wait_recv()
+        whole = kv(y + 2)
+        state["shared"].append(copies.go(whole, whole, "tensor", side))
+
+    open_extras()
+    gather_rows(rows_ref, z, y, core, copies, [middle_extras, pass_extras, close_extras])
+    for copy in state["shared"]:
+        copy.wait_recv()
+    homes[0].wait()
+    copies.finish()
+    assert copies.n == GATHER_COPIES + EXTRA_COPIES, copies.n
+
+
+def enter(tokens, gain, shrink, wkv):
+    rows, width = tokens.shape
+    count = GATHER_COPIES + EXTRA_COPIES
+    return pl.pallas_call(
+        enter_kernel,
+        out_shape=(
+            jax.ShapeDtypeStruct((32, rows, width), jnp.bfloat16),
+            jax.ShapeDtypeStruct((4 * shrink.shape[0],) + shrink.shape[1:], jnp.bfloat16),
+            jax.ShapeDtypeStruct((4, 2) + wkv.shape, jnp.bfloat16),
+        ),
+        in_specs=[
+            pl.BlockSpec(memory_space=pltpu.VMEM),
+            pl.BlockSpec(memory_space=pltpu.VMEM),
+            pl.BlockSpec(memory_space=pl.ANY),
+            pl.BlockSpec(memory_space=pl.ANY),
+        ],
+        out_specs=(
+            pl.BlockSpec(memory_space=pltpu.VMEM),
+            pl.BlockSpec(memory_space=pl.ANY),
+            pl.BlockSpec(memory_space=pl.ANY),
+        ),
+        scratch_shapes=[
+            pltpu.SemaphoreType.DMA((2,)),
+            pltpu.SemaphoreType.DMA((count,)),
+            pltpu.SemaphoreType.DMA((count,)),
+        ],
+        compiler_params=pltpu.CompilerParams(
+            collective_id=0, has_side_effects=True, vmem_limit_bytes=32 << 20
+        ),
+    )(tokens, gain.reshape(1, width), shrink, wkv)
+
+
+def middle_kernel(
+    terms_ref, tokens_ref, gain_ref, out_ref, rows_ref, acc, sib, landed, local, total, send, recv
+):
+    me, z, y, core = whereabouts()
+    greet(partners(z, y, core))
+    copies = Copies(send, recv)
+    scatter_rows(terms_ref, acc, sib, landed, local, z, y, core, copies, total)
+    summed = total[...]
+    out_ref[...] = summed.astype(out_ref.dtype)
+    rows_ref[me] = normalize(tokens_ref[...].astype(jnp.float32) + summed, gain_ref[...]).astype(
+        rows_ref.dtype
+    )
+    gather_rows(rows_ref, z, y, core, copies)
+    copies.finish()
+    assert copies.n == SCATTER_COPIES + GATHER_COPIES, copies.n
+
+
+def middle(terms, tokens, gain):
+    rows, width = tokens.shape
+    count = SCATTER_COPIES + GATHER_COPIES
+    vmem = pl.BlockSpec(memory_space=pltpu.VMEM)
+    return pl.pallas_call(
+        middle_kernel,
+        out_shape=(
+            jax.ShapeDtypeStruct((rows, width), jnp.bfloat16),
+            jax.ShapeDtypeStruct((32, rows, width), jnp.bfloat16),
+        ),
+        in_specs=[pl.BlockSpec(memory_space=pl.ANY), vmem, vmem],
+        out_specs=(vmem, vmem),
+        scratch_shapes=scatter_scratch(width)
+        + [
+            pltpu.VMEM((rows, width), jnp.float32),
+            pltpu.SemaphoreType.DMA((count,)),
+            pltpu.SemaphoreType.DMA((count,)),
+        ],
+        compiler_params=pltpu.CompilerParams(
+            collective_id=1, has_side_effects=True, vmem_limit_bytes=40 << 20
+        ),
+    )(terms, tokens, gain.reshape(1, width))
+
+
+def leave_kernel(terms_ref, out_ref, acc, sib, landed, local, total, send, recv):
+    me, z, y, core = whereabouts()
+    greet(partners(z, y, core))
+    copies = Copies(send, recv)
+    scatter_rows(terms_ref, acc, sib, landed, local, z, y, core, copies, total)
+    out_ref[...] = total[...].astype(out_ref.dtype)
+    copies.finish()
+    assert copies.n == SCATTER_COPIES, copies.n
+
+
+def leave(terms):
+    rows, width = terms.shape[1:]
+    return pl.pallas_call(
+        leave_kernel,
+        out_shape=jax.ShapeDtypeStruct((rows, width), jnp.bfloat16),
+        in_specs=[pl.BlockSpec(memory_space=pl.ANY)],
+        out_specs=pl.BlockSpec(memory_space=pltpu.VMEM),
+        scratch_shapes=scatter_scratch(width)
+        + [
+            pltpu.VMEM((rows, width), jnp.float32),
+            pltpu.SemaphoreType.DMA((SCATTER_COPIES,)),
+            pltpu.SemaphoreType.DMA((SCATTER_COPIES,)),
+        ],
+        compiler_params=pltpu.CompilerParams(
+            collective_id=2, has_side_effects=True, vmem_limit_bytes=32 << 20
+        ),
+    )(terms)
 
 
 def rotate(values, position):
@@ -58,12 +477,6 @@
     cell = page * PAGE + offset % PAGE
     adapter_position = lookup(request, lookup(adapter_row, adapter_slot))
     return (group, rope_pos, cell, adapter_position)
-
-
-def spread_rows(values, adapter_position, adapters):
-    match = adapter_position[:, None] == jnp.arange(adapters, dtype=jnp.int32)[None, :]
-    placed = jnp.where(match[:, :, None], values[:, None, :], jnp.zeros((), values.dtype))
-    return placed.reshape(values.shape[0], -1)
 
 
 def attend(query_rows_out, keys, values, group, scale):
@@ -135,47 +548,41 @@
     group, rope_pos, cell, adapter_position = token_layout(
         lengths[0], groups[0], adapter_of_request[0], adapter_slot, page_table[0], grand_total
     )
-    own_slot = lax.dynamic_slice_in_dim(adapter_position, place * own_rows, own_rows, 0)
-    normed_own = normalize(tokens.astype(jnp.float32), attn_gain).astype(jnp.bfloat16)
-    piece = lax.all_gather(shrink_qkv, "dp", axis=0, tiled=True)
-    projected = jnp.einsum("td,prd->tpr", normed_own, piece, preferred_element_type=jnp.float32)
-    match = own_slot[:, None] == jnp.arange(piece.shape[0], dtype=jnp.int32)[None, :]
-    shrunk_own = jnp.sum(jnp.where(match[:, :, None], projected, 0.0), axis=1)
-    shrunk_own = shrunk_own.astype(jnp.bfloat16)
-    normalized_input, shrunken_rows = (
-        lax.all_gather(normed_own, "tensor", axis=0, tiled=True),
-        lax.all_gather(shrunk_own, "tensor", axis=0, tiled=True),
-    )
+    x_rows, factors, wkv_all = enter(tokens, attn_gain, shrink_qkv, w_kv.transpose(1, 0, 2))
+    normed = x_rows.reshape(grand_total, width)
     head = place * key_value_heads // parts
     local_cols = kv_width // parts
-    token_extent = w_kv.shape[0]
-    span_begin = place * token_extent
-    base_key_value = jnp.einsum(
-        "td,chd->thc", normalized_input, w_kv, preferred_element_type=jnp.float32
-    )
-    upward_split = key_value_up_factors.reshape(adapters, rank, key_value_heads, 2 * head_length)
-    upward_local = lax.dynamic_slice_in_dim(upward_split, span_begin, token_extent, 3).reshape(
-        adapters * rank, key_value_heads * token_extent
-    )
-    key_adapter_delta = jnp.dot(
-        spread_rows(shrunken_rows[:, rank : 2 * rank], adapter_position, adapters),
-        upward_local,
+    head_width = 2 * head_length
+    wkv_head = wkv_all.transpose(2, 0, 1, 3, 4).reshape(head_width, width)
+    ranks = 3 * rank
+    projected = lax.dot_general(
+        normed,
+        factors.reshape(adapters * ranks, width),
+        (((1,), (1,)), ((), ())),
         preferred_element_type=jnp.float32,
     )
-    value_adapter_delta = jnp.dot(
-        spread_rows(shrunken_rows[:, 2 * rank :], adapter_position, adapters),
-        upward_local,
+    slots = jnp.repeat(jnp.arange(adapters, dtype=jnp.int32), ranks)
+    placed = jnp.where(adapter_position[:, None] == slots[None, :], projected, 0.0).astype(
+        jnp.bfloat16
+    )
+    query_cols = query_weight.shape[1]
+    heads_here = query_cols // head_length
+    kv_up = lax.dynamic_slice_in_dim(key_value_up_factors, head * head_width, head_width, 2)
+    raise_table = jnp.zeros((adapters, 3, rank, query_cols + head_width), jnp.bfloat16)
+    raise_table = raise_table.at[:, 0, :, :query_cols].set(query_up_factors)
+    raise_table = raise_table.at[:, 1, :, query_cols : query_cols + head_length].set(
+        kv_up[:, :, :head_length]
+    )
+    raise_table = raise_table.at[:, 2, :, query_cols + head_length :].set(kv_up[:, :, head_length:])
+    lora = ADAPTER_FACTOR * jnp.dot(
+        placed,
+        raise_table.reshape(adapters * ranks, query_cols + head_width),
         preferred_element_type=jnp.float32,
     )
-    whether_key = jnp.tile(
-        span_begin + jnp.arange(token_extent, dtype=jnp.int32) < head_length, key_value_heads
-    )
-    adapter_delta_term = jnp.where(
-        whether_key[None, :], key_adapter_delta, value_adapter_delta
-    ).reshape(grand_total, key_value_heads, token_extent)
-    resident_key_value = (base_key_value + ADAPTER_FACTOR * adapter_delta_term).astype(jnp.bfloat16)
-    every_kv = lax.all_gather(resident_key_value, "tensor", axis=2, tiled=True)
-    head_kv = lax.dynamic_index_in_dim(every_kv, head, 1, keepdims=False)
+    base_kv = lax.dot_general(
+        normed, wkv_head, (((1,), (1,)), ((), ())), preferred_element_type=jnp.float32
+    )
+    head_kv = (base_kv + lora[:, query_cols:]).astype(jnp.bfloat16)
     divided_key_value = head_kv.reshape(grand_total, 2, head_length)
     keys = rotate(normalize(divided_key_value[:, :1].astype(jnp.float32), k_gain), rope_pos).astype(
         jnp.bfloat16
@@ -183,19 +590,13 @@
     values = divided_key_value[:, 1]
     entries = jnp.concatenate([keys, values], axis=1)
     mine = lax.dynamic_slice_in_dim(
-        entries, place * local_cols - head * 2 * head_length, local_cols, 1
+        entries, place * local_cols - head * head_width, local_cols, 1
     )
     pages_held = page_table.shape[1]
     kv_pages = jnp.zeros((pages_held * PAGE, local_cols), jnp.bfloat16).at[cell].set(mine)
     kv_pages = kv_pages.reshape(pages_held, PAGE, local_cols).transpose(0, 2, 1)
-    query_cols = query_weight.shape[1]
-    heads_here = query_cols // head_length
-    query_rows_out = jnp.dot(
-        normalized_input, query_weight, preferred_element_type=jnp.float32
-    ) + ADAPTER_FACTOR * jnp.dot(
-        spread_rows(shrunken_rows[:, :rank], adapter_position, adapters),
-        query_up_factors.reshape(adapters * rank, query_cols),
-        preferred_element_type=jnp.float32,
+    query_rows_out = (
+        jnp.dot(normed, query_weight, preferred_element_type=jnp.float32) + lora[:, :query_cols]
     )
     query_rows_out = rotate(
         normalize(query_rows_out.reshape(grand_total, heads_here, head_length), q_gain), rope_pos
@@ -210,23 +611,17 @@
         adapter_position[:, None] == jnp.arange(adapters, dtype=jnp.int32)[None, :], rank, axis=1
     )
     adapter_contribution = jnp.dot(mixed, w_o, preferred_element_type=jnp.float32)
-    attn_own = lax.psum_scatter(
-        (
-            adapter_contribution
-            + ADAPTER_FACTOR
-            * jnp.dot(
-                jnp.where(retained_mask, lower_rank_rows, 0.0),
-                upward_wide_rows,
-                precision=lax.Precision.HIGHEST,
-            )
-        ).astype(jnp.bfloat16),
-        "tensor",
-        scatter_dimension=0,
-        tiled=True,
-    ).astype(jnp.float32)
-    moe_own = normalize(tokens.astype(jnp.float32) + attn_own, moe_gain).astype(jnp.bfloat16)
+    attn_terms = (
+        adapter_contribution
+        + ADAPTER_FACTOR
+        * jnp.dot(
+            jnp.where(retained_mask, lower_rank_rows, 0.0),
+            upward_wide_rows,
+            precision=lax.Precision.HIGHEST,
+        )
+    ).astype(jnp.bfloat16)
+    attn_out, moe_in = middle(attn_terms.reshape(parts, own_rows, width), tokens, moe_gain)
     experts_here = w_gate.shape[0]
-    moe_in = lax.all_gather(moe_own, "tensor", axis=0, tiled=True)
     own_experts = place * experts_here + jnp.arange(experts_here, dtype=jnp.int32)
     choose = expert_ids[:, :, None] == own_experts[None, None, :]
     share = expert_gates / jnp.sum(expert_gates, axis=1, keepdims=True)
@@ -244,7 +639,7 @@
     rows = jnp.einsum(
         "stek,std->eskd",
         pick,
-        moe_in.reshape(parts, own_rows, width),
+        moe_in,
         preferred_element_type=jnp.float32,
     ).astype(jnp.bfloat16)
     rows = rows.reshape(1, experts_here, parts * CAP_DEV, width)
@@ -256,11 +651,9 @@
         pick,
         weighted.reshape(experts_here, parts, CAP_DEV, width),
         preferred_element_type=jnp.float32,
-    ).reshape(grand_total, width)
-    moe_total = lax.psum_scatter(
-        moe_terms.astype(jnp.bfloat16), "tensor", scatter_dimension=0, tiled=True
-    )
-    return (attn_own.astype(jnp.bfloat16), moe_total, kv_pages)
+    )
+    moe_total = leave(moe_terms.astype(jnp.bfloat16))
+    return (attn_out, moe_total, kv_pages)
 
 
 def solution(mesh):

time: 501 us -> 285 us (0.57); the launches traced: 491 us -> 281 us
  waiting for transfers between devices: 319 us -> 0 us
  Pallas kernels: 0 us -> 136 us
  blocking collectives: 25.8 us -> 0 us
  between operations: 14.9 us -> 1.36 us
  matrix products: 82.3 us -> 88.7 us
    reduce_scatter x2 -> x0, waiting for transfers between devices: 169 us -> none  [the longest x1 89.5 us: local(): lax.psum_scatter((adapter_contribution + ADAPTER_FACTOR * jnp.dot(jnp.whe...]
    all_gather x4 -> x0, waiting for transfers between devices: 149 us -> none  [the longest x1 52.7 us: local(): moe_in = lax.all_gather(moe_own, 'tensor', axis=0, tiled=True)]
    pallas_call x0 -> x3, Pallas kernels: none -> 136 us  [the longest x1 59.5 us: middle(): pl.pallas_call(middle_kernel, out_shape=(jax.ShapeDtypeStruct((rows, widt...]
    all_gather x1 -> x0, blocking collectives: 25.8 us -> none  [local(): lax.all_gather(shrunk_own, 'tensor', axis=0, tiled=True)]
    unnamed x58 -> x50, local copies, waits for them, and re-layouts: 8.03 us -> 15.7 us
    dot_general x6 -> x3, matrix products: 16.7 us -> 22.6 us  [the longest x1 13.2 us: local(): jnp.dot(placed, raise_table.reshape(adapters * ranks, query_cols + head_w...]
    dot_general x1, matrix products: 3.47 us -> 9.24 us  [local(): jnp.dot(mixed, w_o, preferred_element_type=jnp.float32)]
    reshape x3 -> x2, local copies, waits for them, and re-layouts: 6.66 us -> 1.39 us  [the longest x1 0.7 us: enter(): gain.reshape(1, width)]
  transfers between devices with their start and end apart: 6 -> 0, of which waited for: 6 -> 0; matrix products, arithmetic and copies ran while one was open for 7% -> 0% of each run, Pallas kernels for 0% -> 0%
where the time goes in v2:
time: 285 us; the launch traced here: 281 us
  Pallas kernels  136 us (48%)
  matrix products  88.7 us (31%)
  local copies, waits for them, and re-layouts  33.7 us (12%)
  other arithmetic  18.6 us (7%)
  loops' own time  3.26 us (1%)
    pallas_call x1, Pallas kernels, middle(): pl.pallas_call(middle_kernel, out_shape=(jax.ShapeDtypeStruct((rows, widt...  59.5 us
    pallas_call x1, Pallas kernels, enter(): pl.pallas_call(enter_kernel, out_shape=(jax.ShapeDtypeStruct((32, rows, w...  41.9 us
    pallas_call x1, Pallas kernels, leave(): pl.pallas_call(leave_kernel, out_shape=jax.ShapeDtypeStruct((rows, width)...  34.5 us
    unnamed x50, local copies, waits for them, and re-layouts  15.7 us
    dot_general x1, matrix products, expert_apply(): jnp.einsum('secf,efx->secx', hidden, down_rows, preferred_element_type=jn...  13.5 us
    dot_general x1, matrix products, local(): jnp.dot(placed, raise_table.reshape(adapters * ranks, query_cols + head_w...  13.2 us
    dot_general x1, matrix products, local(): jnp.dot(jnp.where(retained_mask, lower_rank_rows, 0.0), upward_wide_rows,...  13 us
    dot_general x4, matrix products, one_block(): jnp.einsum('qhd,kd->hqk', query_block, keys, preferred_element_type=jnp.f...  10.9 us

profile of v2, /device:TPU:1, one launch (start us, length us, event | category | flops | bytes accessed | tf_op | source)
XLA Modules:
  0.0 281.4 jit_solution(6824446637370932124)
XLA Ops:
  21.3 41.9 %shard_map.238 = (bf16[32,64,2048]{2,1,0:T(8,128)(2,1)S(1)}, bf16[16,48,2048]{2,1,0:T(8,128)(2,1)S(1)}, bf16[4,2,4,8,2048]{4,3,2,1,0:T(8,128)(2,1)S(1)}) custom-call(bf16[64,2048]{1,0:T(8,128)(2,1)S(1)} %copy-done.2, bf16[1,2048]{1,0:T(2,128)(2,1)S(1)} %reshape.611.gain_ref, bf16[4,48,2048]{2,1,0:T(8,128)(2,1)S(1)} %copy-done.3, ...), custom_call_target="tpu_custom_call" | custom-call | tf_op jit(solution)/shard_map/pallas_call | solution.py:346
  63.2 3.2 %copy-done.1 = bf16[32,64,2048]{2,1,0:T(8,128)(2,1)} copy-done((bf16[32,64,2048]{2,1,0:T(8,128)(2,1)}, bf16[32,64,2048]{2,1,0:T(8,128)(2,1)S(1)}, u32[]{:S(2)}) %copy-start.1) | copy-done | bytes 8388632
  66.4 1.7 copy-done.4
  68.1 13.2 %fusion.28 = f32[2048,384]{0,1:T(8,128)} fusion(bf16[768,384]{1,0:T(8,128)(2,1)} %bitcast.202, bf16[2048,2048]{1,0:T(8,128)(2,1)} %bitcast.181, bf16[768,2048]{1,0:T(8,128)(2,1)} %bitcast.188, s32[768]{0:T(1024)S(1)} %eq.85, s32[2048]{0:T(1024)S(1)} %get-tuple-element.137), kind=kOutput, calls=%fused_computation.34 | convolution fusion | flops 7655915520 | bytes 15281152 | tf_op jit(solution)/shard_map/dot_general | solution.py:577
  81.5 6.5 %fusion.29 = bf16[2048,256]{0,1:T(8,128)(2,1)S(1)} fusion(bf16[2048,2048]{1,0:T(8,128)(2,1)} %bitcast.182, bf16[256,2048]{1,0:T(8,128)(2,1)S(1)} %bitcast.201, f32[2048,384]{0,1:T(8,128)} %fusion.28), kind=kOutput, calls=%fused_computation.37 | convolution fusion | flops 2148532224 | bytes 12582912 | tf_op jit(solution)/shard_map/dot_general | solution.py:582
  88.7 2.9 %multiply_reduce_fusion = (f32[2048]{0:T(1024)S(1)}, f32[2048,128]{0,1:T(8,128)S(1)}) fusion(f32[2048,384]{0,1:T(8,128)S(1)} %copy-done.8, bf16[2048,2048]{1,0:T(8,128)(2,1)S(1)} %bitcast.185, bf16[2048,128]{1,0:T(8,128)(2,1)S(1)} %copy-done.12), kind=kOutput, calls=%fused_computation.52 | convolution fusion | flops 1074526208 | bytes 11018240 | tf_op jit(solution)/shard_map/dot_general | solution.py:599
  92.3 2.4 fusion.53
  97.0 20.2 %while.14 = (s32[]{:T(128)}, bf16[4,512,128]{2,1,0:T(8,128)(2,1)S(1)}, s32[4]{0:T(128)S(1)}, s32[2048]{0:T(1024)S(1)}, bf16[2048,1,128]{0,2,1:T(8,128)(2,1)}, /*...) while((s32[]{:T(128)}, ...), condition=%wide.region_11.12_spmd.clone, body=%wide.region_9.11_spmd.clone.sunk | while | flops 545325056 | bytes 9722047 | solution.py:503
  98.8 2.7 fusion.110
  103.7 2.7 fusion.110
  108.7 2.7 fusion.110
  113.6 2.7 fusion.110
  118.9 6.8 %scatter_custom_fusion = bf16[8192,32]{1,0:T(8,128)(2,1)S(1)} fusion(s32[2048]{0:T(1024)S(1)} %bitcast.209, bf16[2048,32]{1,0:T(8,128)(2,1)} %copy.66, bf16[]{:T(256)} %constant.176.clone.1), kind=kCustom, calls=%fused_computation.49 | custom fusion | bytes 524800 | tf_op jit(solution)/shard_map/scatter | solution.py:596
  127.3 1.7 convolution_select_fusion
  128.9 9.2 %fusion.75 = f32[2048,2048]{1,0:T(8,128)} fusion(bf16[2048,128]{1,0:T(8,128)(2,1)} %bitcast.196, bf16[128,2048]{1,0:T(8,128)(2,1)} %param.38), kind=kOutput, calls=%fused_computation.136 | convolution fusion | flops 1073741824 | bytes 17825792 | tf_op jit(solution)/shard_map/dot_general | solution.py:613
  138.2 13.0 %add_convert_fusion = bf16[2048,2048]{1,0:T(8,128)(2,1)} fusion(f32[2048,2048]{1,0:T(8,128)} %fusion.75, f32[2048,256]{1,0:T(8,128)S(1)} %convolution_select_fusion, bf16[256,2048]{1,0:T(8,128)(2,1)S(1)} %bitcast.180), kind=kOutput, calls=%fused_computation.16 | convolution fusion | flops 12897484800 | bytes 28311552 | tf_op jit(solution)/shard_map/dot_general | solution.py:617
  151.2 59.5 %shard_map.239 = (bf16[64,2048]{1,0:T(8,128)(2,1)S(1)}, bf16[32,64,2048]{2,1,0:T(8,128)(2,1)S(1)}) custom-call(bf16[32,64,2048]{2,1,0:T(8,128)(2,1)} %bitcast.189, bf16[64,2048]{1,0:T(8,128)(2,1)S(1)} %copy-done.2, bf16[1,2048]{1,0:T(2,128)(2,1)S(1)} %reshape.626.gain_ref), custom_call_target="tpu_custom_call" | custom-call | tf_op jit(solution)/shard_map/pallas_call | solution.py:396
  210.7 4.5 %fusion.76 = f32[32,2048,32]{1,2,0} fusion(bf16[32,64,2048]{2,1,0:T(8,128)(2,1)S(1)} %get-tuple-element.91, pred[32,64,32]{1,2,0:T(8,128)(4,1)S(1)} %bitcast.203), kind=kOutput, calls=%fused_computation.137 | convolution fusion | flops 268435456 | bytes 16842752
  215.1 4.2 %convert_bitcast_fusion.1 = bf16[2,32,16,2048]{3,2,0,1:T(8,128)(2,1)S(1)} fusion(f32[32,2048,2,16]{1,3,2,0:T(8,128)} %bitcast.190), kind=kLoop, calls=%fused_computation.22 | loop fusion | flops 2097152 | bytes 12582912 | tf_op jit(solution)/shard_map/convert_element_type | solution.py:644
  219.9 2.0 copy-done.5
  221.9 5.2 %fusion.77 = f32[2,512,768]{2,1,0:T(8,128)} fusion(bf16[2,512,2048]{2,1,0:T(8,128)(2,1)S(1)} %bitcast.193, bf16[2,768,2048]{2,1,0:T(8,128)(2,1)S(1)} %bitcast.215), kind=kOutput, calls=%fused_computation.138 | convolution fusion | flops 3221225472 | bytes 13631488 | tf_op jit(solution)/shard_map/secx,efx->secf/dot_general | solution.py:510
  227.1 13.5 %convert_bitcast_fusion = bf16[1,2,512,2048]{3,2,1,0:T(8,128)(2,1)} fusion(bf16[2,768,2048]{2,1,0:T(8,128)(2,1)} %param.41, f32[2,512,768]{2,1,0:T(8,128)} %fusion.77, bf16[2,512,2048]{2,1,0:T(8,128)(2,1)} %bitcast.194, bf16[2,768,2048]{2,1,0:T(8,128)(2,1)} %param.39), kind=kOutput, calls=%fused_computation.21 | convolution fusion | flops 6449266688 | bytes 24117248 | tf_op jit(solution)/shard_map/secf,efx->secx/dot_general | solution.py:512
  240.6 4.6 %bitcast_convert_fusion.terms_ref = bf16[32,64,2048]{2,1,0:T(8,128)(2,1)S(1)} fusion(f32[2,32,16]{2,0,1:T(2,128)S(1)} %bitcast.204, f32[32,64,2]{1,2,0:T(2,128)S(1)} %copy-done.11, f32[16]{0:T(128)S(1)} %copy-done.17, pred[32,64,2]{1,2,0:T(4,128)(4,1)S(1)} %copy-done.14, bf16[2,32,16,2048]{3,2,1,0:T(8,128)(2,1)} %bitcast.192), kind=kOutput, calls=%fused_computation.15 | convolution fusion | flops 279052288 | bytes 12607552 | tf_op jit(solution)/shard_map/stek,eskd->std/dot_general | solution.py:649
  245.3 34.5 %shard_map.240 = bf16[64,2048]{1,0:T(8,128)(2,1)S(1)} custom-call(bf16[32,64,2048]{2,1,0:T(8,128)(2,1)S(1)} %bitcast_convert_fusion.terms_ref), custom_call_target="tpu_custom_call" | custom-call | tf_op jit(solution)/shard_map/pallas_call | solution.py:428
  (118 shorter events, 35.4 us)
Async XLA Ops:
  0.6 1.2 copy-start
  0.6 20.6 %copy-start.2 = (bf16[64,2048]{1,0:T(8,128)(2,1)S(1)}, bf16[64,2048]{1,0:T(8,128)(2,1)}, u32[]{:S(2)}) copy-start(bf16[64,2048]{1,0:T(8,128)(2,1)} %tokens_ref.3) | copy-start | bytes 786436
  0.7 20.6 %copy-start.3 = (bf16[4,48,2048]{2,1,0:T(8,128)(2,1)S(1)}, bf16[4,48,2048]{2,1,0:T(8,128)(2,1)}, u32[]{:S(2)}) copy-start(bf16[4,48,2048]{2,1,0:T(8,128)(2,1)} %shrink_ref.1) | copy-start | bytes 2359300
  1.9 79.5 %copy-start.16 = (f32[16]{0:T(128)}, f32[16]{0:T(128)S(1)}, u32[]{:S(2)}) copy-start(f32[16]{0:T(128)S(1)} %iota_add_fusion.1) | copy-start | bytes 196
  7.4 7.7 %copy-start.13 = (pred[32,64,2]{1,2,0:T(4,128)(4,1)}, pred[32,64,2]{1,2,0:T(4,128)(4,1)S(1)}, u32[]{:S(2)}) copy-start(pred[32,64,2]{1,2,0:T(4,128)(4,1)S(1)} %copy.61) | copy-start | bytes 12292
  10.2 5.0 %copy-start.10 = (f32[32,64,2]{1,2,0:T(2,128)}, f32[32,64,2]{1,2,0:T(2,128)S(1)}, u32[]{:S(2)}) copy-start(f32[32,64,2]{1,2,0:T(2,128)S(1)} %copy.62) | copy-start | bytes 49156
  20.4 0.8 copy-start.9
  63.1 3.2 %copy-start.1 = (bf16[32,64,2048]{2,1,0:T(8,128)(2,1)}, bf16[32,64,2048]{2,1,0:T(8,128)(2,1)S(1)}, u32[]{:S(2)}) copy-start(bf16[32,64,2048]{2,1,0:T(8,128)(2,1)S(1)} %get-tuple-element.86) | copy-start | bytes 25165828
  66.4 1.7 copy-start.4
  81.3 6.6 %slice-start = ((s8[8388608]{0:T(1024)(128)(4,1)}), s8[4194304]{0:T(1024)(128)(4,1)S(1)}, s32[]{:S(2)}) async-start(s8[8388608]{0:T(1024)(128)(4,1)} %bitcast.183), calls=%async_computation | async-start | bytes 8388608
  81.4 6.5 %slice-start.1 = ((s8[8388608]{0:T(1024)(128)(4,1)}), s8[4194304]{0:T(1024)(128)(4,1)S(1)}, s32[]{:S(2)}) async-start(s8[8388608]{0:T(1024)(128)(4,1)} %bitcast.183), calls=%async_computation.1 | async-start | bytes 8388608
  81.5 7.3 %copy-start.8 = (f32[2048,384]{0,1:T(8,128)S(1)}, f32[2048,384]{0,1:T(8,128)}, u32[]{:S(2)}) copy-start(f32[2048,384]{0,1:T(8,128)} %fusion.28) | copy-start | bytes 9437188
  81.5 7.3 %copy-start.12 = (bf16[2048,128]{1,0:T(8,128)(2,1)S(1)}, bf16[2048,128]{1,0:T(8,128)(2,1)}, u32[]{:S(2)}) copy-start(bf16[2048,128]{1,0:T(8,128)(2,1)} %param.36) | copy-start | bytes 1572868
  92.3 4.7 %copy-start.6 = (bf16[4,512,128]{2,1,0:T(8,128)(2,1)S(1)}, bf16[4,512,128]{2,1,0:T(8,128)(2,1)}, u32[]{:S(2)}) copy-start(bf16[4,512,128]{2,1,0:T(8,128)(2,1)} %custom-call) | copy-start | bytes 1572868
  117.1 0.8 copy-start.7
  210.6 11.2 %slice-start.2 = ((s8[6291456]{0:T(1024)(128)(4,1)}), s8[2097152]{0:T(1024)(128)(4,1)S(1)}, s32[]{:S(2)}) async-start(s8[6291456]{0:T(1024)(128)(4,1)} %bitcast.214), calls=%async_computation.2 | async-start | bytes 4194304
  215.1 6.8 %slice-start.3 = ((s8[6291456]{0:T(1024)(128)(4,1)}), s8[4194304]{0:T(1024)(128)(4,1)S(1)}, s32[]{:S(2)}) async-start(s8[6291456]{0:T(1024)(128)(4,1)} %bitcast.214), calls=%async_computation.3 | async-start | bytes 8388608
  219.9 2.0 copy-start.5
  227.1 13.5 %copy-start.11 = (f32[32,64,2]{1,2,0:T(2,128)S(1)}, f32[32,64,2]{1,2,0:T(2,128)}, u32[]{:S(2)}) copy-start(f32[32,64,2]{1,2,0:T(2,128)} %copy-done.10) | copy-start | bytes 49156
  227.1 13.5 %copy-start.14 = (pred[32,64,2]{1,2,0:T(4,128)(4,1)S(1)}, pred[32,64,2]{1,2,0:T(4,128)(4,1)}, u32[]{:S(2)}) copy-start(pred[32,64,2]{1,2,0:T(4,128)(4,1)} %copy-done.13) | copy-start | bytes 12292
  227.1 13.5 %copy-start.15 = (f32[32,2,16]{2,1,0:T(2,128)S(1)}, f32[32,2,16]{2,1,0:T(2,128)}, u32[]{:S(2)}) copy-start(f32[32,2,16]{2,1,0:T(2,128)} %select_reduce_fusion.1) | copy-start | bytes 12292
  227.1 13.5 %copy-start.17 = (f32[16]{0:T(128)S(1)}, f32[16]{0:T(128)}, u32[]{:S(2)}) copy-start(f32[16]{0:T(128)} %copy-done.16) | copy-start | bytes 196

commit v3 on v2

--- a/solution.py
+++ b/solution.py
@@ -258,7 +258,7 @@
     copies = Copies(send, recv)
     homes = [
         pltpu.make_async_copy(shrink_ref, factors_ref.at[pl.ds(4 * group, 4)], local.at[0]),
-        pltpu.make_async_copy(wkv_ref.at[z], wkv_all_ref.at[y, core, z], local.at[1]),
+        pltpu.make_async_copy(wkv_ref.at[z], wkv_all_ref.at[z, y, core], local.at[1]),
     ]
     for home in homes:
         home.start()
@@ -285,7 +285,7 @@
             there = lax.rem(z + step, SIDE)
             spread.append(
                 copies.go(
-                    wkv_ref.at[there], wkv_all_ref.at[y, core, z], "tensor", spot(there, y, core)
+                    wkv_ref.at[there], wkv_all_ref.at[z, y, core], "tensor", spot(there, y, core)
                 )
             )
         state["spread"] = spread
@@ -294,7 +294,7 @@
         state["factors"] = [copies.go(mine, half, "dp", up), copies.go(mine, half, "dp", down)]
 
     def kv(y_at, first=0, count=4):
-        return wkv_all_ref.at[lax.rem(y_at, SIDE), core, pl.ds(first, count)]
+        return wkv_all_ref.at[pl.ds(first, count), lax.rem(y_at, SIDE), core]
 
     def middle_extras():
         for copy in state["spread"]:
@@ -348,7 +348,7 @@
         out_shape=(
             jax.ShapeDtypeStruct((32, rows, width), jnp.bfloat16),
             jax.ShapeDtypeStruct((4 * shrink.shape[0],) + shrink.shape[1:], jnp.bfloat16),
-            jax.ShapeDtypeStruct((4, 2) + wkv.shape, jnp.bfloat16),
+            jax.ShapeDtypeStruct((4, 4, 2) + wkv.shape[1:], jnp.bfloat16),
         ),
         in_specs=[
             pl.BlockSpec(memory_space=pltpu.VMEM),
@@ -442,67 +442,265 @@
     )(terms)
 
 
-def rotate(values, position):
-    half = values.shape[-1] // 2
+BLOCK = 512
+KEY_BLOCK = 256
+TRANSPOSED = (((1,), (1,)), ((), ()))
+
+
+def heart_kernel(
+    lens_s,
+    groups_s,
+    pages_s,
+    lens_ref,
+    groups_ref,
+    adapters_ref,
+    slots_ref,
+    q_gain_ref,
+    k_gain_ref,
+    x_ref,
+    factors_ref,
+    wkv_ref,
+    wq_ref,
+    q_up_ref,
+    kv_up_ref,
+    wo_ref,
+    shrink_o_ref,
+    expand_ref,
+    out_ref,
+    pages_ref,
+    tab,
+    keys,
+    values,
+    across,
+    acc,
+):
+    step = pl.program_id(0)
+    place = lax.axis_index("tensor")
+    head = lax.div(place, 8)
+    f32, bf16 = jnp.float32, jnp.bfloat16
+    requests = lens_ref.shape[1]
+    adapters = slots_ref.shape[1]
+    depth = wq_ref.shape[1]
+
+    @pl.when(step == 0)
+    def _():
+        down = lax.broadcasted_iota(jnp.int32, (requests, requests), 0)
+        over = lax.broadcasted_iota(jnp.int32, (requests, requests), 1)
+
+        def column(row, number):
+            a = lax.broadcasted_iota(jnp.int32, (number, number), 0)
+            b = lax.broadcasted_iota(jnp.int32, (number, number), 1)
+            return jnp.sum(
+                jnp.where(a == b, jnp.broadcast_to(row, (number, number)), 0.0),
+                axis=1,
+                keepdims=True,
+            )
+
+        lens = lens_ref[...].astype(f32)
+        groups = groups_ref[...].astype(f32)
+        chosen = adapters_ref[...]
+        slots = column(slots_ref[...].astype(f32), adapters)
+        ends = jnp.sum(jnp.where(down <= over, column(lens, requests), 0.0), axis=0, keepdims=True)
+        starts = ends - lens
+        same = column(groups, requests) == groups
+        firsts = jnp.min(
+            jnp.where(same, column(starts, requests), 1e9), axis=0, keepdims=True
+        )
+        which = lax.broadcasted_iota(jnp.int32, (adapters, requests), 0)
+        slot = jnp.sum(jnp.where(which == chosen, slots, 0.0), axis=0, keepdims=True)
+        tab[0:1, :] = starts
+        tab[1:2, :] = ends
+        tab[2:3, :] = firsts
+        tab[3:4, :] = slot
+
+    first_row = step * BLOCK
+    row = first_row + lax.broadcasted_iota(jnp.int32, (BLOCK, 1), 0)
+    row_f = row.astype(f32)
+    inside = (row_f >= tab[0:1, :]) & (row_f < tab[1:2, :])
+    rope = row_f - jnp.sum(jnp.where(inside, tab[2:3, :], 0.0), axis=1, keepdims=True)
+    slot = jnp.sum(jnp.where(inside, tab[3:4, :], 0.0), axis=1, keepdims=True).astype(jnp.int32)
+
+    lane = lax.broadcasted_iota(jnp.int32, (1, depth), 1)
+    half = depth // 2
+    low = lane < half
     freq = jnp.exp(
-        -jnp.arange(half, dtype=jnp.float32) * (2.0 * math.log(ROPE_BASE) / values.shape[-1])
-    )
-    angle = position.astype(jnp.float32)[:, None, None] * freq[None, None, :]
-    cosine = jnp.cos(angle)
-    sine = jnp.sin(angle)
-    first = values[..., :half]
-    second = values[..., half:]
-    return jnp.concatenate(
-        [first * cosine - second * sine, second * cosine + first * sine], axis=-1
-    )
-
-
-def lookup(index_value, table):
-    match = index_value[:, None] == jnp.arange(table.shape[0], dtype=jnp.int32)[None, :]
-    return jnp.sum(jnp.where(match, table[None, :], 0), axis=1)
-
-
-def token_layout(length_row, group_row, adapter_row, adapter_slot, page_row, grand_total):
-    position = jnp.arange(grand_total, dtype=jnp.int32)
-    ends = jnp.cumsum(length_row)
-    starts = ends - length_row
-    request = jnp.sum((ends[None, :] <= position[:, None]).astype(jnp.int32), axis=1)
-    group = lookup(request, group_row)
-    same = group_row[:, None] == group_row[None, :]
-    group_first = jnp.min(jnp.where(same, starts[None, :], grand_total), axis=1)
-    rope_pos = position - lookup(request, group_first)
-    offset = position - lookup(request, starts)
-    per_request = page_row.shape[0] // length_row.shape[0]
-    page = lookup(request * per_request + offset // PAGE, page_row)
-    cell = page * PAGE + offset % PAGE
-    adapter_position = lookup(request, lookup(adapter_row, adapter_slot))
-    return (group, rope_pos, cell, adapter_position)
-
-
-def attend(query_rows_out, keys, values, group, scale):
-    grand_total = query_rows_out.shape[0]
-    block = min(512, grand_total)
-    position = jnp.arange(grand_total, dtype=jnp.int32)
-
-    def one_block(number):
-        first = number * block
-        query_block = lax.dynamic_slice_in_dim(query_rows_out, first, block, 0)
-        rows_here = first + jnp.arange(block, dtype=jnp.int32)
-        group_here = lax.dynamic_slice_in_dim(group, first, block, 0)
-        allowed = (position[None, :] <= rows_here[:, None]) & (
-            group[None, :] == group_here[:, None]
+        -jnp.where(low, lane, lane - half).astype(f32) * (2.0 * math.log(ROPE_BASE) / depth)
+    )
+    mixed_trig = jnp.sin(rope * freq + jnp.where(low, 0.5 * math.pi, 0.0))
+    other_trig = pltpu.roll(mixed_trig, half, 1)
+    cosine = jnp.where(low, mixed_trig, other_trig)
+    sine = jnp.where(low, -other_trig, mixed_trig)
+
+    def turn(vector):
+        return vector * cosine + pltpu.roll(vector, half, 1) * sine
+
+    def unit(vector, gain_ref):
+        return (
+            vector
+            * lax.rsqrt(jnp.mean(vector * vector, axis=-1, keepdims=True) + NORM_EPS)
+            * gain_ref[...].astype(f32)
         )
-        scores = (
-            jnp.einsum("qhd,kd->hqk", query_block, keys, preferred_element_type=jnp.float32) * scale
+
+    rank = factors_ref.shape[1] // 3
+    mine = slot == lax.div(lax.broadcasted_iota(jnp.int32, (1, adapters * rank), 1), rank)
+    x = x_ref[...]
+    lora = []
+    for part in range(3):
+        table = factors_ref[:, part * rank : (part + 1) * rank, :].reshape(adapters * rank, -1)
+        shrunk = lax.dot_general(x, table, TRANSPOSED, preferred_element_type=f32)
+        placed = jnp.where(mine, shrunk, 0.0).astype(bf16)
+        if part == 0:
+            up = q_up_ref[...]
+        else:
+            begin = pl.multiple_of(head * 2 * depth + (part - 1) * depth, depth)
+            up = kv_up_ref[:, pl.ds(begin, depth)]
+        lora.append(ADAPTER_FACTOR * jnp.dot(placed, up, preferred_element_type=f32))
+    query = jnp.dot(x, wq_ref[...], preferred_element_type=f32) + lora[0]
+    query = turn(unit(query, q_gain_ref)).astype(bf16)
+    kv = lax.dot_general(x, wkv_ref[...], TRANSPOSED, preferred_element_type=f32)
+    raw = (kv[:, :depth] + lora[1]).astype(bf16).astype(f32)
+    key = turn(unit(raw, k_gain_ref)).astype(bf16)
+    value = (kv[:, depth:] + lora[2]).astype(bf16)
+    keys[pl.ds(first_row, BLOCK), :] = key
+    values[pl.ds(first_row, BLOCK), 0:depth] = value
+    values[pl.ds(first_row, BLOCK), depth:] = jnp.broadcast_to(
+        jnp.where(lane == 0, 1.0, 0.0), (BLOCK, depth)
+    ).astype(bf16)
+
+    columns = pages_ref.shape[1]
+    offset = lax.rem(place, 8) * columns
+    pick_row = lax.broadcasted_iota(jnp.int32, (columns, 2 * depth), 0) + offset
+    pick_lane = lax.broadcasted_iota(jnp.int32, (columns, 2 * depth), 1)
+    pick = jnp.where(pick_row == pick_lane, 1.0, 0.0).astype(bf16)
+    across[:, pl.ds(pl.multiple_of(first_row, BLOCK), BLOCK)] = lax.dot_general(
+        pick, jnp.concatenate([key, value], axis=1), TRANSPOSED, preferred_element_type=f32
+    )
+
+    def look(number, carry):
+        start, lead, found, before = carry
+        group = groups_s[0, number]
+        lead = jnp.where(group == before, lead, start)
+        found = jnp.where(start <= first_row, lead, found)
+        return start + lens_s[0, number], lead, found, group
+
+    zero = jnp.int32(0)
+    found = lax.fori_loop(0, requests, look, (zero, zero, zero, jnp.int32(-1)))[2]
+    acc[...] = jnp.zeros_like(acc)
+    gap = lax.broadcasted_iota(jnp.int32, (BLOCK, KEY_BLOCK), 0) - lax.broadcasted_iota(
+        jnp.int32, (BLOCK, KEY_BLOCK), 1
+    )
+    reach = rope.astype(jnp.int32)
+    scale = depth**-0.5
+
+    def over_keys(number, carry):
+        begin = pl.multiple_of(number * KEY_BLOCK, KEY_BLOCK)
+        scores = lax.dot_general(
+            query, keys[pl.ds(begin, KEY_BLOCK), :], TRANSPOSED, preferred_element_type=f32
         )
-        raised = jnp.where(allowed[None], jnp.exp(scores), 0.0)
-        shares = (raised / jnp.sum(raised, axis=-1, keepdims=True)).astype(jnp.bfloat16)
-        mixed = jnp.einsum("hqk,kd->qhd", shares, values, preferred_element_type=jnp.float32)
-        return mixed.astype(jnp.bfloat16).reshape(block, -1)
-
-    return lax.map(one_block, jnp.arange(grand_total // block, dtype=jnp.int32)).reshape(
-        grand_total, -1
-    )
+        behind = gap + (first_row - begin)
+        raised = jnp.where((behind >= 0) & (behind <= reach), jnp.exp(scores * scale), 0.0)
+        acc[...] += jnp.dot(
+            raised.astype(bf16), values[pl.ds(begin, KEY_BLOCK), :], preferred_element_type=f32
+        )
+        return carry
+
+    lax.fori_loop(
+        lax.div(found, KEY_BLOCK), (step + 1) * (BLOCK // KEY_BLOCK), over_keys, jnp.int32(0)
+    )
+    mixed = (acc[:, :depth] / acc[:, depth : depth + 1]).astype(bf16)
+    shrunk = lax.dot_general(mixed, shrink_o_ref[...], TRANSPOSED, preferred_element_type=f32)
+    placed = jnp.where(mine, ADAPTER_FACTOR * shrunk, 0.0).astype(bf16)
+    width = out_ref.shape[-1]
+    for begin in range(0, width, 512):
+        term = jnp.dot(mixed, wo_ref[:, begin : begin + 512], preferred_element_type=f32)
+        term = term + jnp.dot(
+            placed, expand_ref[:, begin : begin + 512], preferred_element_type=f32
+        )
+        out_ref[:, begin : begin + 512] = term.astype(bf16)
+
+    @pl.when(step == pl.num_programs(0) - 1)
+    def _():
+        spot_lane = lax.broadcasted_iota(jnp.int32, (columns, PAGE), 1)
+
+        def fill(number, start):
+            length = lens_s[0, number]
+            for part in range(2):
+                begin = start + part * PAGE
+                aligned = pl.multiple_of(lax.div(begin, PAGE) * PAGE, PAGE)
+                window = across[:, pl.ds(aligned, 2 * PAGE)]
+                shift = lax.rem(2 * PAGE - (begin - aligned), 2 * PAGE)
+                rolled = pltpu.roll(window, shift, 1)[:, :PAGE]
+                kept = jnp.where(spot_lane < length - part * PAGE, rolled, 0.0)
+                pages_ref[pages_s[0, number * 2 + part]] = kept.astype(bf16)
+            return start + length
+
+        lax.fori_loop(0, requests, fill, zero)
+
+
+def heart(
+    lengths,
+    groups,
+    adapter_of_request,
+    adapter_slot,
+    page_table,
+    q_gain,
+    k_gain,
+    x,
+    factors,
+    wkv,
+    query_weight,
+    query_up,
+    kv_up,
+    w_o,
+    shrink_o,
+    expand_o,
+):
+    total, width = x.shape
+    depth = query_weight.shape[1]
+    requests = lengths.shape[1]
+    pages = page_table.shape[1]
+    columns = 2 * kv_up.shape[1] // 64
+    slots = adapter_slot.shape[0]
+    smem = pl.BlockSpec(memory_space=pltpu.SMEM)
+
+    def whole(array):
+        return pl.BlockSpec(
+            array.shape, lambda i: (0,) * array.ndim, pipeline_mode=pl.Buffered(1)
+        )
+
+    small = (
+        lengths,
+        groups,
+        adapter_of_request,
+        adapter_slot.reshape(1, slots),
+        q_gain.reshape(1, depth),
+        k_gain.reshape(1, depth),
+    )
+    tables = (factors, wkv, query_weight, query_up, kv_up, w_o, shrink_o, expand_o)
+    return pl.pallas_call(
+        heart_kernel,
+        grid=(total // BLOCK,),
+        out_shape=(
+            jax.ShapeDtypeStruct((total, width), jnp.bfloat16),
+            jax.ShapeDtypeStruct((pages, columns, PAGE), jnp.bfloat16),
+        ),
+        in_specs=[smem, smem, smem]
+        + [whole(array) for array in small]
+        + [pl.BlockSpec((BLOCK, width), lambda i: (i, 0))]
+        + [whole(array) for array in tables],
+        out_specs=(
+            pl.BlockSpec((BLOCK, width), lambda i: (i, 0)),
+            pl.BlockSpec((pages, columns, PAGE), lambda i: (0, 0, 0)),
+        ),
+        scratch_shapes=[
+            pltpu.VMEM((8, requests), jnp.float32),
+            pltpu.VMEM((total, depth), jnp.bfloat16),
+            pltpu.VMEM((total, 2 * depth), jnp.bfloat16),
+            pltpu.VMEM((columns, total + 4 * PAGE), jnp.float32),
+            pltpu.VMEM((BLOCK, 2 * depth), jnp.float32),
+        ],
+        compiler_params=pltpu.CompilerParams(vmem_limit_bytes=48 << 20),
+    )(lengths, groups, page_table, *small, x, *tables)
 
 
 def expert_apply(rows, gate_rows, up_rows, down_rows):
@@ -542,84 +740,27 @@
     place = lax.axis_index("tensor")
     own_rows, width = tokens.shape
     grand_total = own_rows * parts
-    head_length = q_gain.shape[0]
     adapters, rank, kv_width = key_value_up_factors.shape
-    key_value_heads = kv_width // (2 * head_length)
-    group, rope_pos, cell, adapter_position = token_layout(
-        lengths[0], groups[0], adapter_of_request[0], adapter_slot, page_table[0], grand_total
-    )
     x_rows, factors, wkv_all = enter(tokens, attn_gain, shrink_qkv, w_kv.transpose(1, 0, 2))
-    normed = x_rows.reshape(grand_total, width)
-    head = place * key_value_heads // parts
-    local_cols = kv_width // parts
-    head_width = 2 * head_length
-    wkv_head = wkv_all.transpose(2, 0, 1, 3, 4).reshape(head_width, width)
-    ranks = 3 * rank
-    projected = lax.dot_general(
-        normed,
-        factors.reshape(adapters * ranks, width),
-        (((1,), (1,)), ((), ())),
-        preferred_element_type=jnp.float32,
-    )
-    slots = jnp.repeat(jnp.arange(adapters, dtype=jnp.int32), ranks)
-    placed = jnp.where(adapter_position[:, None] == slots[None, :], projected, 0.0).astype(
-        jnp.bfloat16
-    )
-    query_cols = query_weight.shape[1]
-    heads_here = query_cols // head_length
-    kv_up = lax.dynamic_slice_in_dim(key_value_up_factors, head * head_width, head_width, 2)
-    raise_table = jnp.zeros((adapters, 3, rank, query_cols + head_width), jnp.bfloat16)
-    raise_table = raise_table.at[:, 0, :, :query_cols].set(query_up_factors)
-    raise_table = raise_table.at[:, 1, :, query_cols : query_cols + head_length].set(
-        kv_up[:, :, :head_length]
-    )
-    raise_table = raise_table.at[:, 2, :, query_cols + head_length :].set(kv_up[:, :, head_length:])
-    lora = ADAPTER_FACTOR * jnp.dot(
-        placed,
-        raise_table.reshape(adapters * ranks, query_cols + head_width),
-        preferred_element_type=jnp.float32,
-    )
-    base_kv = lax.dot_general(
-        normed, wkv_head, (((1,), (1,)), ((), ())), preferred_element_type=jnp.float32
-    )
-    head_kv = (base_kv + lora[:, query_cols:]).astype(jnp.bfloat16)
-    divided_key_value = head_kv.reshape(grand_total, 2, head_length)
-    keys = rotate(normalize(divided_key_value[:, :1].astype(jnp.float32), k_gain), rope_pos).astype(
-        jnp.bfloat16
-    )[:, 0]
-    values = divided_key_value[:, 1]
-    entries = jnp.concatenate([keys, values], axis=1)
-    mine = lax.dynamic_slice_in_dim(
-        entries, place * local_cols - head * head_width, local_cols, 1
-    )
-    pages_held = page_table.shape[1]
-    kv_pages = jnp.zeros((pages_held * PAGE, local_cols), jnp.bfloat16).at[cell].set(mine)
-    kv_pages = kv_pages.reshape(pages_held, PAGE, local_cols).transpose(0, 2, 1)
-    query_rows_out = (
-        jnp.dot(normed, query_weight, preferred_element_type=jnp.float32) + lora[:, :query_cols]
-    )
-    query_rows_out = rotate(
-        normalize(query_rows_out.reshape(grand_total, heads_here, head_length), q_gain), rope_pos
-    ).astype(jnp.bfloat16)
-    mixed = attend(query_rows_out, keys, values, group, head_length ** (-0.5))
-    shrink_table = shrink_o.reshape(adapters * rank, query_cols)
-    upward_wide_rows = expand_o.reshape(adapters * rank, width).astype(jnp.float32)
-    lower_rank_rows = lax.dot_general(
-        mixed, shrink_table, (((1,), (1,)), ((), ())), preferred_element_type=jnp.float32
-    )
-    retained_mask = jnp.repeat(
-        adapter_position[:, None] == jnp.arange(adapters, dtype=jnp.int32)[None, :], rank, axis=1
-    )
-    adapter_contribution = jnp.dot(mixed, w_o, preferred_element_type=jnp.float32)
-    attn_terms = (
-        adapter_contribution
-        + ADAPTER_FACTOR
-        * jnp.dot(
-            jnp.where(retained_mask, lower_rank_rows, 0.0),
-            upward_wide_rows,
-            precision=lax.Precision.HIGHEST,
-        )
-    ).astype(jnp.bfloat16)
+    head_width = 2 * q_gain.shape[0]
+    attn_terms, kv_pages = heart(
+        lengths,
+        groups,
+        adapter_of_request,
+        adapter_slot,
+        page_table,
+        q_gain,
+        k_gain,
+        x_rows.reshape(grand_total, width),
+        factors,
+        wkv_all.reshape(head_width, width),
+        query_weight,
+        query_up_factors.reshape(adapters * rank, -1),
+        key_value_up_factors.reshape(adapters * rank, kv_width),
+        w_o,
+        shrink_o.reshape(adapters * rank, -1),
+        expand_o.reshape(adapters * rank, width),
+    )
     attn_out, moe_in = middle(attn_terms.reshape(parts, own_rows, width), tokens, moe_gain)
     experts_here = w_gate.shape[0]
     own_experts = place * experts_here + jnp.arange(experts_here, dtype=jnp.int32)

time: 285 us -> 237 us (0.83); the launches traced: 281 us -> 237 us
  matrix products: 88.7 us -> 27.9 us
  Pallas kernels: 136 us -> 180 us
  other arithmetic: 18.6 us -> 1.46 us
  local copies, waits for them, and re-layouts: 33.7 us -> 26.7 us
  loops' own time: 3.26 us -> 0 us
    dot_general x14 -> x0, matrix products: 60.7 us -> none  [the longest x1 13.2 us: local(): jnp.dot(placed, raise_table.reshape(adapters * ranks, query_cols + head_w...]
    pallas_call x0 -> x1, Pallas kernels: none -> 44.4 us  [heart(): pl.pallas_call(heart_kernel, grid=(total // BLOCK,), out_shape=(jax.Shape...]
    scatter x4 -> x0, local copies, waits for them, and re-layouts: 9.45 us -> none  [the longest x1 6.82 us: local(): jnp.zeros((pages_held * PAGE, local_cols), jnp.bfloat16).at[cell].set(mine)]
    unnamed x50 -> x49, local copies, waits for them, and re-layouts: 15.7 us -> 25.1 us
    dynamic_slice x9 -> x0, local copies, waits for them, and re-layouts: 3.67 us -> none  [the longest x4 2.35 us: attend(): lax.map(one_block, jnp.arange(grand_total // block, dtype=jnp.int32))]
    convert_element_type x1, other arithmetic: 4.18 us -> 0.65 us  [local(): rows = jnp.einsum('stek,std->eskd', pick, moe_in, preferred_element_type=...]
    concatenate x4 -> x0, other arithmetic: 3.37 us -> none  [the longest x3 3.29 us: rotate(): jnp.concatenate([first * cosine - second * sine, second * cosine + first...]
    another operation x1 -> x0, loops' own time: 3.26 us -> none  [attend(): lax.map(one_block, jnp.arange(grand_total // block, dtype=jnp.int32))]
where the time goes in v3:
time: 237 us
  Pallas kernels  180 us (76%)
  matrix products  27.9 us (12%)
  local copies, waits for them, and re-layouts  26.7 us (11%)
    pallas_call x1, Pallas kernels, middle(): pl.pallas_call(middle_kernel, out_shape=(jax.ShapeDtypeStruct((rows, widt...  59.7 us
    pallas_call x1, Pallas kernels, heart(): pl.pallas_call(heart_kernel, grid=(total // BLOCK,), out_shape=(jax.Shape...  44.4 us
    pallas_call x1, Pallas kernels, enter(): pl.pallas_call(enter_kernel, out_shape=(jax.ShapeDtypeStruct((32, rows, w...  41.6 us
    pallas_call x1, Pallas kernels, leave(): pl.pallas_call(leave_kernel, out_shape=jax.ShapeDtypeStruct((rows, width)...  34.2 us
    unnamed x49, local copies, waits for them, and re-layouts  25.1 us
    dot_general x1, matrix products, expert_apply(): jnp.einsum('secf,efx->secx', hidden, down_rows, preferred_element_type=jn...  13 us
    dot_general x1, matrix products, expert_apply(): jnp.einsum('secx,efx->secf', rows, up_rows, preferred_element_type=jnp.fl...  5.58 us

profile of v3, /device:TPU:1, one launch (start us, length us, event | category | flops | bytes accessed | tf_op | source)
XLA Modules:
  0.0 236.8 jit_solution(4117497340248174626)
XLA Ops:
  0.6 0.7 reshape.82.gain_ref
  1.3 1.0 copy.52
  2.3 0.9 copy-done.4
  3.3 1.1 copy-done.6
  4.4 41.6 %shard_map.238 = (bf16[32,64,2048]{2,1,0:T(8,128)(2,1)S(1)}, bf16[16,48,2048]{2,1,0:T(8,128)(2,1)S(1)}, bf16[4,4,2,8,2048]{4,3,2,1,0:T(8,128)(2,1)S(1)}) custom-call(bf16[64,2048]{1,0:T(8,128)(2,1)S(1)} %copy-done.4, bf16[1,2048]{1,0:T(2,128)(2,1)S(1)} %reshape.82.gain_ref, bf16[4,48,2048]{2,1,0:T(8,128)(2,1)S(1)} %copy-done.6, bf16[4,8,2048]{2,1,0:T(8,128)(2,1)S(1)} %bitcast.87), custom_call_target="tpu_custom_call" | custom-call | tf_op jit(solution)/shard_map/pallas_call | solution.py:346
  46.0 3.2 %copy-done = bf16[32,64,2048]{2,1,0:T(8,128)(2,1)} copy-done((bf16[32,64,2048]{2,1,0:T(8,128)(2,1)}, bf16[32,64,2048]{2,1,0:T(8,128)(2,1)S(1)}, u32[]{:S(2)}) %copy-start) | copy-done | bytes 8388632
  49.2 1.6 copy-done.2
  50.8 1.2 copy-done.3
  52.1 1.0 copy-done.7
  53.1 1.0 copy-done.8
  54.2 1.0 copy-done.9
  55.2 0.8 copy-done.10
  56.0 0.8 copy-done.11
  61.5 44.4 %shard_map.239 = (bf16[2048,2048]{1,0:T(8,128)(2,1)}, bf16[64,32,128]{2,1,0:T(8,128)(2,1)}) custom-call(s32[1,32]{1,0:T(1,128)S(1)} %copy-done.12, s32[1,32]{1,0:T(1,128)S(1)} %copy-done.13, s32[1,64]{1,0:T(1,128)S(1)} %copy-done.14, s32[1,32]{1,0:T(1,128)S(1)} %copy-done.12, s32[1,32]{1,0:T(1,128)S(1)} %copy-done.13, s32[1,32]{1,0:T(1,128)S(1)} %copy-done.15, ...), custom_call_target="tpu_custom_call" | custom-call | tf_op jit(solution)/shard_map/pallas_call | solution.py:680
  105.9 59.7 %shard_map.240 = (bf16[64,2048]{1,0:T(8,128)(2,1)S(1)}, bf16[32,64,2048]{2,1,0:T(8,128)(2,1)S(1)}) custom-call(bf16[32,64,2048]{2,1,0:T(8,128)(2,1)} %bitcast.94, bf16[64,2048]{1,0:T(8,128)(2,1)S(1)} %copy-done.5, bf16[1,2048]{1,0:T(2,128)(2,1)S(1)} %reshape.90.gain_ref), custom_call_target="tpu_custom_call" | custom-call | tf_op jit(solution)/shard_map/pallas_call | solution.py:396
  165.7 3.2 %copy-done.1 = bf16[32,64,2048]{2,1,0:T(8,128)(2,1)} copy-done((bf16[32,64,2048]{2,1,0:T(8,128)(2,1)}, bf16[32,64,2048]{2,1,0:T(8,128)(2,1)S(1)}, u32[]{:S(2)}) %copy-start.1) | copy-done | bytes 8388632
  170.2 4.6 %fusion.18 = f32[32,2048,32]{1,2,0:S(1)} fusion(bf16[32,64,2048]{2,1,0:T(8,128)(2,1)} %copy-done.1, pred[32,64,32]{1,2,0:T(8,128)(4,1)S(1)} %bitcast.98), kind=kOutput, calls=%fused_computation.33 | convolution fusion | flops 268435456 | bytes 16842752
  176.0 1.9 copy-done.19
  178.0 5.6 %fusion.19 = f32[2,512,768]{2,1,0:T(8,128)S(1)} fusion(bf16[2,512,2048]{2,1,0:T(8,128)(2,1)S(1)} %bitcast.96, bf16[2,768,2048]{2,1,0:T(8,128)(2,1)} %param.32), kind=kOutput, calls=%fused_computation.34 | convolution fusion | flops 3221225472 | bytes 13631488 | tf_op jit(solution)/shard_map/secx,efx->secf/dot_general | solution.py:708
  183.6 13.0 %convert_bitcast_fusion = bf16[1,2,512,2048]{3,2,1,0:T(8,128)(2,1)} fusion(bf16[2,768,2048]{2,1,0:T(8,128)(2,1)} %param.33, f32[2,512,768]{2,1,0:T(8,128)S(1)} %fusion.19, bf16[2,512,2048]{2,1,0:T(8,128)(2,1)} %bitcast.97, bf16[2,768,2048]{2,1,0:T(8,128)(2,1)} %param.31), kind=kOutput, calls=%fused_computation.4 | convolution fusion | flops 6449266688 | bytes 24117248 | tf_op jit(solution)/shard_map/secf,efx->secx/dot_general | solution.py:710
  196.5 4.6 %bitcast_convert_fusion.terms_ref = bf16[32,64,2048]{2,1,0:T(8,128)(2,1)S(1)} fusion(f32[2,32,16]{2,0,1:T(2,128)S(1)} %bitcast.99, f32[32,64,2]{1,2,0:T(2,128)S(1)} %copy.42, f32[16]{0:T(128)S(1)} %iota_add_fusion, pred[32,64,2]{1,2,0:T(4,128)(4,1)S(1)} %copy.41, bf16[2,32,16,2048]{3,2,1,0:T(8,128)(2,1)} %bitcast.95), kind=kOutput, calls=%fused_computation | convolution fusion | flops 279052288 | bytes 12607552 | tf_op jit(solution)/shard_map/stek,eskd->std/dot_general | solution.py:790
  201.2 34.2 %shard_map.241 = bf16[64,2048]{1,0:T(8,128)(2,1)S(1)} custom-call(bf16[32,64,2048]{2,1,0:T(8,128)(2,1)S(1)} %bitcast_convert_fusion.terms_ref), custom_call_target="tpu_custom_call" | custom-call | tf_op jit(solution)/shard_map/pallas_call | solution.py:428
  235.4 0.7 copy.56
  236.1 0.7 copy.57
  (51 shorter events, 7.1 us)
Async XLA Ops:
  2.3 1.0 copy-start.4
  3.3 1.1 copy-start.6
  46.0 3.2 %copy-start = (bf16[32,64,2048]{2,1,0:T(8,128)(2,1)}, bf16[32,64,2048]{2,1,0:T(8,128)(2,1)S(1)}, u32[]{:S(2)}) copy-start(bf16[32,64,2048]{2,1,0:T(8,128)(2,1)S(1)} %get-tuple-element.10) | copy-start | bytes 25165828
  49.2 1.6 copy-start.2
  50.8 1.2 copy-start.3
  52.1 1.0 copy-start.7
  53.1 1.0 copy-start.8
  54.2 1.0 copy-start.9
  55.2 0.8 copy-start.10
  56.0 0.8 copy-start.11
  56.9 0.7 copy-start.12
  57.5 0.7 copy-start.13
  58.2 0.7 copy-start.14
  58.8 0.7 copy-start.15
  59.5 0.7 copy-start.16
  60.2 0.7 copy-start.17
  60.8 0.7 copy-start.18
  61.5 44.4 %copy-start.22 = (bf16[2048]{0:T(1024)(128)(2,1)S(1)}, bf16[2048]{0:T(1024)(128)(2,1)}, u32[]{:S(2)}) copy-start(bf16[2048]{0:T(1024)(128)(2,1)} %param.25) | copy-start | bytes 12292
  61.5 44.4 %copy-start.5 = (bf16[64,2048]{1,0:T(8,128)(2,1)S(1)}, bf16[64,2048]{1,0:T(8,128)(2,1)}, u32[]{:S(2)}) copy-start(bf16[64,2048]{1,0:T(8,128)(2,1)} %tokens_ref.3) | copy-start | bytes 786436
  105.9 63.0 %copy-start.20 = (f32[2048,8]{0,1:T(8,128)S(1)}, f32[2048,8]{0,1:T(8,128)}, u32[]{:S(2)}) copy-start(f32[2048,8]{0,1:T(8,128)} %param.45) | copy-start | bytes 196612
  105.9 63.0 %copy-start.21 = (s32[2048,8]{0,1:T(8,128)S(1)}, s32[2048,8]{0,1:T(8,128)}, u32[]{:S(2)}) copy-start(s32[2048,8]{0,1:T(8,128)} %param.44) | copy-start | bytes 196612
  165.7 3.2 %copy-start.1 = (bf16[32,64,2048]{2,1,0:T(8,128)(2,1)}, bf16[32,64,2048]{2,1,0:T(8,128)(2,1)S(1)}, u32[]{:S(2)}) copy-start(bf16[32,64,2048]{2,1,0:T(8,128)(2,1)S(1)} %get-tuple-element.15) | copy-start | bytes 25165828
  176.0 2.0 copy-start.19

commit v4 on v3

--- a/solution.py
+++ b/solution.py
@@ -36,9 +36,10 @@
         copy = self.make(src, dst, axis, target)
         copy.start()
         return copy
-    def finish(self):
+    def settle(self):
         for copy in self.all:
             copy.wait_send()
+        self.all = []
 
 def gather_rows(out, z, y, core, copies, hooks=()):
     hooks = list(hooks)
@@ -125,32 +126,22 @@
         dst[pl.ds(start + first, 16)] = total.astype(dst.dtype)
 
 ORDER = (2, 1, 3, 0)
-SCATTER_COPIES = 32 + 32 + 8
-
-def scatter_rows(terms, acc, sib, landed, local, z, y, core, copies, result):
-    side = spot(z, y, 1 - core)
-    loads, shared = {}, {}
-    def cell(number, v, u):
-        return (v, u) if number == 0 else (u, v)
-    for v in ORDER:
-        for u in ORDER:
-            for number in range(2):
-                i, j = cell(number, v, u)
-                rows = pl.ds(number * HALF, HALF)
-                shared[number, v, u] = copies.go(
-                    terms.at[spot(z + i, y + j, 1 - core), rows], sib.at[i, j, rows], "tensor", side)
-                load = pltpu.make_async_copy(
-                    terms.at[spot(z + i, y + j, core), rows], acc.at[i, j, rows], local.at[number * 16 + v * 4 + u])
-                load.start()
-                loads[number, v, u] = load
+FIRST_COPIES = 32 + 32 + 8
+SECOND_COPIES = 16 + 32 + 8
+
+
+def cell(number, v, u):
+    return (v, u) if number == 0 else (u, v)
+
+
+def scatter_rows(acc, sib, landed, z, y, core, copies, result, ensure, arrived):
     def neighbour(number, along_v, step):
         along_z = (number == 0) == along_v
         return spot(z + step, y, core) if along_z else spot(z, y + step, core)
     def own(number, v, u):
         return acc.at[cell(number, v, u)]
     def pair(number, v, u):
-        loads[number, v, u].wait()
-        shared[number, v, u].wait_recv()
+        arrived(number, v, u)
         return (sib.at[cell(number, v, u)], number * HALF)
     def buf(number, u):
         return landed.at[number * 5 + u]
@@ -169,11 +160,13 @@
         ring[number, u].append(
             copies.go(block.at[pl.ds(row, HALF)], b.at[pl.ds(32 + 32 * which, HALF)], "tensor",
                       neighbour(number, along_v, (1, 3)[which])))
+    ensure([(2, u) for u in ORDER] + [(u, 2) for u in ORDER[1:]])
     for u in ORDER:
         for number in range(2):
             block = own(number, 2, u)
             add_rows(block, number * HALF, HALF, [pair(number, 2, u)])
             far(number, True, u, block)
+    ensure([(i, j) for i in ORDER[1:] for j in ORDER[1:]])
     for u in ORDER:
         for number in range(2):
             row = number * HALF
@@ -219,6 +212,32 @@
                         total = total + ref[pl.ds(r + first, 16)].astype(jnp.float32)
                     result[pl.ds(row + first, 16)] = total
 
+def terms_from(terms, acc, sib, local, z, y, core, copies):
+    side = spot(z, y, 1 - core)
+    loads, shared = {}, {}
+    for v in ORDER:
+        for u in ORDER:
+            for number in range(2):
+                i, j = cell(number, v, u)
+                rows = pl.ds(number * HALF, HALF)
+                shared[number, v, u] = copies.go(
+                    terms.at[spot(z + i, y + j, 1 - core), rows], sib.at[i, j, rows], "tensor", side
+                )
+                load = pltpu.make_async_copy(
+                    terms.at[spot(z + i, y + j, core), rows],
+                    acc.at[i, j, rows],
+                    local.at[number * 16 + v * 4 + u],
+                )
+                load.start()
+                loads[number, v, u] = load
+
+    def arrived(number, v, u):
+        loads[number, v, u].wait()
+        shared[number, v, u].wait_recv()
+
+    return (lambda cells: None), arrived
+
+
 def scatter_scratch(width):
     return [
         pltpu.VMEM((4, 4, 64, width), jnp.bfloat16),
@@ -238,6 +257,7 @@
 ADAPTER_FACTOR = 0.5
 PAGE = 128
 CAP_DEV = 16
+VMEM_LIMIT = 62 << 20
 
 
 def normalize(values, gain):
@@ -336,7 +356,7 @@
     for copy in state["shared"]:
         copy.wait_recv()
     homes[0].wait()
-    copies.finish()
+    copies.settle()
     assert copies.n == GATHER_COPIES + EXTRA_COPIES, copies.n
 
 
@@ -367,79 +387,189 @@
             pltpu.SemaphoreType.DMA((count,)),
         ],
         compiler_params=pltpu.CompilerParams(
-            collective_id=0, has_side_effects=True, vmem_limit_bytes=32 << 20
+            collective_id=0, has_side_effects=True, vmem_limit_bytes=VMEM_LIMIT
         ),
     )(tokens, gain.reshape(1, width), shrink, wkv)
 
 
-def middle_kernel(
-    terms_ref, tokens_ref, gain_ref, out_ref, rows_ref, acc, sib, landed, local, total, send, recv
+def late_kernel(
+    terms_ref,
+    tokens_ref,
+    gain_ref,
+    ids_ref,
+    gates_ref,
+    w_gate_ref,
+    w_up_ref,
+    w_down_ref,
+    out_ref,
+    moe_ref,
+    acc,
+    sib,
+    landed,
+    local,
+    total,
+    rows,
+    gate,
+    up,
+    down,
+    slots,
+    stage,
+    pick,
+    mix,
+    weights_sem,
+    send,
+    recv,
 ):
     me, z, y, core = whereabouts()
+    side = spot(z, y, 1 - core)
+    f32, bf16 = jnp.float32, jnp.bfloat16
+    experts, hidden_width, width = w_gate_ref.shape
+    fetches = []
+    for number, (source, held) in enumerate(
+        ((w_gate_ref, gate), (w_up_ref, up), (w_down_ref, down))
+    ):
+        for expert in range(experts):
+            fetch = pltpu.make_async_copy(
+                source.at[expert], held.at[expert], weights_sem.at[number * experts + expert]
+            )
+            fetch.start()
+            fetches.append(fetch)
     greet(partners(z, y, core))
     copies = Copies(send, recv)
-    scatter_rows(terms_ref, acc, sib, landed, local, z, y, core, copies, total)
+    ensure, arrived = terms_from(terms_ref, acc, sib, local, z, y, core, copies)
+
+    tokens_here = ids_ref.shape[1]
+    places = experts * CAP_DEV
+    slot = lax.broadcasted_iota(jnp.int32, (places, 1), 0)
+    expert_of = me * experts + lax.div(slot, CAP_DEV)
+    gates = gates_ref[...]
+    gate_sum = jnp.sum(gates, axis=0, keepdims=True)
+    hit = jnp.zeros((places, tokens_here), f32)
+    weight = jnp.zeros((places, tokens_here), f32)
+    for choice in range(ids_ref.shape[0]):
+        same = ids_ref[choice : choice + 1, :] == expert_of
+        hit = hit + jnp.where(same, 1.0, 0.0)
+        weight = weight + jnp.where(same, gates_ref[choice : choice + 1, :], 0.0)
+    weight = weight / gate_sum
+    chunk = 256
+    block = 64
+    above = lax.broadcasted_iota(jnp.int32, (chunk, chunk), 0)
+    right = lax.broadcasted_iota(jnp.int32, (chunk, chunk), 1)
+    within = lax.div(above, block) == lax.div(right, block)
+    prefix = jnp.where(within & (above <= right), 1.0, 0.0).astype(bf16)
+    same_row = jnp.where(above == right, 1.0, 0.0).astype(bf16)
+    number_in_block = (lax.rem(slot, CAP_DEV) + 1).astype(f32)
+    for begin in range(0, tokens_here, chunk):
+        piece = hit[:, begin : begin + chunk]
+        count = jnp.dot(piece.astype(bf16), prefix, preferred_element_type=f32)
+        taken = (piece > 0.5) & (count == number_in_block)
+        pick[:, begin : begin + chunk] = jnp.where(taken, 1.0, 0.0).astype(bf16)
+        shares = jnp.where(taken, weight[:, begin : begin + chunk], 0.0).astype(bf16)
+        mix[pl.ds(begin, chunk), :] = lax.dot_general(
+            same_row, shares, (((1,), (1,)), ((), ())), preferred_element_type=f32
+        ).astype(bf16)
+
+    scatter_rows(acc, sib, landed, z, y, core, copies, total, ensure, arrived)
     summed = total[...]
     out_ref[...] = summed.astype(out_ref.dtype)
-    rows_ref[me] = normalize(tokens_ref[...].astype(jnp.float32) + summed, gain_ref[...]).astype(
-        rows_ref.dtype
-    )
-    gather_rows(rows_ref, z, y, core, copies)
-    copies.finish()
-    assert copies.n == SCATTER_COPIES + GATHER_COPIES, copies.n
-
-
-def middle(terms, tokens, gain):
+    rows[me] = normalize(tokens_ref[...].astype(f32) + summed, gain_ref[...]).astype(rows.dtype)
+    gather_rows(rows, z, y, core, copies)
+    copies.settle()
+
+    group = chunk // block
+    lane_block = lax.div(lax.broadcasted_iota(jnp.int32, (1, chunk), 1), block)
+    for number in range(tokens_here // chunk):
+        piece = pick[:, number * chunk : (number + 1) * chunk]
+        spread = jnp.concatenate(
+            [jnp.where(lane_block == part, piece, jnp.zeros_like(piece)) for part in range(group)],
+            axis=0,
+        )
+        block_rows = rows[number * group : (number + 1) * group].reshape(chunk, width)
+        taken_rows = jnp.dot(spread, block_rows, preferred_element_type=f32).astype(bf16)
+        slots[number * group : (number + 1) * group] = taken_rows.reshape(group, places, width)
+
+    blocks = tokens_here // block
+    for expert in range(experts):
+        here = slice(expert * CAP_DEV, (expert + 1) * CAP_DEV)
+        taken_rows = slots[:, here, :].reshape(blocks * CAP_DEV, width)
+        fetches[expert].wait()
+        gated = lax.dot_general(
+            taken_rows, gate[expert], (((1,), (1,)), ((), ())), preferred_element_type=f32
+        )
+        fetches[experts + expert].wait()
+        raised = lax.dot_general(
+            taken_rows, up[expert], (((1,), (1,)), ((), ())), preferred_element_type=f32
+        )
+        hidden = (gated / (1.0 + jnp.exp(-gated)) * raised).astype(bf16)
+        fetches[2 * experts + expert].wait()
+        for begin in range(0, width, 512):
+            piece = jnp.dot(
+                hidden, down[expert, :, begin : begin + 512], preferred_element_type=f32
+            ).astype(bf16)
+            slots[:, here, begin : begin + 512] = piece.reshape(blocks, CAP_DEV, 512)
+
+    shared = {}
+    waited = set()
+
+    def combine(index):
+        part = mix[pl.ds(pl.multiple_of(index * block, block), block), :]
+        return jnp.dot(part, slots[index], preferred_element_type=f32).astype(bf16)
+
+    def make(cells):
+        for i, j in cells:
+            if (i, j) in shared:
+                continue
+            stage[i, j] = combine(spot(z + i, y + j, 1 - core))
+            shared[i, j] = copies.go(stage.at[i, j], sib.at[i, j], "tensor", side)
+            acc[i, j] = combine(spot(z + i, y + j, core))
+
+    def came(number, v, u):
+        where = cell(number, v, u)
+        make([where])
+        if where not in waited:
+            waited.add(where)
+            shared[where].wait_recv()
+
+    scatter_rows(acc, sib, landed, z, y, core, copies, total, make, came)
+    moe_ref[...] = total[...].astype(moe_ref.dtype)
+    copies.settle()
+    assert copies.n == LATE_COPIES, copies.n
+
+
+LATE_COPIES = FIRST_COPIES + GATHER_COPIES + SECOND_COPIES
+
+
+def late(terms, tokens, gain, ids, gates, w_gate, w_up, w_down):
     rows, width = tokens.shape
-    count = SCATTER_COPIES + GATHER_COPIES
+    experts = w_gate.shape[0]
+    places = experts * CAP_DEV
+    everyone = terms.shape[0]
     vmem = pl.BlockSpec(memory_space=pltpu.VMEM)
+    far = pl.BlockSpec(memory_space=pl.ANY)
     return pl.pallas_call(
-        middle_kernel,
-        out_shape=(
-            jax.ShapeDtypeStruct((rows, width), jnp.bfloat16),
-            jax.ShapeDtypeStruct((32, rows, width), jnp.bfloat16),
-        ),
-        in_specs=[pl.BlockSpec(memory_space=pl.ANY), vmem, vmem],
+        late_kernel,
+        out_shape=(jax.ShapeDtypeStruct((rows, width), jnp.bfloat16),) * 2,
+        in_specs=[far, vmem, vmem, vmem, vmem, far, far, far],
         out_specs=(vmem, vmem),
         scratch_shapes=scatter_scratch(width)
         + [
             pltpu.VMEM((rows, width), jnp.float32),
-            pltpu.SemaphoreType.DMA((count,)),
-            pltpu.SemaphoreType.DMA((count,)),
+            pltpu.VMEM((everyone, rows, width), jnp.bfloat16),
+            pltpu.VMEM(w_gate.shape, jnp.bfloat16),
+            pltpu.VMEM(w_up.shape, jnp.bfloat16),
+            pltpu.VMEM(w_down.shape, jnp.bfloat16),
+            pltpu.VMEM((everyone, places, width), jnp.bfloat16),
+            pltpu.VMEM((4, 4, rows, width), jnp.bfloat16),
+            pltpu.VMEM((places, everyone * rows), jnp.bfloat16),
+            pltpu.VMEM((everyone * rows, places), jnp.bfloat16),
+            pltpu.SemaphoreType.DMA((3 * experts,)),
+            pltpu.SemaphoreType.DMA((LATE_COPIES,)),
+            pltpu.SemaphoreType.DMA((LATE_COPIES,)),
         ],
         compiler_params=pltpu.CompilerParams(
-            collective_id=1, has_side_effects=True, vmem_limit_bytes=40 << 20
+            collective_id=1, has_side_effects=True, vmem_limit_bytes=VMEM_LIMIT
         ),
-    )(terms, tokens, gain.reshape(1, width))
-
-
-def leave_kernel(terms_ref, out_ref, acc, sib, landed, local, total, send, recv):
-    me, z, y, core = whereabouts()
-    greet(partners(z, y, core))
-    copies = Copies(send, recv)
-    scatter_rows(terms_ref, acc, sib, landed, local, z, y, core, copies, total)
-    out_ref[...] = total[...].astype(out_ref.dtype)
-    copies.finish()
-    assert copies.n == SCATTER_COPIES, copies.n
-
-
-def leave(terms):
-    rows, width = terms.shape[1:]
-    return pl.pallas_call(
-        leave_kernel,
-        out_shape=jax.ShapeDtypeStruct((rows, width), jnp.bfloat16),
-        in_specs=[pl.BlockSpec(memory_space=pl.ANY)],
-        out_specs=pl.BlockSpec(memory_space=pltpu.VMEM),
-        scratch_shapes=scatter_scratch(width)
-        + [
-            pltpu.VMEM((rows, width), jnp.float32),
-            pltpu.SemaphoreType.DMA((SCATTER_COPIES,)),
-            pltpu.SemaphoreType.DMA((SCATTER_COPIES,)),
-        ],
-        compiler_params=pltpu.CompilerParams(
-            collective_id=2, has_side_effects=True, vmem_limit_bytes=32 << 20
-        ),
-    )(terms)
+    )(terms, tokens, gain.reshape(1, width), ids, gates, w_gate, w_up, w_down)
 
 
 BLOCK = 512
@@ -699,16 +829,8 @@
             pltpu.VMEM((columns, total + 4 * PAGE), jnp.float32),
             pltpu.VMEM((BLOCK, 2 * depth), jnp.float32),
         ],
-        compiler_params=pltpu.CompilerParams(vmem_limit_bytes=48 << 20),
+        compiler_params=pltpu.CompilerParams(vmem_limit_bytes=VMEM_LIMIT),
     )(lengths, groups, page_table, *small, x, *tables)
-
-
-def expert_apply(rows, gate_rows, up_rows, down_rows):
-    gate_value = jnp.einsum("secx,efx->secf", rows, gate_rows, preferred_element_type=jnp.float32)
-    up_value = jnp.einsum("secx,efx->secf", rows, up_rows, preferred_element_type=jnp.float32)
-    hidden = (jax.nn.silu(gate_value) * up_value).astype(jnp.bfloat16)
-    out = jnp.einsum("secf,efx->secx", hidden, down_rows, preferred_element_type=jnp.float32)
-    return lax.optimization_barrier(out.astype(jnp.bfloat16))
 
 
 def local(
@@ -761,39 +883,16 @@
         shrink_o.reshape(adapters * rank, -1),
         expand_o.reshape(adapters * rank, width),
     )
-    attn_out, moe_in = middle(attn_terms.reshape(parts, own_rows, width), tokens, moe_gain)
-    experts_here = w_gate.shape[0]
-    own_experts = place * experts_here + jnp.arange(experts_here, dtype=jnp.int32)
-    choose = expert_ids[:, :, None] == own_experts[None, None, :]
-    share = expert_gates / jnp.sum(expert_gates, axis=1, keepdims=True)
-    weight = jnp.sum(jnp.where(choose, share[:, :, None], 0.0), axis=1)
-    hit = jnp.any(choose, axis=1).reshape(parts, own_rows, experts_here)
-    weight = weight.reshape(parts, own_rows, experts_here)
-    below = jnp.tril(jnp.ones((own_rows, own_rows), jnp.bfloat16))
-    rank_in_block = jnp.einsum(
-        "ut,ste->sue", below, hit.astype(jnp.bfloat16), preferred_element_type=jnp.float32
-    )
-    numbers = jnp.arange(1, CAP_DEV + 1, dtype=jnp.float32)
-    picked = hit[..., None] & (rank_in_block[..., None] == numbers)
-    pick = picked.astype(jnp.bfloat16)
-    slot_weight = jnp.sum(jnp.where(picked, weight[..., None], 0.0), axis=1)
-    rows = jnp.einsum(
-        "stek,std->eskd",
-        pick,
-        moe_in,
-        preferred_element_type=jnp.float32,
-    ).astype(jnp.bfloat16)
-    rows = rows.reshape(1, experts_here, parts * CAP_DEV, width)
-    outputs = expert_apply(rows, w_gate, w_up, w_down)[0]
-    slot_weight = slot_weight.transpose(1, 0, 2).reshape(experts_here, parts * CAP_DEV, 1)
-    weighted = (outputs.astype(jnp.float32) * slot_weight).astype(jnp.bfloat16)
-    moe_terms = jnp.einsum(
-        "stek,eskd->std",
-        pick,
-        weighted.reshape(experts_here, parts, CAP_DEV, width),
-        preferred_element_type=jnp.float32,
-    )
-    moe_total = leave(moe_terms.astype(jnp.bfloat16))
+    attn_out, moe_total = late(
+        attn_terms.reshape(parts, own_rows, width),
+        tokens,
+        moe_gain,
+        expert_ids.T,
+        expert_gates.T,
+        w_gate,
+        w_up,
+        w_down,
+    )
     return (attn_out, moe_total, kv_pages)
 
 

time: 237 us -> 224 us (0.945)
  Pallas kernels: 180 us -> 216 us
  matrix products: 27.9 us -> 0 us
  local copies, waits for them, and re-layouts: 26.7 us -> 6.88 us
    dot_general x4 -> x0, matrix products: 23.3 us -> none  [the longest x1 13 us: expert_apply(): jnp.einsum('secf,efx->secx', hidden, down_rows, preferred_element_type=jn...]
    pallas_call x1, Pallas kernels: 41.6 us -> 62.1 us  [enter(): pl.pallas_call(enter_kernel, out_shape=(jax.ShapeDtypeStruct((32, rows, w...]
    unnamed x49 -> x5, local copies, waits for them, and re-layouts: 25.1 us -> 4.98 us
    pallas_call x2 -> x1, Pallas kernels: 93.9 us -> 108 us  [late(): pl.pallas_call(late_kernel, out_shape=(jax.ShapeDtypeStruct((rows, width)...]
    unnamed x1 -> x0, matrix products: 4.61 us -> none
where the time goes in v4:
time: 224 us; the launch traced here: 223 us
  Pallas kernels  216 us (96%)
  local copies, waits for them, and re-layouts  6.88 us (3%)
    pallas_call x1, Pallas kernels, late(): pl.pallas_call(late_kernel, out_shape=(jax.ShapeDtypeStruct((rows, width)...  108 us
    pallas_call x1, Pallas kernels, enter(): pl.pallas_call(enter_kernel, out_shape=(jax.ShapeDtypeStruct((32, rows, w...  62.1 us
    pallas_call x1, Pallas kernels, heart(): pl.pallas_call(heart_kernel, grid=(total // BLOCK,), out_shape=(jax.Shape...  46 us
    unnamed x5, local copies, waits for them, and re-layouts  4.98 us

profile of v4, /device:TPU:1, one launch (start us, length us, event | category | flops | bytes accessed | tf_op | source)
XLA Modules:
  0.0 223.4 jit_solution(7142291482775435642)
XLA Ops:
  0.6 1.6 copy.28
  2.3 1.3 reshape.45.gain_ref
  3.6 62.1 %shard_map.238 = (bf16[32,64,2048]{2,1,0:T(8,128)(2,1)}, bf16[16,48,2048]{2,1,0:T(8,128)(2,1)}, bf16[4,4,2,8,2048]{4,3,2,1,0:T(8,128)(2,1)}) custom-call(bf16[64,2048]{1,0:T(8,128)(2,1)} %tokens_ref.3, bf16[1,2048]{1,0:T(2,128)(2,1)} %reshape.45.gain_ref, bf16[4,48,2048]{2,1,0:T(8,128)(2,1)} %shrink_ref.1, bf16[4,8,2048]{2,1,0:T(8,128)(2,1)} %bitcast.20), custom_call_target="tpu_custom_call" | custom-call | tf_op jit(solution)/shard_map/pallas_call | solution.py:366
  65.7 0.0 copy-start
  65.7 46.0 %shard_map.239 = (bf16[2048,2048]{1,0:T(8,128)(2,1)}, bf16[64,32,128]{2,1,0:T(8,128)(2,1)}) custom-call(s32[1,32]{1,0:T(1,128)} %lens_ref.1, s32[1,32]{1,0:T(1,128)} %groups_ref.1, s32[1,64]{1,0:T(1,128)} %pages_s.1, s32[1,32]{1,0:T(1,128)} %lens_ref.1, s32[1,32]{1,0:T(1,128)} %groups_ref.1, s32[1,32]{1,0:T(1,128)} %adapters_ref.1, s32[1,16]{1,0:T(1,128)} %bitcast.25, ...), custom_call_target="tpu_custom_call" | custom-call | tf_op jit(solution)/shard_map/pallas_call | solution.py:810
  111.7 0.0 copy-done
  111.7 0.6 reshape.53.gain_ref
  112.3 107.8 %shard_map.240 = (bf16[64,2048]{1,0:T(8,128)(2,1)}, bf16[64,2048]{1,0:T(8,128)(2,1)}) custom-call(bf16[32,64,2048]{2,1,0:T(8,128)(2,1)} %bitcast.16, bf16[64,2048]{1,0:T(8,128)(2,1)} %tokens_ref.3, bf16[1,2048]{1,0:T(2,128)(2,1)} %reshape.53.gain_ref, s32[8,2048]{1,0:T(8,128)} %bitcast.23, f32[8,2048]{1,0:T(8,128)} %bitcast.24, ...), custom_call_target="tpu_custom_call" | custom-call | tf_op jit(solution)/shard_map/pallas_call | solution.py:549
  220.0 1.7 copy.31
  221.7 1.7 copy.32
Async XLA Ops:
  65.7 46.0 %copy-start = (bf16[2048]{0:T(1024)(128)(2,1)S(1)}, bf16[2048]{0:T(1024)(128)(2,1)}, u32[]{:S(2)}) copy-start(bf16[2048]{0:T(1024)(128)(2,1)} %param.25) | copy-start | bytes 12292

commit v5 on v4

--- a/solution.py
+++ b/solution.py
@@ -41,16 +41,33 @@
             copy.wait_send()
         self.all = []
 
-def gather_rows(out, z, y, core, copies, hooks=()):
-    hooks = list(hooks)
-    def hook():
-        if hooks:
-            hooks.pop(0)()
+EARLY = ((0, 0), (0, 1), (0, 3), (1, 0), (3, 0))
+MIDDLE = ((2, 0), (0, 2), (3, 3), (3, 1), (1, 3), (1, 1))
+LAST = ((3, 2), (2, 3), (2, 1), (1, 2), (2, 2))
+CELLS = EARLY + MIDDLE + LAST
+
+
+def gather_rows(out, z, y, core, copies, hooks):
     side = spot(z, y, 1 - core)
-    shared = []
-    def share(block, row, rows):
+    shared = {}
+    waited = set()
+
+    def ready(cells):
+        for i, j in cells:
+            for key in ((0, i, j), (1, i, j)):
+                if key in shared and key not in waited:
+                    waited.add(key)
+                    shared[key].wait_recv()
+
+    def hook(name):
+        if name in hooks:
+            hooks[name](ready)
+
+    def share(block, row, rows, number, u, v):
         piece = out.at[block, pl.ds(row, rows)]
-        shared.append(copies.go(piece, piece, "tensor", side))
+        where = (number, v, u) if number == 0 else (number, u, v)
+        shared[where] = copies.go(piece, piece, "tensor", side)
+
     def send(block, row, rows, target):
         piece = out.at[block, pl.ds(row, rows)]
         return copies.go(piece, piece, "tensor", target)
@@ -59,6 +76,7 @@
     for number in range(2):
         p = Part()
         p.row = number * HALF
+        p.number = number
         if number == 0:
             p.at = lambda u, v: spot(z + v, y + u, core)
         else:
@@ -74,15 +92,15 @@
         block = p.at(off, 0) if along_u else p.at(u, off)
         target = (p.at(1, 0), p.at(3, 0))[which] if along_u else (p.at(0, 1), p.at(0, 3))[which]
         fwd = send(block, p.row + which * (HALF // 2), HALF // 2, target)
-        share(block, p.row, HALF)
+        share(block, p.row, HALF, p.number, *((off, 0) if along_u else (u, off)))
         return fwd
     me = spot(z, y, core)
     for p in parts:
         p.u = ring_open(p, True, 0)
     for p in parts:
         p.v = {0: ring_open(p, False, 0)}
-    share(me, 0, 2 * HALF)
-    hook()
+    share(me, 0, 2 * HALF, 0, 0, 0)
+    hook("opened")
     for which in range(2):
         for p in parts:
             p.u.append(ring_pass(p, True, 0, p.u, which))
@@ -91,11 +109,11 @@
     for which in range(2):
         for p in parts:
             p.v[0].append(ring_pass(p, False, 0, p.v[0], which))
-    hook()
+    hook("early")
     for p in parts:
         p.u[2].wait_recv()
         p.u[3].wait_recv()
-        share(p.at(2, 0), p.row, HALF)
+        share(p.at(2, 0), p.row, HALF, p.number, 2, 0)
         p.v[2] = ring_open(p, False, 2)
     for off in (3, 1):
         for which in range(2):
@@ -105,18 +123,21 @@
             done = 0 if off == 3 else 3
             p.v[done][2].wait_recv()
             p.v[done][3].wait_recv()
-            share(p.at(done, 2), p.row, HALF)
-        hook()
+            share(p.at(done, 2), p.row, HALF, p.number, done, 2)
+        if off == 3:
+            hook("third")
     for which in range(2):
         for p in parts:
             p.v[2].append(ring_pass(p, False, 2, p.v[2], which))
+    hook("middle")
     for off in (1, 2):
         for p in parts:
             p.v[off][2].wait_recv()
             p.v[off][3].wait_recv()
-            share(p.at(off, 2), p.row, HALF)
-    for copy in shared:
-        copy.wait_recv()
+            share(p.at(off, 2), p.row, HALF, p.number, off, 2)
+    hook("last")
+    ready(CELLS)
+    assert len(waited) == len(shared)
 
 def add_rows(dst, start, rows, sources):
     for first in range(0, rows, 16):
@@ -251,7 +272,7 @@
 
 
 GATHER_COPIES = 2 * 20 + 31
-EXTRA_COPIES = 7 + 11
+EXTRA_COPIES = 9 + 11
 NORM_EPS = 1e-06
 ROPE_BASE = 1000000.0
 ADAPTER_FACTOR = 0.5
@@ -277,9 +298,10 @@
     across = lax.rem(group + 2, SIDE)
     copies = Copies(send, recv)
     homes = [
-        pltpu.make_async_copy(shrink_ref, factors_ref.at[pl.ds(4 * group, 4)], local.at[0]),
-        pltpu.make_async_copy(wkv_ref.at[z], wkv_all_ref.at[z, y, core], local.at[1]),
+        pltpu.make_async_copy(shrink_ref.at[held], factors_ref.at[:, 4 * group + held], local.at[held])
+        for held in range(4)
     ]
+    homes.append(pltpu.make_async_copy(wkv_ref.at[z], wkv_all_ref.at[z, y, core], local.at[4]))
     for home in homes:
         home.start()
     rows_ref[me] = normalize(tokens_ref[...].astype(jnp.float32), gain_ref[...]).astype(
@@ -309,29 +331,40 @@
                 )
             )
         state["spread"] = spread
-        half = factors_ref.at[pl.ds(4 * group + 2 * core, 2)]
-        mine = shrink_ref.at[pl.ds(2 * core, 2)]
-        state["factors"] = [copies.go(mine, half, "dp", up), copies.go(mine, half, "dp", down)]
+        state["factors"] = [[], []]
+        for held in range(2):
+            slot = 2 * core + held
+            for which, target in enumerate((up, down)):
+                state["factors"][which].append(
+                    copies.go(
+                        shrink_ref.at[slot], factors_ref.at[:, 4 * group + slot], "dp", target
+                    )
+                )
 
     def kv(y_at, first=0, count=4):
         return wkv_all_ref.at[pl.ds(first, count), lax.rem(y_at, SIDE), core]
 
-    def middle_extras():
+    def kv_extras(ready):
         for copy in state["spread"]:
             copy.wait_recv()
-        homes[1].wait()
+        homes[4].wait()
         block = kv(y)
         state["kv"] = [
             copies.go(block, block, "tensor", spot(z, y + 1, core)),
             copies.go(block, block, "tensor", spot(z, y + 3, core)),
         ]
         state["shared"] = [copies.go(block, block, "tensor", side)]
+
+    def factor_extras(ready):
+        state["far"] = []
         for which, (origin, target) in enumerate(((down, up), (up, down))):
-            state["factors"][which].wait_recv()
-            one = factors_ref.at[4 * origin + 2 * core + which]
-            state["factors"].append(copies.go(one, one, "dp", target))
-            both = factors_ref.at[pl.ds(4 * origin + 2 * core, 2)]
+            for copy in state["factors"][which]:
+                copy.wait_recv()
+            one = factors_ref.at[:, 4 * origin + 2 * core + which]
+            state["far"].append(copies.go(one, one, "dp", target))
+            both = factors_ref.at[:, pl.ds(4 * origin + 2 * core, 2)]
             state["shared"].append(copies.go(both, both, "tensor", side))
+        pass_extras()
 
     def pass_extras():
         for which, (origin, target) in enumerate(((y + 3, y + 1), (y + 1, y + 3))):
@@ -340,22 +373,26 @@
             state["kv"].append(copies.go(piece, piece, "tensor", spot(z, target, core)))
             whole = kv(origin)
             state["shared"].append(copies.go(whole, whole, "tensor", side))
-        state["factors"][2].wait_recv()
-        state["factors"][3].wait_recv()
-        both = factors_ref.at[pl.ds(4 * across + 2 * core, 2)]
+
+    def close_extras():
+        for copy in state["far"]:
+            copy.wait_recv()
+        both = factors_ref.at[:, pl.ds(4 * across + 2 * core, 2)]
         state["shared"].append(copies.go(both, both, "tensor", side))
-
-    def close_extras():
         state["kv"][2].wait_recv()
         state["kv"][3].wait_recv()
         whole = kv(y + 2)
         state["shared"].append(copies.go(whole, whole, "tensor", side))
 
     open_extras()
-    gather_rows(rows_ref, z, y, core, copies, [middle_extras, pass_extras, close_extras])
+    gather_rows(
+        rows_ref, z, y, core, copies, {"opened": kv_extras, "third": factor_extras}
+    )
+    close_extras()
     for copy in state["shared"]:
         copy.wait_recv()
-    homes[0].wait()
+    for home in homes[:4]:
+        home.wait()
     copies.settle()
     assert copies.n == GATHER_COPIES + EXTRA_COPIES, copies.n
 
@@ -367,7 +404,7 @@
         enter_kernel,
         out_shape=(
             jax.ShapeDtypeStruct((32, rows, width), jnp.bfloat16),
-            jax.ShapeDtypeStruct((4 * shrink.shape[0],) + shrink.shape[1:], jnp.bfloat16),
+            jax.ShapeDtypeStruct((shrink.shape[1], 4 * shrink.shape[0]) + shrink.shape[2:], jnp.bfloat16),
             jax.ShapeDtypeStruct((4, 4, 2) + wkv.shape[1:], jnp.bfloat16),
         ),
         in_specs=[
@@ -378,11 +415,11 @@
         ],
         out_specs=(
             pl.BlockSpec(memory_space=pltpu.VMEM),
-            pl.BlockSpec(memory_space=pl.ANY),
-            pl.BlockSpec(memory_space=pl.ANY),
+            pl.BlockSpec(memory_space=pltpu.VMEM),
+            pl.BlockSpec(memory_space=pltpu.VMEM),
         ),
         scratch_shapes=[
-            pltpu.SemaphoreType.DMA((2,)),
+            pltpu.SemaphoreType.DMA((5,)),
             pltpu.SemaphoreType.DMA((count,)),
             pltpu.SemaphoreType.DMA((count,)),
         ],
@@ -473,55 +510,74 @@
     summed = total[...]
     out_ref[...] = summed.astype(out_ref.dtype)
     rows[me] = normalize(tokens_ref[...].astype(f32) + summed, gain_ref[...]).astype(rows.dtype)
-    gather_rows(rows, z, y, core, copies)
+    pair_rows = 2 * block
+    lane_block = lax.div(lax.broadcasted_iota(jnp.int32, (1, pair_rows), 1), block)
+
+    def apply_experts(cells):
+        first = CELLS.index(cells[0])
+        for number, (i, j) in enumerate(cells):
+            index = spot(z + i, y + j, 0)
+            piece = pick[:, pl.ds(pl.multiple_of(index * block, pair_rows), pair_rows)]
+            spread = jnp.concatenate(
+                [jnp.where(lane_block == part, piece, jnp.zeros_like(piece)) for part in range(2)],
+                axis=0,
+            )
+            taken_rows = jnp.dot(
+                spread, rows[pl.ds(index, 2)].reshape(pair_rows, width), preferred_element_type=f32
+            )
+            slots[2 * (first + number) : 2 * (first + number) + 2] = taken_rows.astype(bf16).reshape(
+                2, places, width
+            )
+        blocks = slice(2 * first, 2 * (first + len(cells)))
+        count = 2 * len(cells)
+        for expert in range(experts):
+            here = slice(expert * CAP_DEV, (expert + 1) * CAP_DEV)
+            taken_rows = slots[blocks, here, :].reshape(count * CAP_DEV, width)
+            gated = lax.dot_general(
+                taken_rows, gate[expert], (((1,), (1,)), ((), ())), preferred_element_type=f32
+            )
+            raised = lax.dot_general(
+                taken_rows, up[expert], (((1,), (1,)), ((), ())), preferred_element_type=f32
+            )
+            hidden = (gated / (1.0 + jnp.exp(-gated)) * raised).astype(bf16)
+            for begin in range(0, width, 512):
+                piece = jnp.dot(
+                    hidden, down[expert, :, begin : begin + 512], preferred_element_type=f32
+                ).astype(bf16)
+                slots[blocks, here, begin : begin + 512] = piece.reshape(count, CAP_DEV, 512)
+
+    def early_experts(ready):
+        for fetch in fetches:
+            fetch.wait()
+        ready(EARLY)
+        apply_experts(EARLY)
+
+    def middle_experts(ready):
+        ready(EARLY + MIDDLE)
+        apply_experts(MIDDLE)
+
+    gather_rows(
+        rows, z, y, core, copies, {"early": early_experts, "middle": middle_experts}
+    )
+    apply_experts(LAST)
     copies.settle()
-
-    group = chunk // block
-    lane_block = lax.div(lax.broadcasted_iota(jnp.int32, (1, chunk), 1), block)
-    for number in range(tokens_here // chunk):
-        piece = pick[:, number * chunk : (number + 1) * chunk]
-        spread = jnp.concatenate(
-            [jnp.where(lane_block == part, piece, jnp.zeros_like(piece)) for part in range(group)],
-            axis=0,
-        )
-        block_rows = rows[number * group : (number + 1) * group].reshape(chunk, width)
-        taken_rows = jnp.dot(spread, block_rows, preferred_element_type=f32).astype(bf16)
-        slots[number * group : (number + 1) * group] = taken_rows.reshape(group, places, width)
-
-    blocks = tokens_here // block
-    for expert in range(experts):
-        here = slice(expert * CAP_DEV, (expert + 1) * CAP_DEV)
-        taken_rows = slots[:, here, :].reshape(blocks * CAP_DEV, width)
-        fetches[expert].wait()
-        gated = lax.dot_general(
-            taken_rows, gate[expert], (((1,), (1,)), ((), ())), preferred_element_type=f32
-        )
-        fetches[experts + expert].wait()
-        raised = lax.dot_general(
-            taken_rows, up[expert], (((1,), (1,)), ((), ())), preferred_element_type=f32
-        )
-        hidden = (gated / (1.0 + jnp.exp(-gated)) * raised).astype(bf16)
-        fetches[2 * experts + expert].wait()
-        for begin in range(0, width, 512):
-            piece = jnp.dot(
-                hidden, down[expert, :, begin : begin + 512], preferred_element_type=f32
-            ).astype(bf16)
-            slots[:, here, begin : begin + 512] = piece.reshape(blocks, CAP_DEV, 512)
 
     shared = {}
     waited = set()
 
-    def combine(index):
+    def combine(i, j, which):
+        index = spot(z + i, y + j, which)
         part = mix[pl.ds(pl.multiple_of(index * block, block), block), :]
-        return jnp.dot(part, slots[index], preferred_element_type=f32).astype(bf16)
+        held = slots[2 * CELLS.index((i, j)) + which]
+        return jnp.dot(part, held, preferred_element_type=f32).astype(bf16)
 
     def make(cells):
         for i, j in cells:
             if (i, j) in shared:
                 continue
-            stage[i, j] = combine(spot(z + i, y + j, 1 - core))
+            stage[i, j] = combine(i, j, 1 - core)
             shared[i, j] = copies.go(stage.at[i, j], sib.at[i, j], "tensor", side)
-            acc[i, j] = combine(spot(z + i, y + j, core))
+            acc[i, j] = combine(i, j, core)
 
     def came(number, v, u):
         where = cell(number, v, u)
@@ -671,13 +727,14 @@
             * gain_ref[...].astype(f32)
         )
 
-    rank = factors_ref.shape[1] // 3
+    total_rank = q_up_ref.shape[0]
+    rank = total_rank // adapters
     mine = slot == lax.div(lax.broadcasted_iota(jnp.int32, (1, adapters * rank), 1), rank)
     x = x_ref[...]
     lora = []
+    projected = lax.dot_general(x, factors_ref[...], TRANSPOSED, preferred_element_type=f32)
     for part in range(3):
-        table = factors_ref[:, part * rank : (part + 1) * rank, :].reshape(adapters * rank, -1)
-        shrunk = lax.dot_general(x, table, TRANSPOSED, preferred_element_type=f32)
+        shrunk = projected[:, part * total_rank : (part + 1) * total_rank]
         placed = jnp.where(mine, shrunk, 0.0).astype(bf16)
         if part == 0:
             up = q_up_ref[...]
@@ -863,7 +920,12 @@
     own_rows, width = tokens.shape
     grand_total = own_rows * parts
     adapters, rank, kv_width = key_value_up_factors.shape
-    x_rows, factors, wkv_all = enter(tokens, attn_gain, shrink_qkv, w_kv.transpose(1, 0, 2))
+    x_rows, factors, wkv_all = enter(
+        tokens,
+        attn_gain,
+        shrink_qkv.reshape(-1, 3, rank, width),
+        w_kv.transpose(1, 0, 2),
+    )
     head_width = 2 * q_gain.shape[0]
     attn_terms, kv_pages = heart(
         lengths,
@@ -874,7 +936,7 @@
         q_gain,
         k_gain,
         x_rows.reshape(grand_total, width),
-        factors,
+        factors.reshape(-1, width),
         wkv_all.reshape(head_width, width),
         query_weight,
         query_up_factors.reshape(adapters * rank, -1),

time: 224 us -> 196 us (0.88)
  Pallas kernels: 216 us -> 188 us
    pallas_call x1, Pallas kernels: 62.1 us -> 46.1 us  [enter(): pl.pallas_call(enter_kernel, out_shape=(jax.ShapeDtypeStruct((32, rows, w...]
    pallas_call x1, Pallas kernels: 46 us -> 40.2 us  [heart(): pl.pallas_call(heart_kernel, grid=(total // BLOCK,), out_shape=(jax.Shape...]
    pallas_call x1, Pallas kernels: 108 us -> 102 us  [late(): pl.pallas_call(late_kernel, out_shape=(jax.ShapeDtypeStruct((rows, width)...]
where the time goes in v5:
time: 196 us
  Pallas kernels  188 us (96%)
  local copies, waits for them, and re-layouts  6.88 us (4%)
    pallas_call x1, Pallas kernels, late(): pl.pallas_call(late_kernel, out_shape=(jax.ShapeDtypeStruct((rows, width)...  102 us
    pallas_call x1, Pallas kernels, enter(): pl.pallas_call(enter_kernel, out_shape=(jax.ShapeDtypeStruct((32, rows, w...  46.1 us
    pallas_call x1, Pallas kernels, heart(): pl.pallas_call(heart_kernel, grid=(total // BLOCK,), out_shape=(jax.Shape...  40.2 us
    unnamed x5, local copies, waits for them, and re-layouts  4.98 us

profile of v5, /device:TPU:1, one launch (start us, length us, event | category | flops | bytes accessed | tf_op | source)
XLA Modules:
  0.0 195.9 jit_solution(1984043064803043316)
XLA Ops:
  0.6 1.6 copy.28
  2.3 1.3 reshape.51.gain_ref
  3.6 46.1 %shard_map.238 = (bf16[32,64,2048]{2,1,0:T(8,128)(2,1)}, bf16[3,16,16,2048]{3,2,1,0:T(8,128)(2,1)}, bf16[4,4,2,8,2048]{4,3,2,1,0:T(8,128)(2,1)}) custom-call(bf16[64,2048]{1,0:T(8,128)(2,1)} %tokens_ref.3, bf16[1,2048]{1,0:T(2,128)(2,1)} %reshape.51.gain_ref, bf16[4,3,16,2048]{3,2,1,0:T(8,128)(2,1)} %bitcast.22, bf16[4,8,2048]{2,1,0:T(8,128)(2,1)} %bitcast.24), custom_call_target="tpu_custom_call" | custom-call | tf_op jit(solution)/shard_map/pallas_call | solution.py:403
  49.6 0.0 copy-start
  49.6 40.2 %shard_map.239 = (bf16[2048,2048]{1,0:T(8,128)(2,1)}, bf16[64,32,128]{2,1,0:T(8,128)(2,1)}) custom-call(s32[1,32]{1,0:T(1,128)} %lens_ref.1, s32[1,32]{1,0:T(1,128)} %groups_ref.1, s32[1,64]{1,0:T(1,128)} %pages_s.1, s32[1,32]{1,0:T(1,128)} %lens_ref.1, s32[1,32]{1,0:T(1,128)} %groups_ref.1, s32[1,32]{1,0:T(1,128)} %adapters_ref.1, s32[1,16]{1,0:T(1,128)} %bitcast.29, ...), custom_call_target="tpu_custom_call" | custom-call | tf_op jit(solution)/shard_map/pallas_call | solution.py:867
  89.8 0.0 copy-done
  89.8 0.6 reshape.61.gain_ref
  90.4 102.2 %shard_map.240 = (bf16[64,2048]{1,0:T(8,128)(2,1)}, bf16[64,2048]{1,0:T(8,128)(2,1)}) custom-call(bf16[32,64,2048]{2,1,0:T(8,128)(2,1)} %bitcast.18, bf16[64,2048]{1,0:T(8,128)(2,1)} %tokens_ref.3, bf16[1,2048]{1,0:T(2,128)(2,1)} %reshape.61.gain_ref, s32[8,2048]{1,0:T(8,128)} %bitcast.27, f32[8,2048]{1,0:T(8,128)} %bitcast.28, ...), custom_call_target="tpu_custom_call" | custom-call | tf_op jit(solution)/shard_map/pallas_call | solution.py:605
  192.6 1.7 copy.31
  194.3 1.7 copy.32
Async XLA Ops:
  49.6 40.2 %copy-start = (bf16[2048]{0:T(1024)(128)(2,1)S(1)}, bf16[2048]{0:T(1024)(128)(2,1)}, u32[]{:S(2)}) copy-start(bf16[2048]{0:T(1024)(128)(2,1)} %param.25) | copy-start | bytes 12292

commit v6 on v5

--- a/solution.py
+++ b/solution.py
@@ -289,13 +289,51 @@
     )
 
 
-def enter_kernel(
-    tokens_ref, gain_ref, shrink_ref, wkv_ref, rows_ref, factors_ref, wkv_all_ref, local, send, recv
+def front_kernel(
+    lens_ref,
+    groups_ref,
+    adapters_ref,
+    slots_ref,
+    q_gain_ref,
+    k_gain_ref,
+    gain_ref,
+    tokens_ref,
+    shrink_ref,
+    wkv_ref,
+    wq_far,
+    q_up_far,
+    kv_up_far,
+    wo_far,
+    shrink_o_far,
+    expand_far,
+    terms_ref,
+    across,
+    rows_ref,
+    factors_ref,
+    wkv_all_ref,
+    wkv_held,
+    wq_ref,
+    q_up_ref,
+    kv_up_ref,
+    out_table,
+    shrink_o_ref,
+    tab,
+    trig,
+    queries,
+    keys,
+    values,
+    acc,
+    stage,
+    fetch_sem,
+    store_sem,
+    local,
+    send,
+    recv,
 ):
     me, z, y, core = whereabouts()
     group = lax.axis_index("dp")
     up, down = lax.rem(group + 1, SIDE), lax.rem(group + 3, SIDE)
-    across = lax.rem(group + 2, SIDE)
+    opposite = lax.rem(group + 2, SIDE)
     copies = Copies(send, recv)
     homes = [
         pltpu.make_async_copy(shrink_ref.at[held], factors_ref.at[:, 4 * group + held], local.at[held])
@@ -304,6 +342,21 @@
     homes.append(pltpu.make_async_copy(wkv_ref.at[z], wkv_all_ref.at[z, y, core], local.at[4]))
     for home in homes:
         home.start()
+    depth = wq_ref.shape[1]
+    fetches = []
+    for number, (far, held) in enumerate(
+        (
+            (wq_far, wq_ref),
+            (q_up_far, q_up_ref),
+            (kv_up_far, kv_up_ref),
+            (shrink_o_far, shrink_o_ref),
+            (wo_far, out_table.at[pl.ds(0, depth)]),
+            (expand_far, out_table.at[pl.ds(depth, expand_far.shape[0])]),
+        )
+    ):
+        fetch = pltpu.make_async_copy(far, held, fetch_sem.at[number])
+        fetch.start()
+        fetches.append(fetch)
     rows_ref[me] = normalize(tokens_ref[...].astype(jnp.float32), gain_ref[...]).astype(
         rows_ref.dtype
     )
@@ -377,48 +430,318 @@
     def close_extras():
         for copy in state["far"]:
             copy.wait_recv()
-        both = factors_ref.at[:, pl.ds(4 * across + 2 * core, 2)]
+        both = factors_ref.at[:, pl.ds(4 * opposite + 2 * core, 2)]
         state["shared"].append(copies.go(both, both, "tensor", side))
         state["kv"][2].wait_recv()
         state["kv"][3].wait_recv()
         whole = kv(y + 2)
         state["shared"].append(copies.go(whole, whole, "tensor", side))
 
+    f32, bf16 = jnp.float32, jnp.bfloat16
+    head = z
+    requests = lens_ref.shape[1]
+    adapters = slots_ref.shape[1]
+    width = rows_ref.shape[-1]
+    total = rows_ref.shape[0] * rows_ref.shape[1]
+    half = depth // 2
+    lane = lax.broadcasted_iota(jnp.int32, (1, depth), 1)
+    low = lane < half
+    total_rank = q_up_ref.shape[0]
+    rank_lane = lax.div(
+        lax.broadcasted_iota(jnp.int32, (1, total_rank), 1), total_rank // adapters
+    ).astype(f32)
+
+    def build_tables():
+        down_ = lax.broadcasted_iota(jnp.int32, (requests, requests), 0)
+        over = lax.broadcasted_iota(jnp.int32, (requests, requests), 1)
+
+        def column(row, number):
+            p = lax.broadcasted_iota(jnp.int32, (number, number), 0)
+            q = lax.broadcasted_iota(jnp.int32, (number, number), 1)
+            return jnp.sum(
+                jnp.where(p == q, jnp.broadcast_to(row, (number, number)), 0.0),
+                axis=1,
+                keepdims=True,
+            )
+
+        lens = lens_ref[...].astype(f32)
+        groups = groups_ref[...].astype(f32)
+        slots = column(slots_ref[...].astype(f32), adapters)
+        ends = jnp.sum(jnp.where(down_ <= over, column(lens, requests), 0.0), axis=0, keepdims=True)
+        starts = ends - lens
+        same = column(groups, requests) == groups
+        firsts = jnp.min(jnp.where(same, column(starts, requests), 1e9), axis=0, keepdims=True)
+        which = lax.broadcasted_iota(jnp.int32, (adapters, requests), 0)
+        slot = jnp.sum(jnp.where(which == adapters_ref[...], slots, 0.0), axis=0, keepdims=True)
+        tab[0:1, :] = starts
+        tab[1:2, :] = ends
+        tab[2:3, :] = firsts
+        tab[3:4, :] = slot
+
+    def look_up(row, which):
+        row_f = row.astype(f32)
+        inside = (row_f >= tab[0:1, :]) & (row_f < tab[1:2, :])
+        return jnp.sum(jnp.where(inside, tab[which : which + 1, :], 0.0), axis=1, keepdims=True)
+
+    def natural(first, count):
+        return first + lax.broadcasted_iota(jnp.int32, (count, 1), 0)
+
+    def turns(first, count):
+        freq = jnp.exp(
+            -jnp.where(low, lane, lane - half).astype(f32) * (2.0 * math.log(ROPE_BASE) / depth)
+        )
+
+        def some(number, carry):
+            begin = pl.multiple_of(first + number * PAGE, PAGE)
+            row = natural(begin, PAGE)
+            rope = row.astype(f32) - look_up(row, 2)
+            trig[pl.ds(begin, PAGE), :] = jnp.sin(
+                rope * freq + jnp.where(low, 0.5 * math.pi, 0.0)
+            )
+            return carry
+
+        lax.fori_loop(0, count // PAGE, some, jnp.int32(0))
+
+    def unit(vector, norm_ref):
+        return (
+            vector
+            * lax.rsqrt(jnp.mean(vector * vector, axis=-1, keepdims=True) + NORM_EPS)
+            * norm_ref[...].astype(f32)
+        )
+
+    columns = across.shape[0]
+
+    def project(cells):
+        pair = 2 * rows_ref.shape[1]
+        bases = [
+            pl.multiple_of(spot(z + i, y + j, 0) * rows_ref.shape[1], pair) for i, j in cells
+        ]
+        x = jnp.concatenate(
+            [rows_ref[pl.ds(spot(z + i, y + j, 0), 2)].reshape(pair, width) for i, j in cells],
+            axis=0,
+        )
+        slot = jnp.concatenate([look_up(natural(base, pair), 3) for base in bases], axis=0)
+        mixed_trig = jnp.concatenate([trig[pl.ds(base, pair), :] for base in bases], axis=0)
+        other_trig = pltpu.roll(mixed_trig, half, 1)
+        cosine = jnp.where(low, mixed_trig, other_trig)
+        sine = jnp.where(low, -other_trig, mixed_trig)
+
+        def turn(vector):
+            return vector * cosine + pltpu.roll(vector, half, 1) * sine
+
+        mine = slot == rank_lane
+        projected = lax.dot_general(
+            x, factors_ref[...].reshape(3 * total_rank, width), TRANSPOSED, preferred_element_type=f32
+        )
+        lora = []
+        for part in range(3):
+            shrunk = projected[:, part * total_rank : (part + 1) * total_rank]
+            placed = jnp.where(mine, shrunk, 0.0).astype(bf16)
+            if part == 0:
+                up_table = q_up_ref[...]
+            else:
+                begin = pl.multiple_of(head * 2 * depth + (part - 1) * depth, depth)
+                up_table = kv_up_ref[:, pl.ds(begin, depth)]
+            lora.append(
+                ADAPTER_FACTOR * jnp.dot(placed, up_table, preferred_element_type=f32)
+            )
+        query = jnp.dot(x, wq_ref[...], preferred_element_type=f32) + lora[0]
+        query = turn(unit(query, q_gain_ref)).astype(bf16)
+        both = lax.dot_general(x, wkv_held[...], TRANSPOSED, preferred_element_type=f32)
+        raw = (both[:, :depth] + lora[1]).astype(bf16).astype(f32)
+        key = turn(unit(raw, k_gain_ref)).astype(bf16)
+        value = (both[:, depth:] + lora[2]).astype(bf16)
+        offset = lax.rem(me, 8) * columns
+        pick_row = lax.broadcasted_iota(jnp.int32, (columns, 2 * depth), 0) + offset
+        pick_lane = lax.broadcasted_iota(jnp.int32, (columns, 2 * depth), 1)
+        pick = jnp.where(pick_row == pick_lane, 1.0, 0.0).astype(bf16)
+        turned = lax.dot_general(
+            pick, jnp.concatenate([key, value], axis=1), TRANSPOSED, preferred_element_type=f32
+        )
+        for number, base in enumerate(bases):
+            here = slice(number * pair, (number + 1) * pair)
+            queries[pl.ds(base, pair), :] = query[here]
+            keys[pl.ds(base, pair), :] = key[here]
+            values[pl.ds(base, pair), 0:depth] = value[here]
+            across[:, pl.ds(base, pair)] = turned[:, here]
+
+    def opened(ready):
+        kv_extras(ready)
+        build_tables()
+        turns(0, 512)
+
+    def early(ready):
+        turns(512, 512)
+
+    def third(ready):
+        factor_extras(ready)
+        turns(1024, 512)
+        turns(1536, 512)
+        values[:, depth:] = jnp.broadcast_to(
+            jnp.where(lane == 0, 1.0, 0.0), (total, depth)
+        ).astype(bf16)
+        across[:, total:] = jnp.zeros((columns, across.shape[1] - total), f32)
+
+    def middle(ready):
+        close_extras()
+        for copy in state["shared"]:
+            copy.wait_recv()
+        for home in homes[:4]:
+            home.wait()
+        for fetch in fetches:
+            fetch.wait()
+        wkv_held[...] = (
+            wkv_all_ref[...].astype(f32).reshape(wkv_held.shape).astype(bf16)
+        )
+        ready(EARLY)
+        project(EARLY)
+
+    def last(ready):
+        ready(EARLY + MIDDLE)
+        project(MIDDLE)
+
     open_extras()
     gather_rows(
-        rows_ref, z, y, core, copies, {"opened": kv_extras, "third": factor_extras}
+        rows_ref,
+        z,
+        y,
+        core,
+        copies,
+        {"opened": opened, "early": early, "third": third, "middle": middle, "last": last},
     )
-    close_extras()
-    for copy in state["shared"]:
-        copy.wait_recv()
-    for home in homes[:4]:
-        home.wait()
+    project(LAST)
+
+    gap = lax.broadcasted_iota(jnp.int32, (BLOCK, KEY_BLOCK), 0) - lax.broadcasted_iota(
+        jnp.int32, (BLOCK, KEY_BLOCK), 1
+    )
+    scale = depth**-0.5
+
+    def store(step):
+        return pltpu.make_async_copy(
+            stage.at[step],
+            terms_ref.at[pl.ds(pl.multiple_of(step * BLOCK, BLOCK), BLOCK)],
+            store_sem.at[step],
+        )
+
+    def attend(step, carry):
+        first_row = pl.multiple_of(step * BLOCK, BLOCK)
+        row = natural(first_row, BLOCK)
+        reach = (row.astype(f32) - look_up(row, 2)).astype(jnp.int32)
+        mine = look_up(row, 3) == rank_lane
+        query = queries[pl.ds(first_row, BLOCK), :]
+        acc[...] = jnp.zeros_like(acc)
+
+        def over_keys(number, carry):
+            begin = pl.multiple_of(number * KEY_BLOCK, KEY_BLOCK)
+            scores = lax.dot_general(
+                query, keys[pl.ds(begin, KEY_BLOCK), :], TRANSPOSED, preferred_element_type=f32
+            )
+            behind = gap + (first_row - begin)
+            raised = jnp.where((behind >= 0) & (behind <= reach), jnp.exp(scores * scale), 0.0)
+            acc[...] += jnp.dot(
+                raised.astype(bf16), values[pl.ds(begin, KEY_BLOCK), :], preferred_element_type=f32
+            )
+            return carry
+
+        lax.fori_loop(0, (step + 1) * (BLOCK // KEY_BLOCK), over_keys, jnp.int32(0))
+        mixed = (acc[:, :depth] / acc[:, depth : depth + 1]).astype(bf16)
+        shrunk = lax.dot_general(mixed, shrink_o_ref[...], TRANSPOSED, preferred_element_type=f32)
+        placed = jnp.where(mine, ADAPTER_FACTOR * shrunk, 0.0).astype(bf16)
+        joined = jnp.concatenate([mixed, placed], axis=1)
+        for begin in range(0, width, 512):
+            stage[step, :, begin : begin + 512] = jnp.dot(
+                joined, out_table[:, begin : begin + 512], preferred_element_type=f32
+            ).astype(bf16)
+        store(step).start()
+        return carry
+
+    lax.fori_loop(0, total // BLOCK, attend, jnp.int32(0))
+    for step in range(total // BLOCK):
+        store(step).wait()
     copies.settle()
     assert copies.n == GATHER_COPIES + EXTRA_COPIES, copies.n
 
 
-def enter(tokens, gain, shrink, wkv):
+def pages_kernel(lens_s, pages_s, across, pages_ref):
+    columns = pages_ref.shape[1]
+    spot_lane = lax.broadcasted_iota(jnp.int32, (columns, PAGE), 1)
+
+    def fill(number, start):
+        length = lens_s[0, number]
+        for part in range(2):
+            begin = start + part * PAGE
+            aligned = pl.multiple_of(lax.div(begin, PAGE) * PAGE, PAGE)
+            window = across[:, pl.ds(aligned, 2 * PAGE)]
+            shift = lax.rem(2 * PAGE - (begin - aligned), 2 * PAGE)
+            rolled = pltpu.roll(window, shift, 1)[:, :PAGE]
+            kept = jnp.where(spot_lane < length - part * PAGE, rolled, 0.0)
+            pages_ref[pages_s[0, number * 2 + part]] = kept.astype(jnp.bfloat16)
+        return start + length
+
+    lax.fori_loop(0, lens_s.shape[1], fill, jnp.int32(0))
+
+
+BLOCK = 512
+KEY_BLOCK = 256
+TRANSPOSED = (((1,), (1,)), ((), ()))
+
+
+def front(
+    lengths,
+    groups,
+    adapter_of_request,
+    adapter_slot,
+    page_table,
+    q_gain,
+    k_gain,
+    gain,
+    tokens,
+    shrink,
+    wkv,
+    query_weight,
+    query_up,
+    kv_up,
+    w_o,
+    shrink_o,
+    expand_o,
+):
     rows, width = tokens.shape
+    total = 32 * rows
+    depth = query_weight.shape[1]
+    columns = kv_up.shape[1] // 32
+    pages = page_table.shape[1]
     count = GATHER_COPIES + EXTRA_COPIES
-    return pl.pallas_call(
-        enter_kernel,
+    vmem = pl.BlockSpec(memory_space=pltpu.VMEM)
+    smem = pl.BlockSpec(memory_space=pltpu.SMEM)
+    far = pl.BlockSpec(memory_space=pl.ANY)
+    bf16, f32 = jnp.bfloat16, jnp.float32
+    terms, across = pl.pallas_call(
+        front_kernel,
         out_shape=(
-            jax.ShapeDtypeStruct((32, rows, width), jnp.bfloat16),
-            jax.ShapeDtypeStruct((shrink.shape[1], 4 * shrink.shape[0]) + shrink.shape[2:], jnp.bfloat16),
-            jax.ShapeDtypeStruct((4, 4, 2) + wkv.shape[1:], jnp.bfloat16),
+            jax.ShapeDtypeStruct((total, width), bf16),
+            jax.ShapeDtypeStruct((columns, total + 4 * PAGE), f32),
         ),
-        in_specs=[
-            pl.BlockSpec(memory_space=pltpu.VMEM),
-            pl.BlockSpec(memory_space=pltpu.VMEM),
-            pl.BlockSpec(memory_space=pl.ANY),
-            pl.BlockSpec(memory_space=pl.ANY),
-        ],
-        out_specs=(
-            pl.BlockSpec(memory_space=pltpu.VMEM),
-            pl.BlockSpec(memory_space=pltpu.VMEM),
-            pl.BlockSpec(memory_space=pltpu.VMEM),
-        ),
+        in_specs=[vmem] * 8 + [far] * 8,
+        out_specs=(far, vmem),
         scratch_shapes=[
+            pltpu.VMEM((32, rows, width), bf16),
+            pltpu.VMEM((shrink.shape[1], 4 * shrink.shape[0]) + shrink.shape[2:], bf16),
+            pltpu.VMEM((4, 4, 2) + wkv.shape[1:], bf16),
+            pltpu.VMEM((2 * depth, width), bf16),
+            pltpu.VMEM(query_weight.shape, bf16),
+            pltpu.VMEM(query_up.shape, bf16),
+            pltpu.VMEM(kv_up.shape, bf16),
+            pltpu.VMEM((w_o.shape[0] + expand_o.shape[0], width), bf16),
+            pltpu.VMEM(shrink_o.shape, bf16),
+            pltpu.VMEM((8, lengths.shape[1]), f32),
+            pltpu.VMEM((total, depth), f32),
+            pltpu.VMEM((total, depth), bf16),
+            pltpu.VMEM((total, depth), bf16),
+            pltpu.VMEM((total, 2 * depth), bf16),
+            pltpu.VMEM((BLOCK, 2 * depth), f32),
+            pltpu.VMEM((total // BLOCK, BLOCK, width), bf16),
+            pltpu.SemaphoreType.DMA((6,)),
+            pltpu.SemaphoreType.DMA((total // BLOCK,)),
             pltpu.SemaphoreType.DMA((5,)),
             pltpu.SemaphoreType.DMA((count,)),
             pltpu.SemaphoreType.DMA((count,)),
@@ -426,7 +749,32 @@
         compiler_params=pltpu.CompilerParams(
             collective_id=0, has_side_effects=True, vmem_limit_bytes=VMEM_LIMIT
         ),
-    )(tokens, gain.reshape(1, width), shrink, wkv)
+    )(
+        lengths,
+        groups,
+        adapter_of_request,
+        adapter_slot.reshape(1, -1),
+        q_gain.reshape(1, depth),
+        k_gain.reshape(1, depth),
+        gain.reshape(1, width),
+        tokens,
+        shrink,
+        wkv,
+        query_weight,
+        query_up,
+        kv_up,
+        w_o,
+        shrink_o,
+        expand_o,
+    )
+    kv_pages = pl.pallas_call(
+        pages_kernel,
+        out_shape=jax.ShapeDtypeStruct((pages, columns, PAGE), bf16),
+        in_specs=[smem, smem, vmem],
+        out_specs=vmem,
+        compiler_params=pltpu.CompilerParams(vmem_limit_bytes=VMEM_LIMIT),
+    )(lengths, page_table, across)
+    return terms, kv_pages
 
 
 def late_kernel(
@@ -530,21 +878,23 @@
             )
         blocks = slice(2 * first, 2 * (first + len(cells)))
         count = 2 * len(cells)
-        for expert in range(experts):
-            here = slice(expert * CAP_DEV, (expert + 1) * CAP_DEV)
+
+        def one_expert(expert, carry):
+            here = pl.ds(pl.multiple_of(expert * CAP_DEV, CAP_DEV), CAP_DEV)
             taken_rows = slots[blocks, here, :].reshape(count * CAP_DEV, width)
             gated = lax.dot_general(
-                taken_rows, gate[expert], (((1,), (1,)), ((), ())), preferred_element_type=f32
+                taken_rows, gate[expert], TRANSPOSED, preferred_element_type=f32
             )
-            raised = lax.dot_general(
-                taken_rows, up[expert], (((1,), (1,)), ((), ())), preferred_element_type=f32
-            )
+            raised = lax.dot_general(taken_rows, up[expert], TRANSPOSED, preferred_element_type=f32)
             hidden = (gated / (1.0 + jnp.exp(-gated)) * raised).astype(bf16)
             for begin in range(0, width, 512):
                 piece = jnp.dot(
                     hidden, down[expert, :, begin : begin + 512], preferred_element_type=f32
                 ).astype(bf16)
                 slots[blocks, here, begin : begin + 512] = piece.reshape(count, CAP_DEV, 512)
+            return carry
+
+        lax.fori_loop(0, experts, one_expert, jnp.int32(0))
 
     def early_experts(ready):
         for fetch in fetches:
@@ -628,268 +978,6 @@
     )(terms, tokens, gain.reshape(1, width), ids, gates, w_gate, w_up, w_down)
 
 
-BLOCK = 512
-KEY_BLOCK = 256
-TRANSPOSED = (((1,), (1,)), ((), ()))
-
-
-def heart_kernel(
-    lens_s,
-    groups_s,
-    pages_s,
-    lens_ref,
-    groups_ref,
-    adapters_ref,
-    slots_ref,
-    q_gain_ref,
-    k_gain_ref,
-    x_ref,
-    factors_ref,
-    wkv_ref,
-    wq_ref,
-    q_up_ref,
-    kv_up_ref,
-    wo_ref,
-    shrink_o_ref,
-    expand_ref,
-    out_ref,
-    pages_ref,
-    tab,
-    keys,
-    values,
-    across,
-    acc,
-):
-    step = pl.program_id(0)
-    place = lax.axis_index("tensor")
-    head = lax.div(place, 8)
-    f32, bf16 = jnp.float32, jnp.bfloat16
-    requests = lens_ref.shape[1]
-    adapters = slots_ref.shape[1]
-    depth = wq_ref.shape[1]
-
-    @pl.when(step == 0)
-    def _():
-        down = lax.broadcasted_iota(jnp.int32, (requests, requests), 0)
-        over = lax.broadcasted_iota(jnp.int32, (requests, requests), 1)
-
-        def column(row, number):
-            a = lax.broadcasted_iota(jnp.int32, (number, number), 0)
-            b = lax.broadcasted_iota(jnp.int32, (number, number), 1)
-            return jnp.sum(
-                jnp.where(a == b, jnp.broadcast_to(row, (number, number)), 0.0),
-                axis=1,
-                keepdims=True,
-            )
-
-        lens = lens_ref[...].astype(f32)
-        groups = groups_ref[...].astype(f32)
-        chosen = adapters_ref[...]
-        slots = column(slots_ref[...].astype(f32), adapters)
-        ends = jnp.sum(jnp.where(down <= over, column(lens, requests), 0.0), axis=0, keepdims=True)
-        starts = ends - lens
-        same = column(groups, requests) == groups
-        firsts = jnp.min(
-            jnp.where(same, column(starts, requests), 1e9), axis=0, keepdims=True
-        )
-        which = lax.broadcasted_iota(jnp.int32, (adapters, requests), 0)
-        slot = jnp.sum(jnp.where(which == chosen, slots, 0.0), axis=0, keepdims=True)
-        tab[0:1, :] = starts
-        tab[1:2, :] = ends
-        tab[2:3, :] = firsts
-        tab[3:4, :] = slot
-
-    first_row = step * BLOCK
-    row = first_row + lax.broadcasted_iota(jnp.int32, (BLOCK, 1), 0)
-    row_f = row.astype(f32)
-    inside = (row_f >= tab[0:1, :]) & (row_f < tab[1:2, :])
-    rope = row_f - jnp.sum(jnp.where(inside, tab[2:3, :], 0.0), axis=1, keepdims=True)
-    slot = jnp.sum(jnp.where(inside, tab[3:4, :], 0.0), axis=1, keepdims=True).astype(jnp.int32)
-
-    lane = lax.broadcasted_iota(jnp.int32, (1, depth), 1)
-    half = depth // 2
-    low = lane < half
-    freq = jnp.exp(
-        -jnp.where(low, lane, lane - half).astype(f32) * (2.0 * math.log(ROPE_BASE) / depth)
-    )
-    mixed_trig = jnp.sin(rope * freq + jnp.where(low, 0.5 * math.pi, 0.0))
-    other_trig = pltpu.roll(mixed_trig, half, 1)
-    cosine = jnp.where(low, mixed_trig, other_trig)
-    sine = jnp.where(low, -other_trig, mixed_trig)
-
-    def turn(vector):
-        return vector * cosine + pltpu.roll(vector, half, 1) * sine
-
-    def unit(vector, gain_ref):
-        return (
-            vector
-            * lax.rsqrt(jnp.mean(vector * vector, axis=-1, keepdims=True) + NORM_EPS)
-            * gain_ref[...].astype(f32)
-        )
-
-    total_rank = q_up_ref.shape[0]
-    rank = total_rank // adapters
-    mine = slot == lax.div(lax.broadcasted_iota(jnp.int32, (1, adapters * rank), 1), rank)
-    x = x_ref[...]
-    lora = []
-    projected = lax.dot_general(x, factors_ref[...], TRANSPOSED, preferred_element_type=f32)
-    for part in range(3):
-        shrunk = projected[:, part * total_rank : (part + 1) * total_rank]
-        placed = jnp.where(mine, shrunk, 0.0).astype(bf16)
-        if part == 0:
-            up = q_up_ref[...]
-        else:
-            begin = pl.multiple_of(head * 2 * depth + (part - 1) * depth, depth)
-            up = kv_up_ref[:, pl.ds(begin, depth)]
-        lora.append(ADAPTER_FACTOR * jnp.dot(placed, up, preferred_element_type=f32))
-    query = jnp.dot(x, wq_ref[...], preferred_element_type=f32) + lora[0]
-    query = turn(unit(query, q_gain_ref)).astype(bf16)
-    kv = lax.dot_general(x, wkv_ref[...], TRANSPOSED, preferred_element_type=f32)
-    raw = (kv[:, :depth] + lora[1]).astype(bf16).astype(f32)
-    key = turn(unit(raw, k_gain_ref)).astype(bf16)
-    value = (kv[:, depth:] + lora[2]).astype(bf16)
-    keys[pl.ds(first_row, BLOCK), :] = key
-    values[pl.ds(first_row, BLOCK), 0:depth] = value
-    values[pl.ds(first_row, BLOCK), depth:] = jnp.broadcast_to(
-        jnp.where(lane == 0, 1.0, 0.0), (BLOCK, depth)
-    ).astype(bf16)
-
-    columns = pages_ref.shape[1]
-    offset = lax.rem(place, 8) * columns
-    pick_row = lax.broadcasted_iota(jnp.int32, (columns, 2 * depth), 0) + offset
-    pick_lane = lax.broadcasted_iota(jnp.int32, (columns, 2 * depth), 1)
-    pick = jnp.where(pick_row == pick_lane, 1.0, 0.0).astype(bf16)
-    across[:, pl.ds(pl.multiple_of(first_row, BLOCK), BLOCK)] = lax.dot_general(
-        pick, jnp.concatenate([key, value], axis=1), TRANSPOSED, preferred_element_type=f32
-    )
-
-    def look(number, carry):
-        start, lead, found, before = carry
-        group = groups_s[0, number]
-        lead = jnp.where(group == before, lead, start)
-        found = jnp.where(start <= first_row, lead, found)
-        return start + lens_s[0, number], lead, found, group
-
-    zero = jnp.int32(0)
-    found = lax.fori_loop(0, requests, look, (zero, zero, zero, jnp.int32(-1)))[2]
-    acc[...] = jnp.zeros_like(acc)
-    gap = lax.broadcasted_iota(jnp.int32, (BLOCK, KEY_BLOCK), 0) - lax.broadcasted_iota(
-        jnp.int32, (BLOCK, KEY_BLOCK), 1
-    )
-    reach = rope.astype(jnp.int32)
-    scale = depth**-0.5
-
-    def over_keys(number, carry):
-        begin = pl.multiple_of(number * KEY_BLOCK, KEY_BLOCK)
-        scores = lax.dot_general(
-            query, keys[pl.ds(begin, KEY_BLOCK), :], TRANSPOSED, preferred_element_type=f32
-        )
-        behind = gap + (first_row - begin)
-        raised = jnp.where((behind >= 0) & (behind <= reach), jnp.exp(scores * scale), 0.0)
-        acc[...] += jnp.dot(
-            raised.astype(bf16), values[pl.ds(begin, KEY_BLOCK), :], preferred_element_type=f32
-        )
-        return carry
-
-    lax.fori_loop(
-        lax.div(found, KEY_BLOCK), (step + 1) * (BLOCK // KEY_BLOCK), over_keys, jnp.int32(0)
-    )
-    mixed = (acc[:, :depth] / acc[:, depth : depth + 1]).astype(bf16)
-    shrunk = lax.dot_general(mixed, shrink_o_ref[...], TRANSPOSED, preferred_element_type=f32)
-    placed = jnp.where(mine, ADAPTER_FACTOR * shrunk, 0.0).astype(bf16)
-    width = out_ref.shape[-1]
-    for begin in range(0, width, 512):
-        term = jnp.dot(mixed, wo_ref[:, begin : begin + 512], preferred_element_type=f32)
-        term = term + jnp.dot(
-            placed, expand_ref[:, begin : begin + 512], preferred_element_type=f32
-        )
-        out_ref[:, begin : begin + 512] = term.astype(bf16)
-
-    @pl.when(step == pl.num_programs(0) - 1)
-    def _():
-        spot_lane = lax.broadcasted_iota(jnp.int32, (columns, PAGE), 1)
-
-        def fill(number, start):
-            length = lens_s[0, number]
-            for part in range(2):
-                begin = start + part * PAGE
-                aligned = pl.multiple_of(lax.div(begin, PAGE) * PAGE, PAGE)
-                window = across[:, pl.ds(aligned, 2 * PAGE)]
-                shift = lax.rem(2 * PAGE - (begin - aligned), 2 * PAGE)
-                rolled = pltpu.roll(window, shift, 1)[:, :PAGE]
-                kept = jnp.where(spot_lane < length - part * PAGE, rolled, 0.0)
-                pages_ref[pages_s[0, number * 2 + part]] = kept.astype(bf16)
-            return start + length
-
-        lax.fori_loop(0, requests, fill, zero)
-
-
-def heart(
-    lengths,
-    groups,
-    adapter_of_request,
-    adapter_slot,
-    page_table,
-    q_gain,
-    k_gain,
-    x,
-    factors,
-    wkv,
-    query_weight,
-    query_up,
-    kv_up,
-    w_o,
-    shrink_o,
-    expand_o,
-):
-    total, width = x.shape
-    depth = query_weight.shape[1]
-    requests = lengths.shape[1]
-    pages = page_table.shape[1]
-    columns = 2 * kv_up.shape[1] // 64
-    slots = adapter_slot.shape[0]
-    smem = pl.BlockSpec(memory_space=pltpu.SMEM)
-
-    def whole(array):
-        return pl.BlockSpec(
-            array.shape, lambda i: (0,) * array.ndim, pipeline_mode=pl.Buffered(1)
-        )
-
-    small = (
-        lengths,
-        groups,
-        adapter_of_request,
-        adapter_slot.reshape(1, slots),
-        q_gain.reshape(1, depth),
-        k_gain.reshape(1, depth),
-    )
-    tables = (factors, wkv, query_weight, query_up, kv_up, w_o, shrink_o, expand_o)
-    return pl.pallas_call(
-        heart_kernel,
-        grid=(total // BLOCK,),
-        out_shape=(
-            jax.ShapeDtypeStruct((total, width), jnp.bfloat16),
-            jax.ShapeDtypeStruct((pages, columns, PAGE), jnp.bfloat16),
-        ),
-        in_specs=[smem, smem, smem]
-        + [whole(array) for array in small]
-        + [pl.BlockSpec((BLOCK, width), lambda i: (i, 0))]
-        + [whole(array) for array in tables],
-        out_specs=(
-            pl.BlockSpec((BLOCK, width), lambda i: (i, 0)),
-            pl.BlockSpec((pages, columns, PAGE), lambda i: (0, 0, 0)),
-        ),
-        scratch_shapes=[
-            pltpu.VMEM((8, requests), jnp.float32),
-            pltpu.VMEM((total, depth), jnp.bfloat16),
-            pltpu.VMEM((total, 2 * depth), jnp.bfloat16),
-            pltpu.VMEM((columns, total + 4 * PAGE), jnp.float32),
-            pltpu.VMEM((BLOCK, 2 * depth), jnp.float32),
-        ],
-        compiler_params=pltpu.CompilerParams(vmem_limit_bytes=VMEM_LIMIT),
-    )(lengths, groups, page_table, *small, x, *tables)
-
-
 def local(
     tokens,
     attn_gain,
@@ -920,14 +1008,7 @@
     own_rows, width = tokens.shape
     grand_total = own_rows * parts
     adapters, rank, kv_width = key_value_up_factors.shape
-    x_rows, factors, wkv_all = enter(
-        tokens,
-        attn_gain,
-        shrink_qkv.reshape(-1, 3, rank, width),
-        w_kv.transpose(1, 0, 2),
-    )
-    head_width = 2 * q_gain.shape[0]
-    attn_terms, kv_pages = heart(
+    attn_terms, kv_pages = front(
         lengths,
         groups,
         adapter_of_request,
@@ -935,9 +1016,10 @@
         page_table,
         q_gain,
         k_gain,
-        x_rows.reshape(grand_total, width),
-        factors.reshape(-1, width),
-        wkv_all.reshape(head_width, width),
+        attn_gain,
+        tokens,
+        shrink_qkv.reshape(-1, 3, rank, width),
+        w_kv.transpose(1, 0, 2),
         query_weight,
         query_up_factors.reshape(adapters * rank, -1),
         key_value_up_factors.reshape(adapters * rank, kv_width),

time: 196 us -> 189 us (0.964)
  Pallas kernels: 188 us -> 181 us
    pallas_call x2, Pallas kernels: 86.2 us -> 78.3 us  [the longest x1 73.9 us: front(): pl.pallas_call(front_kernel, out_shape=(jax.ShapeDtypeStruct((total, widt...]
    unnamed x5 -> x3, local copies, waits for them, and re-layouts: 4.98 us -> 4.97 us
where the time goes in v6:
time: 189 us
  Pallas kernels  181 us (96%)
  local copies, waits for them, and re-layouts  7.55 us (4%)
    pallas_call x1, Pallas kernels, late(): pl.pallas_call(late_kernel, out_shape=(jax.ShapeDtypeStruct((rows, width)...  102 us
    pallas_call x1, Pallas kernels, front(): pl.pallas_call(front_kernel, out_shape=(jax.ShapeDtypeStruct((total, widt...  73.9 us
    unnamed x3, local copies, waits for them, and re-layouts  4.97 us
    pallas_call x1, Pallas kernels, front(): pl.pallas_call(pages_kernel, out_shape=jax.ShapeDtypeStruct((pages, colum...  4.4 us

profile of v6, /device:TPU:1, one launch (start us, length us, event | category | flops | bytes accessed | tf_op | source)
XLA Modules:
  0.0 188.9 jit_solution(5509385036609959501)
XLA Ops:
  0.6 1.3 reshape.42.gain_ref
  1.9 1.3 reshape.49.gain_ref
  3.2 1.6 copy.28
  4.8 73.9 %shard_map.238 = (bf16[2048,2048]{1,0:T(8,128)(2,1)}, f32[32,2560]{1,0:T(8,128)}) custom-call(s32[1,32]{1,0:T(1,128)} %lens_s.1, s32[1,32]{1,0:T(1,128)} %groups_ref.1, s32[1,32]{1,0:T(1,128)} %adapters_ref.1, s32[1,16]{1,0:T(1,128)} %bitcast.23, bf16[1,128]{1,0:T(2,128)(2,1)} %bitcast.24, bf16[1,128]{1,0:T(2,128)(2,1)} %bitcast.25, ...), custom_call_target="tpu_custom_call" | custom-call | tf_op jit(solution)/shard_map/pallas_call | solution.py:718
  78.8 102.4 %shard_map.239 = (bf16[64,2048]{1,0:T(8,128)(2,1)}, bf16[64,2048]{1,0:T(8,128)(2,1)}) custom-call(bf16[32,64,2048]{2,1,0:T(8,128)(2,1)} %bitcast.14, bf16[64,2048]{1,0:T(8,128)(2,1)} %tokens_ref.3, bf16[1,2048]{1,0:T(2,128)(2,1)} %reshape.49.gain_ref, s32[8,2048]{1,0:T(8,128)} %bitcast.21, f32[8,2048]{1,0:T(8,128)} %bitcast.22, ...), custom_call_target="tpu_custom_call" | custom-call | tf_op jit(solution)/shard_map/pallas_call | solution.py:955
  181.2 4.4 %shard_map.240 = bf16[64,32,128]{2,1,0:T(8,128)(2,1)} custom-call(s32[1,32]{1,0:T(1,128)} %lens_s.1, s32[1,64]{1,0:T(1,128)} %pages_s.1, f32[32,2560]{1,0:T(8,128)} %get-tuple-element.10.across), custom_call_target="tpu_custom_call" | custom-call | tf_op jit(solution)/shard_map/pallas_call | solution.py:770
  185.6 1.7 copy.31
  187.3 1.7 copy.32

commit v7 on v6

--- a/solution.py
+++ b/solution.py
@@ -45,6 +45,9 @@
 MIDDLE = ((2, 0), (0, 2), (3, 3), (3, 1), (1, 3), (1, 1))
 LAST = ((3, 2), (2, 3), (2, 1), (1, 2), (2, 2))
 CELLS = EARLY + MIDDLE + LAST
+FAR = ((2, 2), (2, 1), (1, 2), (2, 3), (3, 2), (2, 0), (0, 2))
+NEAR = ((1, 1), (3, 1), (1, 3), (3, 3))
+SLOT_CELLS = EARLY + FAR + NEAR
 
 
 def gather_rows(out, z, y, core, copies, hooks):
@@ -115,6 +118,7 @@
         p.u[3].wait_recv()
         share(p.at(2, 0), p.row, HALF, p.number, 2, 0)
         p.v[2] = ring_open(p, False, 2)
+    hook("wide")
     for off in (3, 1):
         for which in range(2):
             for p in parts:
@@ -126,6 +130,7 @@
             share(p.at(done, 2), p.row, HALF, p.number, done, 2)
         if off == 3:
             hook("third")
+    hook("fourth")
     for which in range(2):
         for p in parts:
             p.v[2].append(ring_pass(p, False, 2, p.v[2], which))
@@ -155,7 +160,9 @@
     return (v, u) if number == 0 else (u, v)
 
 
-def scatter_rows(acc, sib, landed, z, y, core, copies, result, ensure, arrived):
+def scatter_rows(
+    acc, sib, landed, z, y, core, copies, result, ensure, arrived, between=lambda: None
+):
     def neighbour(number, along_v, step):
         along_z = (number == 0) == along_v
         return spot(z + step, y, core) if along_z else spot(z, y + step, core)
@@ -181,18 +188,23 @@
         ring[number, u].append(
             copies.go(block.at[pl.ds(row, HALF)], b.at[pl.ds(32 + 32 * which, HALF)], "tensor",
                       neighbour(number, along_v, (1, 3)[which])))
-    ensure([(2, u) for u in ORDER] + [(u, 2) for u in ORDER[1:]])
+    coming = [(2, 2)] + [where for u in ORDER[1:] for where in ((2, u), (u, 2))]
+    ensure(coming[:3])
     for u in ORDER:
         for number in range(2):
+            ensure(coming[: 2 * ORDER.index(u) + number + 3])
             block = own(number, 2, u)
             add_rows(block, number * HALF, HALF, [pair(number, 2, u)])
             far(number, True, u, block)
-    ensure([(i, j) for i in ORDER[1:] for j in ORDER[1:]])
+    ensure(coming)
+    between()
+    coming = [cell(number, v, u) for u in ORDER for number in range(2) for v in (1, 3)]
     for u in ORDER:
         for number in range(2):
             row = number * HALF
             for which in range(2):
                 v = (1, 3)[which]
+                ensure(coming[: 4 * ORDER.index(u) + 2 * number + which + 4])
                 block = own(number, v, u)
                 other, first = pair(number, v, u)
                 ring[number, u][which].wait_recv()
@@ -662,7 +674,9 @@
     assert copies.n == GATHER_COPIES + EXTRA_COPIES, copies.n
 
 
-def pages_kernel(lens_s, pages_s, across, pages_ref):
+def final_kernel(lens_s, pages_s, across, attn_ref, moe_ref, attn_out, moe_out, pages_ref):
+    attn_out[...] = attn_ref[...]
+    moe_out[...] = moe_ref[...]
     columns = pages_ref.shape[1]
     spot_lane = lax.broadcasted_iota(jnp.int32, (columns, PAGE), 1)
 
@@ -691,7 +705,6 @@
     groups,
     adapter_of_request,
     adapter_slot,
-    page_table,
     q_gain,
     k_gain,
     gain,
@@ -709,10 +722,8 @@
     total = 32 * rows
     depth = query_weight.shape[1]
     columns = kv_up.shape[1] // 32
-    pages = page_table.shape[1]
     count = GATHER_COPIES + EXTRA_COPIES
     vmem = pl.BlockSpec(memory_space=pltpu.VMEM)
-    smem = pl.BlockSpec(memory_space=pltpu.SMEM)
     far = pl.BlockSpec(memory_space=pl.ANY)
     bf16, f32 = jnp.bfloat16, jnp.float32
     terms, across = pl.pallas_call(
@@ -756,7 +767,7 @@
         adapter_slot.reshape(1, -1),
         q_gain.reshape(1, depth),
         k_gain.reshape(1, depth),
-        gain.reshape(1, width),
+        gain,
         tokens,
         shrink,
         wkv,
@@ -767,14 +778,24 @@
         shrink_o,
         expand_o,
     )
-    kv_pages = pl.pallas_call(
-        pages_kernel,
-        out_shape=jax.ShapeDtypeStruct((pages, columns, PAGE), bf16),
-        in_specs=[smem, smem, vmem],
-        out_specs=vmem,
+    return terms, across
+
+
+def final(lengths, page_table, across, attn, moe):
+    pages = page_table.shape[1]
+    vmem = pl.BlockSpec(memory_space=pltpu.VMEM)
+    smem = pl.BlockSpec(memory_space=pltpu.SMEM)
+    return pl.pallas_call(
+        final_kernel,
+        out_shape=(
+            jax.ShapeDtypeStruct(attn.shape, attn.dtype),
+            jax.ShapeDtypeStruct(moe.shape, moe.dtype),
+            jax.ShapeDtypeStruct((pages, across.shape[0], PAGE), jnp.bfloat16),
+        ),
+        in_specs=[smem, smem, vmem, vmem, vmem],
+        out_specs=(vmem, vmem, vmem),
         compiler_params=pltpu.CompilerParams(vmem_limit_bytes=VMEM_LIMIT),
-    )(lengths, page_table, across)
-    return terms, kv_pages
+    )(lengths, page_table, across, attn, moe)
 
 
 def late_kernel(
@@ -862,7 +883,7 @@
     lane_block = lax.div(lax.broadcasted_iota(jnp.int32, (1, pair_rows), 1), block)
 
     def apply_experts(cells):
-        first = CELLS.index(cells[0])
+        first = SLOT_CELLS.index(cells[0])
         for number, (i, j) in enumerate(cells):
             index = spot(z + i, y + j, 0)
             piece = pick[:, pl.ds(pl.multiple_of(index * block, pair_rows), pair_rows)]
@@ -902,15 +923,9 @@
         ready(EARLY)
         apply_experts(EARLY)
 
-    def middle_experts(ready):
-        ready(EARLY + MIDDLE)
-        apply_experts(MIDDLE)
-
-    gather_rows(
-        rows, z, y, core, copies, {"early": early_experts, "middle": middle_experts}
-    )
-    apply_experts(LAST)
+    gather_rows(rows, z, y, core, copies, {"wide": early_experts})
     copies.settle()
+    apply_experts(FAR)
 
     shared = {}
     waited = set()
@@ -918,7 +933,7 @@
     def combine(i, j, which):
         index = spot(z + i, y + j, which)
         part = mix[pl.ds(pl.multiple_of(index * block, block), block), :]
-        held = slots[2 * CELLS.index((i, j)) + which]
+        held = slots[2 * SLOT_CELLS.index((i, j)) + which]
         return jnp.dot(part, held, preferred_element_type=f32).astype(bf16)
 
     def make(cells):
@@ -936,7 +951,7 @@
             waited.add(where)
             shared[where].wait_recv()
 
-    scatter_rows(acc, sib, landed, z, y, core, copies, total, make, came)
+    scatter_rows(acc, sib, landed, z, y, core, copies, total, make, came, lambda: apply_experts(NEAR))
     moe_ref[...] = total[...].astype(moe_ref.dtype)
     copies.settle()
     assert copies.n == LATE_COPIES, copies.n
@@ -975,7 +990,7 @@
         compiler_params=pltpu.CompilerParams(
             collective_id=1, has_side_effects=True, vmem_limit_bytes=VMEM_LIMIT
         ),
-    )(terms, tokens, gain.reshape(1, width), ids, gates, w_gate, w_up, w_down)
+    )(terms, tokens, gain, ids, gates, w_gate, w_up, w_down)
 
 
 def local(
@@ -1008,12 +1023,11 @@
     own_rows, width = tokens.shape
     grand_total = own_rows * parts
     adapters, rank, kv_width = key_value_up_factors.shape
-    attn_terms, kv_pages = front(
+    attn_terms, across = front(
         lengths,
         groups,
         adapter_of_request,
         adapter_slot,
-        page_table,
         q_gain,
         k_gain,
         attn_gain,
@@ -1027,7 +1041,7 @@
         shrink_o.reshape(adapters * rank, -1),
         expand_o.reshape(adapters * rank, width),
     )
-    attn_out, moe_total = late(
+    attn, moe = late(
         attn_terms.reshape(parts, own_rows, width),
         tokens,
         moe_gain,
@@ -1037,7 +1051,7 @@
         w_up,
         w_down,
     )
-    return (attn_out, moe_total, kv_pages)
+    return tuple(final(lengths, page_table, across, attn, moe))
 
 
 def solution(mesh):

time: 189 us -> 188 us (level)
  local copies, waits for them, and re-layouts: 7.55 us -> 1.64 us
  Pallas kernels: 181 us -> 186 us
    pallas_call x1, Pallas kernels: 102 us -> 107 us  [late(): pl.pallas_call(late_kernel, out_shape=(jax.ShapeDtypeStruct((rows, width)...]
    unnamed x3 -> x1, local copies, waits for them, and re-layouts: 4.97 us -> 1.64 us
    reshape x2 -> x0, local copies, waits for them, and re-layouts: 2.58 us -> none  [the longest x1 1.29 us: front(): gain.reshape(1, width)]
where the time goes in v7:
time: 188 us
  Pallas kernels  186 us (99%)
    pallas_call x1, Pallas kernels, late(): pl.pallas_call(late_kernel, out_shape=(jax.ShapeDtypeStruct((rows, width)...  107 us
    pallas_call x1, Pallas kernels, front(): pl.pallas_call(front_kernel, out_shape=(jax.ShapeDtypeStruct((total, widt...  73.9 us
    pallas_call x1, Pallas kernels, final(): pl.pallas_call(final_kernel, out_shape=(jax.ShapeDtypeStruct(attn.shape,...  4.69 us

profile of v7, /device:TPU:1, one launch (start us, length us, event | category | flops | bytes accessed | tf_op | source)
XLA Modules:
  0.0 187.9 jit_solution(14282854999617796109)
XLA Ops:
  0.6 1.6 copy.28
  2.3 73.9 %shard_map.238 = (bf16[2048,2048]{1,0:T(8,128)(2,1)}, f32[32,2560]{1,0:T(8,128)}) custom-call(s32[1,32]{1,0:T(1,128)} %lens_s.1, s32[1,32]{1,0:T(1,128)} %groups_ref.1, s32[1,32]{1,0:T(1,128)} %adapters_ref.1, s32[1,16]{1,0:T(1,128)} %bitcast.23, bf16[1,128]{1,0:T(2,128)(2,1)} %bitcast.24, bf16[1,128]{1,0:T(2,128)(2,1)} %bitcast.25, ...), custom_call_target="tpu_custom_call" | custom-call | tf_op jit(solution)/shard_map/pallas_call | solution.py:729
  76.2 107.1 %shard_map.239 = (bf16[64,2048]{1,0:T(8,128)(2,1)}, bf16[64,2048]{1,0:T(8,128)(2,1)}) custom-call(bf16[32,64,2048]{2,1,0:T(8,128)(2,1)} %bitcast.14, bf16[64,2048]{1,0:T(8,128)(2,1)} %tokens_ref.3, bf16[2048]{0:T(1024)(128)(2,1)} %gain_ref.3, s32[8,2048]{1,0:T(8,128)} %bitcast.21, f32[8,2048]{1,0:T(8,128)} %bitcast.22, bf16[2,768,2048]{2,1,0:T(8,128)(2,1)} %w_gate_ref.1, ...), custom_call_target="tpu_custom_call" | custom-call | tf_op jit(solution)/shard_map/pallas_call | solution.py:970
  183.3 4.7 %shard_map.240 = (bf16[64,2048]{1,0:T(8,128)(2,1)}, bf16[64,2048]{1,0:T(8,128)(2,1)}, bf16[64,32,128]{2,1,0:T(8,128)(2,1)}) custom-call(s32[1,32]{1,0:T(1,128)} %lens_s.1, s32[1,64]{1,0:T(1,128)} %pages_s.1, f32[32,2560]{1,0:T(8,128)} %get-tuple-element.7.across, bf16[64,2048]{1,0:T(8,128)(2,1)} %get-tuple-element.9.attn_ref, ...), custom_call_target="tpu_custom_call" | custom-call | tf_op jit(solution)/shard_map/pallas_call | solution.py:788

commit v8 on v7

--- a/solution.py
+++ b/solution.py
@@ -45,9 +45,6 @@
 MIDDLE = ((2, 0), (0, 2), (3, 3), (3, 1), (1, 3), (1, 1))
 LAST = ((3, 2), (2, 3), (2, 1), (1, 2), (2, 2))
 CELLS = EARLY + MIDDLE + LAST
-FAR = ((2, 2), (2, 1), (1, 2), (2, 3), (3, 2), (2, 0), (0, 2))
-NEAR = ((1, 1), (3, 1), (1, 3), (3, 3))
-SLOT_CELLS = EARLY + FAR + NEAR
 
 
 def gather_rows(out, z, y, core, copies, hooks):
@@ -161,7 +158,7 @@
 
 
 def scatter_rows(
-    acc, sib, landed, z, y, core, copies, result, ensure, arrived, between=lambda: None
+    acc, sib, landed, z, y, core, copies, result, ensure, arrived
 ):
     def neighbour(number, along_v, step):
         along_z = (number == 0) == along_v
@@ -197,7 +194,6 @@
             add_rows(block, number * HALF, HALF, [pair(number, 2, u)])
             far(number, True, u, block)
     ensure(coming)
-    between()
     coming = [cell(number, v, u) for u in ORDER for number in range(2) for v in (1, 3)]
     for u in ORDER:
         for number in range(2):
@@ -696,7 +692,7 @@
 
 
 BLOCK = 512
-KEY_BLOCK = 256
+KEY_BLOCK = 512
 TRANSPOSED = (((1,), (1,)), ((), ()))
 
 
@@ -883,7 +879,7 @@
     lane_block = lax.div(lax.broadcasted_iota(jnp.int32, (1, pair_rows), 1), block)
 
     def apply_experts(cells):
-        first = SLOT_CELLS.index(cells[0])
+        first = CELLS.index(cells[0])
         for number, (i, j) in enumerate(cells):
             index = spot(z + i, y + j, 0)
             piece = pick[:, pl.ds(pl.multiple_of(index * block, pair_rows), pair_rows)]
@@ -900,8 +896,8 @@
         blocks = slice(2 * first, 2 * (first + len(cells)))
         count = 2 * len(cells)
 
-        def one_expert(expert, carry):
-            here = pl.ds(pl.multiple_of(expert * CAP_DEV, CAP_DEV), CAP_DEV)
+        def one_expert(expert):
+            here = slice(expert * CAP_DEV, (expert + 1) * CAP_DEV)
             taken_rows = slots[blocks, here, :].reshape(count * CAP_DEV, width)
             gated = lax.dot_general(
                 taken_rows, gate[expert], TRANSPOSED, preferred_element_type=f32
@@ -913,19 +909,15 @@
                     hidden, down[expert, :, begin : begin + 512], preferred_element_type=f32
                 ).astype(bf16)
                 slots[blocks, here, begin : begin + 512] = piece.reshape(count, CAP_DEV, 512)
-            return carry
-
-        lax.fori_loop(0, experts, one_expert, jnp.int32(0))
-
-    def early_experts(ready):
-        for fetch in fetches:
-            fetch.wait()
-        ready(EARLY)
-        apply_experts(EARLY)
-
-    gather_rows(rows, z, y, core, copies, {"wide": early_experts})
+
+        for expert in range(experts):
+            one_expert(expert)
+
+    gather_rows(rows, z, y, core, copies, {})
     copies.settle()
-    apply_experts(FAR)
+    for fetch in fetches:
+        fetch.wait()
+    apply_experts(CELLS)
 
     shared = {}
     waited = set()
@@ -933,7 +925,7 @@
     def combine(i, j, which):
         index = spot(z + i, y + j, which)
         part = mix[pl.ds(pl.multiple_of(index * block, block), block), :]
-        held = slots[2 * SLOT_CELLS.index((i, j)) + which]
+        held = slots[2 * CELLS.index((i, j)) + which]
         return jnp.dot(part, held, preferred_element_type=f32).astype(bf16)
 
     def make(cells):
@@ -951,7 +943,7 @@
             waited.add(where)
             shared[where].wait_recv()
 
-    scatter_rows(acc, sib, landed, z, y, core, copies, total, make, came, lambda: apply_experts(NEAR))
+    scatter_rows(acc, sib, landed, z, y, core, copies, total, make, came)
     moe_ref[...] = total[...].astype(moe_ref.dtype)
     copies.settle()
     assert copies.n == LATE_COPIES, copies.n

time: 188 us -> 181 us (0.963)
  Pallas kernels: 186 us -> 179 us
    pallas_call x1, Pallas kernels: 107 us -> 103 us  [late(): pl.pallas_call(late_kernel, out_shape=(jax.ShapeDtypeStruct((rows, width)...]
    pallas_call x1, Pallas kernels: 73.9 us -> 71 us  [front(): pl.pallas_call(front_kernel, out_shape=(jax.ShapeDtypeStruct((total, widt...]
where the time goes in v8:
time: 181 us
  Pallas kernels  179 us (99%)
    pallas_call x1, Pallas kernels, late(): pl.pallas_call(late_kernel, out_shape=(jax.ShapeDtypeStruct((rows, width)...  103 us
    pallas_call x1, Pallas kernels, front(): pl.pallas_call(front_kernel, out_shape=(jax.ShapeDtypeStruct((total, widt...  71 us
    pallas_call x1, Pallas kernels, final(): pl.pallas_call(final_kernel, out_shape=(jax.ShapeDtypeStruct(attn.shape,...  4.69 us

profile of v8, /device:TPU:1, one launch (start us, length us, event | category | flops | bytes accessed | tf_op | source)
XLA Modules:
  0.0 181.0 jit_solution(10091273522835821930)
XLA Ops:
  0.6 1.6 copy.28
  2.3 71.0 %shard_map.238 = (bf16[2048,2048]{1,0:T(8,128)(2,1)}, f32[32,2560]{1,0:T(8,128)}) custom-call(s32[1,32]{1,0:T(1,128)} %lens_s.1, s32[1,32]{1,0:T(1,128)} %groups_ref.1, s32[1,32]{1,0:T(1,128)} %adapters_ref.1, s32[1,16]{1,0:T(1,128)} %bitcast.23, bf16[1,128]{1,0:T(2,128)(2,1)} %bitcast.24, bf16[1,128]{1,0:T(2,128)(2,1)} %bitcast.25, ...), custom_call_target="tpu_custom_call" | custom-call | tf_op jit(solution)/shard_map/pallas_call | solution.py:725
  73.3 103.0 %shard_map.239 = (bf16[64,2048]{1,0:T(8,128)(2,1)}, bf16[64,2048]{1,0:T(8,128)(2,1)}) custom-call(bf16[32,64,2048]{2,1,0:T(8,128)(2,1)} %bitcast.14, bf16[64,2048]{1,0:T(8,128)(2,1)} %tokens_ref.3, bf16[2048]{0:T(1024)(128)(2,1)} %gain_ref.3, s32[8,2048]{1,0:T(8,128)} %bitcast.21, f32[8,2048]{1,0:T(8,128)} %bitcast.22, bf16[2,768,2048]{2,1,0:T(8,128)(2,1)} %w_gate_ref.1, ...), custom_call_target="tpu_custom_call" | custom-call | tf_op jit(solution)/shard_map/pallas_call | solution.py:962
  176.3 4.7 %shard_map.240 = (bf16[64,2048]{1,0:T(8,128)(2,1)}, bf16[64,2048]{1,0:T(8,128)(2,1)}, bf16[64,32,128]{2,1,0:T(8,128)(2,1)}) custom-call(s32[1,32]{1,0:T(1,128)} %lens_s.1, s32[1,64]{1,0:T(1,128)} %pages_s.1, f32[32,2560]{1,0:T(8,128)} %get-tuple-element.7.across, bf16[64,2048]{1,0:T(8,128)(2,1)} %get-tuple-element.9.attn_ref, ...), custom_call_target="tpu_custom_call" | custom-call | tf_op jit(solution)/shard_map/pallas_call | solution.py:784

commit v9 on v8

--- a/solution.py
+++ b/solution.py
@@ -186,10 +186,10 @@
             copies.go(block.at[pl.ds(row, HALF)], b.at[pl.ds(32 + 32 * which, HALF)], "tensor",
                       neighbour(number, along_v, (1, 3)[which])))
     coming = [(2, 2)] + [where for u in ORDER[1:] for where in ((2, u), (u, 2))]
-    ensure(coming[:3])
+    ensure(coming[:5])
     for u in ORDER:
         for number in range(2):
-            ensure(coming[: 2 * ORDER.index(u) + number + 3])
+            ensure(coming[: 2 * ORDER.index(u) + number + 5])
             block = own(number, 2, u)
             add_rows(block, number * HALF, HALF, [pair(number, 2, u)])
             far(number, True, u, block)

time: 181 us -> 182 us (level)
  no operation moved by 1% of the time
where the time goes in v9:
time: 182 us
  Pallas kernels  179 us (98%)
    pallas_call x1, Pallas kernels, late(): pl.pallas_call(late_kernel, out_shape=(jax.ShapeDtypeStruct((rows, width)...  104 us
    pallas_call x1, Pallas kernels, front(): pl.pallas_call(front_kernel, out_shape=(jax.ShapeDtypeStruct((total, widt...  71 us
    pallas_call x1, Pallas kernels, final(): pl.pallas_call(final_kernel, out_shape=(jax.ShapeDtypeStruct(attn.shape,...  4.69 us

profile of v9, /device:TPU:1, one launch (start us, length us, event | category | flops | bytes accessed | tf_op | source)
XLA Modules:
  0.0 181.7 jit_solution(3043977807038561843)
XLA Ops:
  0.6 1.6 copy.28
  2.3 71.0 %shard_map.238 = (bf16[2048,2048]{1,0:T(8,128)(2,1)}, f32[32,2560]{1,0:T(8,128)}) custom-call(s32[1,32]{1,0:T(1,128)} %lens_s.1, s32[1,32]{1,0:T(1,128)} %groups_ref.1, s32[1,32]{1,0:T(1,128)} %adapters_ref.1, s32[1,16]{1,0:T(1,128)} %bitcast.23, bf16[1,128]{1,0:T(2,128)(2,1)} %bitcast.24, bf16[1,128]{1,0:T(2,128)(2,1)} %bitcast.25, ...), custom_call_target="tpu_custom_call" | custom-call | tf_op jit(solution)/shard_map/pallas_call | solution.py:725
  73.3 103.7 %shard_map.239 = (bf16[64,2048]{1,0:T(8,128)(2,1)}, bf16[64,2048]{1,0:T(8,128)(2,1)}) custom-call(bf16[32,64,2048]{2,1,0:T(8,128)(2,1)} %bitcast.14, bf16[64,2048]{1,0:T(8,128)(2,1)} %tokens_ref.3, bf16[2048]{0:T(1024)(128)(2,1)} %gain_ref.3, s32[8,2048]{1,0:T(8,128)} %bitcast.21, f32[8,2048]{1,0:T(8,128)} %bitcast.22, bf16[2,768,2048]{2,1,0:T(8,128)(2,1)} %w_gate_ref.1, ...), custom_call_target="tpu_custom_call" | custom-call | tf_op jit(solution)/shard_map/pallas_call | solution.py:962
  177.0 4.7 %shard_map.240 = (bf16[64,2048]{1,0:T(8,128)(2,1)}, bf16[64,2048]{1,0:T(8,128)(2,1)}, bf16[64,32,128]{2,1,0:T(8,128)(2,1)}) custom-call(s32[1,32]{1,0:T(1,128)} %lens_s.1, s32[1,64]{1,0:T(1,128)} %pages_s.1, f32[32,2560]{1,0:T(8,128)} %get-tuple-element.7.across, bf16[64,2048]{1,0:T(8,128)(2,1)} %get-tuple-element.9.attn_ref, ...), custom_call_target="tpu_custom_call" | custom-call | tf_op jit(solution)/shard_map/pallas_call | solution.py:784
